TPU v7x, 128 devices: a whole 4x4x4 slice. The times are simulated.
128 devices in a mesh: row: 16 (over z_lo, y, core), col: 8 (over z_hi, x).
Axes of the slice: x: 4, y: 4, z: 4 (z_hi: 2, z_lo: 2; z = z_hi * 2 + z_lo), core: 2. Of those that a mesh axis runs over, the one named last changes fastest.
Arguments:
- a_values: float32 [8192, 8192], P('row', 'col'), may hold values from -6 to 6
- a_mask: int32 [64, 64], P('row', 'col'), may hold values from 0 to 1, as said below
- b_values: float32 [8192, 8192], P('row', 'col'), may hold values from -0.5 to 0.5
- b_mask: int32 [64, 64], P('row', 'col'), may hold values from 0 to 1, as said below
- keep: int32 [64, 64, 64], P('row', None, 'col'), may hold values from 0 to 1, as said below
Outputs:
- product: float32 [8192, 8192], P('row', 'col')
Inputs may be any that keep to these rules, and one draw needn't show every extreme that they name: `keep`: 0 means the triple is filtered out, 1 that it counts. `a_mask`: 1 means the block is stored; on one device at most 20 blocks are stored, and some device holds exactly 20. `b_mask`: 1 means the block is stored; on one device at most 20 blocks are stored, and some device holds exactly 20.
All inputs are finite; a program needn't handle non-finite values.
Results may differ from a plain program's by a relative error of at most 0.000071.
Values sent between devices are 32-bit elements; how exact they have to be, the bound alone decides.
No kernel may reach another device: no remote copies, remote signals or barrier semaphores. Data moves between devices by JAX's collectives and lax.ppermute only.
A program may use at most 384 MiB of HBM per device.

v0:
```python
import jax
import jax.numpy as jnp
from jax import lax
from jax.sharding import PartitionSpec as P


def per_device(a_values, a_mask, b_values, b_mask, keep):
    row_blocks, inner_local = a_mask.shape
    inner_rows, col_blocks = b_mask.shape
    width = a_values.shape[0] // row_blocks
    first = (
        a_values.reshape(row_blocks, width, inner_local, width)
        * a_mask.astype(jnp.float32)[:, None, :, None]
    ).reshape(a_values.shape)
    first_whole = lax.all_gather(first, "col", axis=1, tiled=True)
    second = (
        b_values.reshape(inner_rows, width, col_blocks, width)
        * b_mask.astype(jnp.float32)[:, None, :, None]
    ).reshape(b_values.shape)
    weights = jnp.repeat(keep.astype(jnp.float32), width, axis=1)
    piece = lax.all_gather(second, "row", axis=0, tiled=True)
    count = piece.shape[0]
    shaped = first_whole.reshape(row_blocks, width, count)
    results = []
    for column in range(col_blocks):
        masked = (shaped * weights[:, None, :, column]).reshape(row_blocks * width, count)
        results.append(
            jnp.dot(
                masked,
                piece[:, column * width : (column + 1) * width],
                precision=lax.Precision.HIGHEST,
                preferred_element_type=jnp.float32,
            )
        )
    return jnp.concatenate(results, axis=1)


def solution(mesh):
    return jax.shard_map(
        per_device,
        mesh=mesh,
        in_specs=(
            P("row", "col"),
            P("row", "col"),
            P("row", "col"),
            P("row", "col"),
            P("row", None, "col"),
        ),
        out_specs=P("row", "col"),
        check_vma=False,
    )
```

profile of v0, /device:TPU:1, one launch (start us, length us, event | category | flops | bytes accessed | tf_op | source)
XLA Modules:
  0.0 541.8 jit_solution(7089609412667732679)
XLA Ops:
  6.5 0.7 convert_element_type.9
  7.2 0.2 mul.126
  7.4 3.6 bitcast_multiply_fusion.9
  11.1 0.0 all-gather.3.cloned.1.call-update
  11.1 0.0 all-gather.5.cloned.1.call-start
  11.1 0.7 convert_element_type.11
  11.8 0.2 mul.133
  12.0 3.6 bitcast_multiply_fusion.8
  15.6 0.0 all-gather.5.cloned.1.call-update
  15.7 0.3 broadcast_in_dim.2
  16.0 0.4 reshape.36
  16.5 0.1 slice_bitcast_fusion
  16.5 183.4 %all-gather.3.cloned.1.call-done = f32[512,8192]{1,0:T(8,128)} async-done(((f32[512,1024]{1,0:T(8,128)}), f32[512,8192]{1,0:T(8,128)}) %all-gather.3.cloned.1.call-update) | async-done | bytes 16777232 | tf_op jit(solution)/shard_map/all_gather | solution.py:15
  200.0 51.5 %bitcast_multiply_fusion = (f32[512,8192]{1,0:T(8,128)}, f32[512,8192]{1,0:T(8,128)}, f32[512,8192]{1,0:T(8,128)}, f32[512,8192]{1,0:T(8,128)}, f32[512,8192]{1,...) fusion(f32[512,8192]{1,0:T(8,128)} %all-gather.3.cloned.1.call-done, ...), kind=kLoop, calls=%fused_computation | loop fusion | flops 33554432 | bytes 152043520 | tf_op jit(solution)/shard_map/mul | solution.py:26
  251.4 119.5 %all-gather.5.cloned.1.call-done = f32[8192,1024]{1,0:T(8,128)} async-done(((f32[512,1024]{1,0:T(8,128)}), f32[8192,1024]{1,0:T(8,128)}) %all-gather.5.cloned.1.call-update) | async-done | bytes 33554448 | tf_op jit(solution)/shard_map/all_gather | solution.py:21
  370.9 18.5 %fusion.16 = f32[512,1024]{0,1:T(8,128)S(1)} fusion(f32[512,8192]{1,0:T(8,128)} %get-tuple-element.12, f32[8192,1024]{1,0:T(8,128)} %all-gather.5.cloned.1.call-done), kind=kOutput, calls=%fused_computation.26 | convolution fusion | flops 6442450944 | bytes 21233664 | tf_op jit(solution)/shard_map/dot_general | solution.py:28
  389.4 30.7 %fusion.19 = f32[512,1024]{0,1:T(8,128)S(1)} fusion(f32[512,1024]{0,1:T(8,128)S(1)} %fusion.16, f32[512,8192]{1,0:T(8,128)S(1)} %copy-done, f32[8192,1024]{1,0:T(8,128)} %all-gather.5.cloned.1.call-done), kind=kOutput, calls=%fused_computation.27 | convolution fusion | flops 6442450944 | bytes 21233664 | tf_op jit(solution)/shard_map/dot_general | solution.py:28
  420.1 18.2 %fusion.22 = f32[512,1024]{0,1:T(8,128)S(1)} fusion(f32[512,1024]{0,1:T(8,128)S(1)} %fusion.19, f32[512,8192]{1,0:T(8,128)} %get-tuple-element.10, f32[8192,1024]{1,0:T(8,128)} %all-gather.5.cloned.1.call-done), kind=kOutput, calls=%fused_computation.28 | convolution fusion | flops 6442450944 | bytes 21233664 | tf_op jit(solution)/shard_map/dot_general | solution.py:28
  438.3 18.6 %fusion.25 = f32[512,1024]{0,1:T(8,128)S(1)} fusion(f32[512,1024]{0,1:T(8,128)S(1)} %fusion.22, f32[512,8192]{1,0:T(8,128)} %get-tuple-element.9, f32[8192,1024]{1,0:T(8,128)} %all-gather.5.cloned.1.call-done), kind=kOutput, calls=%fused_computation.29 | convolution fusion | flops 6442450944 | bytes 21233664 | tf_op jit(solution)/shard_map/dot_general | solution.py:28
  456.9 19.7 %fusion.28 = f32[512,1024]{0,1:T(8,128)S(1)} fusion(f32[512,1024]{0,1:T(8,128)S(1)} %fusion.25, f32[512,8192]{1,0:T(8,128)S(1)} %bitcast.55, f32[8192,1024]{1,0:T(8,128)} %all-gather.5.cloned.1.call-done), kind=kOutput, calls=%fused_computation.30 | convolution fusion | flops 6442450944 | bytes 21233664 | tf_op jit(solution)/shard_map/dot_general | solution.py:28
  476.6 18.2 %fusion.31 = f32[512,1024]{0,1:T(8,128)S(1)} fusion(f32[512,1024]{0,1:T(8,128)S(1)} %fusion.28, f32[512,8192]{1,0:T(8,128)} %get-tuple-element.7, f32[8192,1024]{1,0:T(8,128)} %all-gather.5.cloned.1.call-done), kind=kOutput, calls=%fused_computation.31 | convolution fusion | flops 6442450944 | bytes 21233664 | tf_op jit(solution)/shard_map/dot_general | solution.py:28
  494.8 18.4 %fusion.34 = f32[512,1024]{0,1:T(8,128)S(1)} fusion(f32[512,1024]{0,1:T(8,128)S(1)} %fusion.31, f32[512,8192]{1,0:T(8,128)} %get-tuple-element.6, f32[8192,1024]{1,0:T(8,128)} %all-gather.5.cloned.1.call-done), kind=kOutput, calls=%fused_computation.32 | convolution fusion | flops 6442450944 | bytes 21233664 | tf_op jit(solution)/shard_map/dot_general | solution.py:28
  513.3 19.5 %fusion.37 = f32[512,1024]{0,1:T(8,128)S(1)} fusion(f32[512,1024]{0,1:T(8,128)S(1)} %fusion.34, f32[512,8192]{1,0:T(8,128)S(1)} %bitcast.53, f32[8192,1024]{1,0:T(8,128)} %all-gather.5.cloned.1.call-done), kind=kOutput, calls=%fused_computation.33 | convolution fusion | flops 6442450944 | bytes 21233664 | tf_op jit(solution)/shard_map/dot_general | solution.py:28
  532.8 1.8 copy.7
  (25 shorter events, 0.1 us)
Async XLA Ops:
  6.5 9.1 %copy-start.1 = (s32[4,64,8]{1,2,0:T(8,128)S(1)}, s32[4,64,8]{1,2,0:T(8,128)}, u32[]{:S(2)}) copy-start(s32[4,64,8]{1,2,0:T(8,128)} %param.9) | copy-start | bytes 24580
  6.5 193.4 %all-gather.3.cloned.1.call-start = ((), (), s32[]{:S(2)}) async-start(), calls=%async_computation | async-start | bytes 18874368 | tf_op jit(solution)/shard_map/all_gather | solution.py:15
  11.1 359.8 %all-gather.5.cloned.1.call-start = ((), (), s32[]{:S(2)}) async-start(), calls=%async_computation.1 | async-start | bytes 35651584 | tf_op jit(solution)/shard_map/all_gather | solution.py:21
  370.9 18.5 %copy-start = (f32[512,8192]{1,0:T(8,128)S(1)}, f32[512,8192]{1,0:T(8,128)}, u32[]{:S(2)}) copy-start(f32[512,8192]{1,0:T(8,128)} %get-tuple-element.11) | copy-start | bytes 50331652
  420.1 36.8 %slice-start.4 = ((s8[16777216]{0:T(1024)(128)(4,1)}), s8[4194304]{0:T(1024)(128)(4,1)S(1)}, s32[]{:S(2)}) async-start(s8[16777216]{0:T(1024)(128)(4,1)} %bitcast.54), calls=%async_computation.6 | async-start | bytes 8388608
  420.1 36.8 %slice-start.5 = ((s8[16777216]{0:T(1024)(128)(4,1)}), s8[4194304]{0:T(1024)(128)(4,1)S(1)}, s32[]{:S(2)}) async-start(s8[16777216]{0:T(1024)(128)(4,1)} %bitcast.54), calls=%async_computation.7 | async-start | bytes 8388608
  438.3 18.6 %slice-start.6 = ((s8[16777216]{0:T(1024)(128)(4,1)}), s8[4194304]{0:T(1024)(128)(4,1)S(1)}, s32[]{:S(2)}) async-start(s8[16777216]{0:T(1024)(128)(4,1)} %bitcast.54), calls=%async_computation.8 | async-start | bytes 8388608
  438.3 18.6 %slice-start.7 = ((s8[16777216]{0:T(1024)(128)(4,1)}), s8[4194304]{0:T(1024)(128)(4,1)S(1)}, s32[]{:S(2)}) async-start(s8[16777216]{0:T(1024)(128)(4,1)} %bitcast.54), calls=%async_computation.9 | async-start | bytes 8388608
  476.6 36.6 %slice-start = ((s8[16777216]{0:T(1024)(128)(4,1)}), s8[4194304]{0:T(1024)(128)(4,1)S(1)}, s32[]{:S(2)}) async-start(s8[16777216]{0:T(1024)(128)(4,1)} %bitcast.52), calls=%async_computation.2 | async-start | bytes 8388608
  476.6 36.6 %slice-start.1 = ((s8[16777216]{0:T(1024)(128)(4,1)}), s8[4194304]{0:T(1024)(128)(4,1)S(1)}, s32[]{:S(2)}) async-start(s8[16777216]{0:T(1024)(128)(4,1)} %bitcast.52), calls=%async_computation.3 | async-start | bytes 8388608
  494.8 18.4 %slice-start.2 = ((s8[16777216]{0:T(1024)(128)(4,1)}), s8[4194304]{0:T(1024)(128)(4,1)S(1)}, s32[]{:S(2)}) async-start(s8[16777216]{0:T(1024)(128)(4,1)} %bitcast.52), calls=%async_computation.4 | async-start | bytes 8388608
  494.8 18.4 %slice-start.3 = ((s8[16777216]{0:T(1024)(128)(4,1)}), s8[4194304]{0:T(1024)(128)(4,1)S(1)}, s32[]{:S(2)}) async-start(s8[16777216]{0:T(1024)(128)(4,1)} %bitcast.52), calls=%async_computation.5 | async-start | bytes 8388608
Sparse Core Ops, SparseCore 0:
  11.2 188.7 all-gather.2
  201.7 169.1 all-gather.4
where the time goes:
time: 550 us; the launch traced here: 542 us
  waiting for transfers between devices  303 us (55%)
  matrix products  162 us (29%)
  other arithmetic  60.1 us (11%)
  between operations  14.1 us (3%)
    all_gather x1, waiting for transfers between devices, per_device(): first_whole = lax.all_gather(first, 'col', axis=1, tiled=True)  183 us
    dot_general x8, matrix products, per_device(): jnp.dot(masked, piece[:, column * width:(column + 1) * width], precision=...  162 us
    all_gather x1, waiting for transfers between devices, per_device(): piece = lax.all_gather(second, 'row', axis=0, tiled=True)  119 us
    mul x1, other arithmetic, per_device(): shaped * weights[:, None, :, column]  51.5 us
  transfers between devices with their start and end apart: 2, of which 2 were waited for; matrix products, arithmetic and copies ran while one was open for 10% of the time, Pallas kernels for 0%

commit v1 on v0

v1 whole, which is shorter than its diff:
```python
import functools

import jax
import jax.numpy as jnp
import numpy as np
from jax import lax
from jax.experimental import pallas as pl
from jax.experimental.pallas import tpu as pltpu
from jax.sharding import Mesh
from jax.sharding import PartitionSpec as P

W = 128
SLOTS = 20
DATA = SLOTS * W
ROWS = DATA + 8
HALF = DATA // 2
ROW = ("zl", "y", "core")
COL = ("zh", "x")


def pack_kernel(am_ref, bm_ref, a_ref, b_ref, am_tile, bm_tile, pa_ref, pb_ref, sem_a, sem_b, sem_m):
    tiles = (
        pltpu.make_async_copy(am_tile, pa_ref.at[pl.ds(DATA, 8), :], sem_m.at[0]),
        pltpu.make_async_copy(bm_tile, pb_ref.at[pl.ds(DATA, 8), :], sem_m.at[1]),
    )
    for tile in tiles:
        tile.start()

    def move(mask, src, dst, sem):
        rows, cols = mask.shape
        slot = jnp.int32(0)
        for r in range(rows):
            for c in range(cols):
                on = mask[r, c] != 0

                @pl.when(on)
                def _():
                    at = pl.multiple_of(slot * W, W)
                    pltpu.make_async_copy(
                        src.at[pl.ds(r * W, W), pl.ds(c * W, W)], dst.at[pl.ds(at, W), :], sem.at[r * cols + c]
                    ).start()

                slot = slot + on.astype(jnp.int32)

    def finish(mask, src, dst, sem):
        rows, cols = mask.shape
        for r in range(rows):
            for c in range(cols):

                @pl.when(mask[r, c] != 0)
                def _():
                    pltpu.make_async_copy(
                        src.at[pl.ds(r * W, W), pl.ds(c * W, W)], dst.at[pl.ds(0, W), :], sem.at[r * cols + c]
                    ).wait()

    move(am_ref, a_ref, pa_ref, sem_a)
    move(bm_ref, b_ref, pb_ref, sem_b)
    finish(am_ref, a_ref, pa_ref, sem_a)
    finish(bm_ref, b_ref, pb_ref, sem_b)
    for tile in tiles:
        tile.wait()


def pack(a_mask, b_mask, a_values, b_values, a_tile, b_tile):
    smem = pl.BlockSpec(memory_space=pltpu.SMEM)
    hbm = pl.BlockSpec(memory_space=pl.ANY)
    shape = jax.ShapeDtypeStruct((ROWS, W), jnp.float32)
    return pl.pallas_call(
        pack_kernel,
        out_shape=(shape, shape),
        in_specs=[smem, smem, hbm, hbm, hbm, hbm],
        out_specs=(hbm, hbm),
        scratch_shapes=[
            pltpu.SemaphoreType.DMA((32,)),
            pltpu.SemaphoreType.DMA((32,)),
            pltpu.SemaphoreType.DMA((2,)),
        ],
        name="pack",
    )(a_mask, b_mask, a_values, b_values, a_tile, b_tile)


def split(x):
    high = x.astype(jnp.bfloat16)
    low = (x - high.astype(jnp.float32)).astype(jnp.bfloat16)
    return high, low


def product_kernel(plan, where_ref, keep_ref, *refs):
    count = len(plan)
    pieces = refs[:count]
    out_ref, a_all, b_all, a_meta, b_meta, table, words, table_s, words_s, sem, sem_t = refs[count:]
    copies = []
    for n, (which, part) in enumerate(plan):
        at = where_ref[n]
        data, meta, step = (a_all, a_meta, 8) if which == "a" else (b_all, b_meta, 8)
        base = at * DATA
        piece = pieces[n]
        if part != "first":
            copies.append((piece.at[pl.ds(piece.shape[0] - 8, 8), :], meta.at[pl.ds(at * 8, 8), :]))
        if part == "whole":
            copies.append((piece.at[pl.ds(0, DATA), :], data.at[pl.ds(base, DATA), :]))
        elif part == "first":
            copies.append((piece, data.at[pl.ds(base, HALF), :]))
        else:
            copies.append((piece.at[pl.ds(0, HALF), :], data.at[pl.ds(base + HALF, HALF), :]))
    copies = [pltpu.make_async_copy(src, dst, sem.at[n]) for n, (src, dst) in enumerate(copies)]
    for copy in copies:
        copy.start()
    for copy in copies:
        copy.wait()

    k8 = lax.broadcasted_iota(jnp.int32, (8, W), 0)
    one = jnp.ones((8, W), jnp.int32)
    low = jnp.zeros((8, W), jnp.int32)
    high = jnp.zeros((8, W), jnp.int32)
    for c in range(8):
        a_slot = a_meta[pl.ds(c * 8, 8), :].astype(jnp.int32)
        b0 = b_meta[pl.ds(c * 16, 8), :].astype(jnp.int32)
        b1 = pltpu.roll(b_meta[pl.ds(c * 16 + 8, 8), :], 4, 0).astype(jnp.int32)
        b_slot = jnp.where(k8 < 4, b0, b1)
        live = (keep_ref[pl.ds(c * 8, 8), :] != 0) & (a_slot > 0) & (b_slot > 0)
        b_at = jnp.where(k8 < 4, 2 * c, 2 * c + 1) * SLOTS + b_slot - 1
        a_at = c * SLOTS + a_slot - 1
        table[pl.ds(c * 8, 8), :] = jnp.where(live, a_at + b_at * 65536, 0)
        bit = jnp.where(live, lax.shift_left(one, k8 + 8 * (c % 4)), 0)
        if c < 4:
            low = low | bit
        else:
            high = high | bit
    for n, word in enumerate((low, high)):
        word = word | pltpu.roll(word, 4, 0)
        word = word | pltpu.roll(word, 2, 0)
        word = word | pltpu.roll(word, 1, 0)
        words[pl.ds(8 * n, 8), :] = jnp.where(k8 == 0, word, lax.population_count(word))
    t0 = pltpu.make_async_copy(table, table_s, sem_t.at[0])
    t1 = pltpu.make_async_copy(words, words_s, sem_t.at[1])
    t0.start()
    t1.start()
    t0.wait()
    t1.wait()

    def block(p, _):
        acc = jnp.zeros((W, W), jnp.float32)
        for n in range(2):
            bits = words_s[8 * n, p]

            def step(_, state):
                bits, acc = state
                lowest = bits & -bits
                k = 31 - lax.clz(lowest) + 32 * n
                entry = table_s[k, p]
                a_at = pl.multiple_of((entry & 65535) * W, W)
                b_at = pl.multiple_of(lax.shift_right_logical(entry, 16) * W, W)
                a_high, a_low = split(a_all[pl.ds(a_at, W), :])
                b_high, b_low = split(b_all[pl.ds(b_at, W), :])
                left = jnp.concatenate([a_high, a_low], axis=1)
                right = jnp.concatenate(
                    [jnp.concatenate([b_high, b_low], axis=1), jnp.concatenate([b_low, b_high], axis=1)], axis=0
                )
                both = jnp.dot(left, right, preferred_element_type=jnp.float32)
                return bits ^ lowest, acc + (both[:, :W] + both[:, W:])

            bits, acc = lax.fori_loop(0, words_s[8 * n + 1, p], step, (bits, acc))
        i = p // 8
        j = p - i * 8
        out_ref[pl.ds(pl.multiple_of(i * W, W), W), pl.ds(pl.multiple_of(j * W, W), W)] = acc
        return 0

    lax.fori_loop(0, 32, block, 0)


def product(plan, where, keep_tile, pieces):
    hbm = pl.BlockSpec(memory_space=pl.ANY)
    return pl.pallas_call(
        functools.partial(product_kernel, plan),
        out_shape=jax.ShapeDtypeStruct((512, 1024), jnp.float32),
        in_specs=[pl.BlockSpec(memory_space=pltpu.SMEM), pl.BlockSpec(memory_space=pltpu.VMEM)] + [hbm] * len(pieces),
        out_specs=pl.BlockSpec(memory_space=pltpu.VMEM),
        scratch_shapes=[
            pltpu.VMEM((8 * DATA, W), jnp.float32),
            pltpu.VMEM((16 * DATA, W), jnp.float32),
            pltpu.VMEM((64, W), jnp.float32),
            pltpu.VMEM((128, W), jnp.float32),
            pltpu.VMEM((64, W), jnp.int32),
            pltpu.VMEM((16, W), jnp.int32),
            pltpu.SMEM((64, W), jnp.int32),
            pltpu.SMEM((16, W), jnp.int32),
            pltpu.SemaphoreType.DMA((2 * len(pieces),)),
            pltpu.SemaphoreType.DMA((2,)),
        ],
        compiler_params=pltpu.CompilerParams(vmem_limit_bytes=48 * 1024 * 1024),
        name="product",
    )(where, keep_tile, *pieces)


def swap(x, axis):
    return lax.ppermute(x, axis, [(0, 1), (1, 0)])


def right(x, axis):
    return lax.ppermute(x, axis, [(n, (n + 1) % 4) for n in range(4)])


def left(x, axis):
    return lax.ppermute(x, axis, [(n, (n - 1) % 4) for n in range(4)])


def ring(x, axis):
    from_left = right(x, axis)
    from_right = left(x, axis)
    first = right(from_left[:HALF], axis)
    second = left(from_right[HALF:], axis)
    return [(3, "whole", from_left), (1, "whole", from_right), (2, "first", first), (2, "second", second)]


def slots_of(mask):
    flat = (mask.reshape(-1) != 0).astype(jnp.float32)
    n = flat.shape[0]
    upto = jnp.asarray(np.tril(np.ones((n, n), np.float32)))
    rank = jnp.sum(upto * flat[None, :], axis=1)
    return (flat * rank).reshape(mask.shape)


def per_device(a_values, a_mask, b_values, b_mask, keep):
    a_slot = slots_of(a_mask)
    b_slot = slots_of(b_mask)
    a_tile = jnp.pad(jnp.repeat(a_slot.T, 8, axis=1), ((0, 0), (0, W - 32)))
    b_tile = jnp.pad(jnp.tile(b_slot, (1, 4)), ((0, 4), (0, W - 32)))
    keep_tile = jnp.pad(jnp.transpose(keep, (1, 0, 2)).reshape(64, 32), ((0, 0), (0, W - 32)))
    a, b = pack(a_mask, b_mask, a_values, b_values, a_tile, b_tile)

    zl, y, core = (lax.axis_index(n) for n in ROW)
    zh, x = (lax.axis_index(n) for n in COL)
    plan, where, pieces = [], [], []

    def add(which, part, at, piece):
        plan.append((which, part))
        where.append(at)
        pieces.append(piece)

    a_other = swap(a, "zh")
    b_other = swap(b, "zl")
    b_pieces = []
    for z, own_a, own_b in ((0, a, b), (1, a_other, b_other)):
        add("a", "whole", (zh ^ z) * 4 + x, own_a)
        for shift, part, piece in ring(own_a, "x"):
            add("a", part, (zh ^ z) * 4 + (x + shift) % 4, piece)
        b_pieces.append((z, 0, "whole", own_b))
        for shift, part, piece in ring(own_b, "y"):
            b_pieces.append((z, shift, part, piece))
    for z, shift, part, piece in b_pieces:
        chip = (zl ^ z) * 8 + ((y + shift) % 4) * 2
        add("b", part, chip + core, piece)
        add("b", part, chip + 1 - core, swap(piece, "core"))
    return product(tuple(plan), jnp.stack(where).astype(jnp.int32), keep_tile, pieces)


def solution(mesh):
    fine = Mesh(mesh.devices.reshape(2, 4, 2, 2, 4), ROW + COL)
    return jax.shard_map(
        per_device,
        mesh=fine,
        in_specs=(P(ROW, COL), P(ROW, COL), P(ROW, COL), P(ROW, COL), P(ROW, None, COL)),
        out_specs=P(ROW, COL),
        check_vma=False,
    )
```

time: 550 us -> 229 us (0.42)
  the two profiles are of different devices: /device:TPU:1 before, /device:TPU:32 now
where the time goes in v1:
time: 229 us; the launch traced here: 227 us
  waiting for transfers between devices  102 us (45%)
  Pallas kernels  59 us (26%)
  starting transfers between devices  53.8 us (23%)
  local copies, waits for them, and re-layouts  9.96 us (4%)
    ppermute x8, waiting for transfers between devices, left(): return lax.ppermute(x, axis, [(n, (n - 1) % 4) for n in range(4)])  41.8 us
    ppermute x8, starting transfers between devices, left(): return lax.ppermute(x, axis, [(n, (n - 1) % 4) for n in range(4)])  32.5 us
    ppermute x8, waiting for transfers between devices, right(): return lax.ppermute(x, axis, [(n, (n + 1) % 4) for n in range(4)])  31.5 us
    pallas_call x1, Pallas kernels, pack(): pl.pallas_call(pack_kernel, out_shape=(shape, shape), in_specs=[smem, sme...  30.5 us
    pallas_call x1, Pallas kernels, product(): pl.pallas_call(functools.partial(product_kernel, plan), out_shape=jax.Sha...  28.6 us
    ppermute x12, waiting for transfers between devices, swap(): return lax.ppermute(x, axis, [(0, 1), (1, 0)])  28.3 us
    ppermute x12, starting transfers between devices, swap(): return lax.ppermute(x, axis, [(0, 1), (1, 0)])  14.6 us
    ppermute x8, starting transfers between devices, right(): return lax.ppermute(x, axis, [(n, (n + 1) % 4) for n in range(4)])  6.66 us
  transfers between devices with their start and end apart: 28, of which 11 were waited for; matrix products, arithmetic and copies ran while one was open for 2% of the time, Pallas kernels for 0%

profile of v1, /device:TPU:32, one launch (start us, length us, event | category | flops | bytes accessed | tf_op | source)
XLA Modules:
  0.0 227.0 jit_solution(14862112714661669679)
XLA Ops:
  4.1 30.5 %pack.1 = (f32[2568,128]{1,0:T(8,128)}, f32[2568,128]{1,0:T(8,128)}) custom-call(s32[4,8]{1,0:T(4,128)} %am_ref.1, s32[4,8]{1,0:T(4,128)} %bm_ref.1, f32[512,1024]{1,0:T(8,128)} %a_ref.1, f32[512,1024]{1,0:T(8,128)} %b_ref.1, f32[8,128]{1,0:T(8,128)} %pad.13.am_tile, f32[8,128]{1,0:T(8,128)} %pad.14.bm_tile), custom_call_target="tpu_custom_call" | custom-call | tf_op jit(solution)/shard_map/pack/pallas_call | solution.py:68
  34.6 11.0 %collective-permute-start.4 = (f32[2568,128]{1,0:T(8,128)}, f32[2568,128]{1,0:T(8,128)S(1)}, u32[]{:S(2)}, u32[]{:S(2)}) collective-permute-start(f32[2568,128]{1,0:T(8,128)} %get-tuple-element.7.refs_0_), channel_id=1, source_target_pairs={{0,4},{4,0},{1,5},{5,1},{2,6},{6,2},{3,7},{7,3},{8,12},{12,8},{9,1... | collective-permute-start | bytes 3944456 | tf_op jit(solution)/shard_map/ppermute | solution.py:197
  45.6 3.2 %collective-permute-start.1 = (f32[2568,128]{1,0:T(8,128)}, f32[2568,128]{1,0:T(8,128)S(1)}, u32[]{:S(2)}, u32[]{:S(2)}) collective-permute-start(f32[2568,128]{1,0:T(8,128)} %get-tuple-element.7.refs_0_), channel_id=1, source_target_pairs={{0,3},{1,0},{2,1},{3,2},{4,7},{5,4},{6,5},{7,6},{8,11},{9,8},{10,9... | collective-permute-start | bytes 3944456 | tf_op jit(solution)/shard_map/ppermute | solution.py:205
  48.8 15.5 %collective-permute-start.12 = (f32[2568,128]{1,0:T(8,128)}, f32[2568,128]{1,0:T(8,128)S(1)}, u32[]{:S(2)}, u32[]{:S(2)}) collective-permute-start(f32[2568,128]{1,0:T(8,128)} %get-tuple-element.8.refs_10_), channel_id=1, source_target_pairs={{0,48},{16,0},{32,16},{48,32},{1,49},{17,1},{33,17},{49,33},{2,50}... | collective-permute-start | bytes 3944456 | tf_op jit(solution)/shard_map/ppermute | solution.py:205
  64.3 11.3 %collective-permute-done.4.refs_5_ = f32[2568,128]{1,0:T(8,128)S(1)} collective-permute-done((f32[2568,128]{1,0:T(8,128)}, f32[2568,128]{1,0:T(8,128)S(1)}, u32[]{:S(2)}, u32[]{:S(2)}) %collective-permute-start.4) | collective-permute-done | bytes 1314848 | tf_op jit(solution)/shard_map/ppermute | solution.py:197
  76.7 1.8 collective-permute-start.2
  78.5 17.0 %collective-permute-done.18.refs_20_ = f32[2568,128]{1,0:T(8,128)S(1)} collective-permute-done((f32[2568,128]{1,0:T(8,128)}, f32[2568,128]{1,0:T(8,128)S(1)}, u32[]{:S(2)}, u32[]{:S(2)}) %collective-permute-start.18) | collective-permute-done | bytes 1314848 | tf_op jit(solution)/shard_map/ppermute | solution.py:197
  95.5 2.8 %collective-permute-start.3 = (f32[1288,128]{1,0:T(8,128)S(1)}, f32[1288,128]{1,0:T(8,128)S(1)}, u32[]{:S(2)}, u32[]{:S(2)}) collective-permute-start(f32[1288,128]{1,0:T(8,128)S(1)} %slice.33), channel_id=1, source_target_pairs={{0,3},{1,0},{2,1},{3,2},{4,7},{5,4},{6,5},{7,6},{8,11},{9,8},{10,9... | collective-permute-start | bytes 1978376 | tf_op jit(solution)/shard_map/ppermute | solution.py:205
  98.3 5.6 %collective-permute-start.6 = (f32[2568,128]{1,0:T(8,128)S(1)}, f32[2568,128]{1,0:T(8,128)S(1)}, u32[]{:S(2)}, u32[]{:S(2)}) collective-permute-start(f32[2568,128]{1,0:T(8,128)S(1)} %collective-permute-done.4.refs_5_), channel_id=1, source_target_pairs={{0,3},{1,0},{2,1},{3,2},{4,7},{5,4},{6,5},{7,6},{8,11},{9,8},{10,9... | collective-permute-start | bytes 3944456 | tf_op jit(solution)/shard_map/ppermute | solution.py:205
  103.8 4.6 %collective-permute-done.10.refs_12_ = f32[2568,128]{1,0:T(8,128)S(1)} collective-permute-done((f32[2568,128]{1,0:T(8,128)}, f32[2568,128]{1,0:T(8,128)S(1)}, u32[]{:S(2)}, u32[]{:S(2)}) %collective-permute-start.10) | collective-permute-done | bytes 1314848 | tf_op jit(solution)/shard_map/ppermute | solution.py:201
  108.4 2.0 collective-permute-start.5
  111.7 2.3 %collective-permute-start.16 = (f32[1288,128]{1,0:T(8,128)S(1)}, f32[1288,128]{1,0:T(8,128)S(1)}, u32[]{:S(2)}, u32[]{:S(2)}) collective-permute-start(f32[1288,128]{1,0:T(8,128)S(1)} %slice.37), channel_id=1, source_target_pairs={{0,48},{16,0},{32,16},{48,32},{1,49},{17,1},{33,17},{49,33},{2,50}... | collective-permute-start | bytes 1978376 | tf_op jit(solution)/shard_map/ppermute | solution.py:205
  114.0 12.6 %collective-permute-done.14.refs_16_ = f32[1280,128]{1,0:T(8,128)S(1)} collective-permute-done((f32[1280,128]{1,0:T(8,128)S(1)}, f32[1280,128]{1,0:T(8,128)S(1)}, u32[]{:S(2)}, u32[]{:S(2)}) %collective-permute-start.14) | collective-permute-done | bytes 655392 | tf_op jit(solution)/shard_map/ppermute | solution.py:201
  126.6 2.0 collective-permute-start.20
  128.8 10.8 %collective-permute-done.6.refs_7_ = f32[2568,128]{1,0:T(8,128)S(1)} collective-permute-done((f32[2568,128]{1,0:T(8,128)S(1)}, f32[2568,128]{1,0:T(8,128)S(1)}, u32[]{:S(2)}, u32[]{:S(2)}) %collective-permute-start.6) | collective-permute-done | bytes 1314848 | tf_op jit(solution)/shard_map/ppermute | solution.py:205
  139.6 2.0 collective-permute-start.13
  141.7 16.2 %collective-permute-done.22.refs_24_ = f32[2568,128]{1,0:T(8,128)} collective-permute-done((f32[2568,128]{1,0:T(8,128)S(1)}, f32[2568,128]{1,0:T(8,128)}, u32[]{:S(2)}, u32[]{:S(2)}) %collective-permute-start.22) | collective-permute-done | bytes 1314848 | tf_op jit(solution)/shard_map/ppermute | solution.py:205
  157.9 1.1 slice.39
  159.2 1.4 collective-permute-start.26
  161.4 1.6 slice.38
  164.6 14.3 %collective-permute-done.7.refs_8_ = f32[1280,128]{1,0:T(8,128)S(1)} collective-permute-done((f32[1280,128]{1,0:T(8,128)S(1)}, f32[1280,128]{1,0:T(8,128)S(1)}, u32[]{:S(2)}, u32[]{:S(2)}) %collective-permute-start.7) | collective-permute-done | bytes 655392 | tf_op jit(solution)/shard_map/ppermute | solution.py:201
  179.7 1.7 collective-permute-start.8
  182.4 13.8 %collective-permute-done.8.refs_9_ = f32[1288,128]{1,0:T(8,128)S(1)} collective-permute-done((f32[1288,128]{1,0:T(8,128)}, f32[1288,128]{1,0:T(8,128)S(1)}, u32[]{:S(2)}, u32[]{:S(2)}) %collective-permute-start.8) | collective-permute-done | bytes 659488 | tf_op jit(solution)/shard_map/ppermute | solution.py:205
  198.4 28.6 %product.1 = f32[512,1024]{1,0:T(8,128)} custom-call(s32[30]{0:T(128)S(1)} %stack.105.where_ref, s32[64,128]{1,0:T(8,128)S(1)} %pad.12.keep_ref, f32[2568,128]{1,0:T(8,128)} %get-tuple-element.7.refs_0_, f32[2568,128]{1,0:T(8,128)} %copy-done.7, f32[2568,128]{1,0:T(8,128)} %copy-done.4, f32[1280,128]{1,0:T(8,128)S(1)} %collective-permute-done.2.refs_3_, ...), custom_call_target="tpu_custom_call" | custom-call | tf_op jit(solution)/shard_map/product/pallas_call | solution.py:174
  (97 shorter events, 13.0 us)
Async XLA Ops:
  34.6 41.0 %collective-permute-start.4 = (f32[2568,128]{1,0:T(8,128)}, f32[2568,128]{1,0:T(8,128)S(1)}, u32[]{:S(2)}, u32[]{:S(2)}) collective-permute-start(f32[2568,128]{1,0:T(8,128)} %get-tuple-element.7.refs_0_), channel_id=1, source_target_pairs={{0,4},{4,0},{1,5},{5,1},{2,6},{6,2},{3,7},{7,3},{8,12},{12,8},{9,1... | collective-permute-start | bytes 3944456 | tf_op jit(solution)/shard_map/ppermute | solution.py:197
  45.6 30.0 %collective-permute-start = (f32[2568,128]{1,0:T(8,128)}, f32[2568,128]{1,0:T(8,128)S(1)}, u32[]{:S(2)}, u32[]{:S(2)}) collective-permute-start(f32[2568,128]{1,0:T(8,128)} %get-tuple-element.7.refs_0_), channel_id=1, source_target_pairs={{0,1},{1,2},{2,3},{3,0},{4,5},{5,6},{6,7},{7,4},{8,9},{9,10},{10,1... | collective-permute-start | bytes 3944456 | tf_op jit(solution)/shard_map/ppermute | solution.py:201
  45.6 31.1 %collective-permute-start.1 = (f32[2568,128]{1,0:T(8,128)}, f32[2568,128]{1,0:T(8,128)S(1)}, u32[]{:S(2)}, u32[]{:S(2)}) collective-permute-start(f32[2568,128]{1,0:T(8,128)} %get-tuple-element.7.refs_0_), channel_id=1, source_target_pairs={{0,3},{1,0},{2,1},{3,2},{4,7},{5,4},{6,5},{7,6},{8,11},{9,8},{10,9... | collective-permute-start | bytes 3944456 | tf_op jit(solution)/shard_map/ppermute | solution.py:205
  48.8 46.7 %collective-permute-start.18 = (f32[2568,128]{1,0:T(8,128)}, f32[2568,128]{1,0:T(8,128)S(1)}, u32[]{:S(2)}, u32[]{:S(2)}) collective-permute-start(f32[2568,128]{1,0:T(8,128)} %get-tuple-element.8.refs_10_), channel_id=1, source_target_pairs={{0,64},{64,0},{1,65},{65,1},{2,66},{66,2},{3,67},{67,3},{4,68},{68... | collective-permute-start | bytes 3944456 | tf_op jit(solution)/shard_map/ppermute | solution.py:197
  48.8 49.5 %collective-permute-start.12 = (f32[2568,128]{1,0:T(8,128)}, f32[2568,128]{1,0:T(8,128)S(1)}, u32[]{:S(2)}, u32[]{:S(2)}) collective-permute-start(f32[2568,128]{1,0:T(8,128)} %get-tuple-element.8.refs_10_), channel_id=1, source_target_pairs={{0,48},{16,0},{32,16},{48,32},{1,49},{17,1},{33,17},{49,33},{2,50}... | collective-permute-start | bytes 3944456 | tf_op jit(solution)/shard_map/ppermute | solution.py:205
  75.5 32.9 %collective-permute-start.10 = (f32[2568,128]{1,0:T(8,128)}, f32[2568,128]{1,0:T(8,128)S(1)}, u32[]{:S(2)}, u32[]{:S(2)}) collective-permute-start(f32[2568,128]{1,0:T(8,128)} %get-tuple-element.8.refs_10_), channel_id=1, source_target_pairs={{0,16},{16,32},{32,48},{48,0},{1,17},{17,33},{33,49},{49,1},{2,18}... | collective-permute-start | bytes 3944456 | tf_op jit(solution)/shard_map/ppermute | solution.py:201
  75.6 34.9 %collective-permute-start.9 = (f32[2568,128]{1,0:T(8,128)}, f32[2568,128]{1,0:T(8,128)S(1)}, u32[]{:S(2)}, u32[]{:S(2)}) collective-permute-start(f32[2568,128]{1,0:T(8,128)} %get-tuple-element.8.refs_10_), channel_id=1, source_target_pairs={{0,8},{8,0},{1,9},{9,1},{2,10},{10,2},{3,11},{11,3},{4,12},{12,4},... | collective-permute-start | bytes 3944456 | tf_op jit(solution)/shard_map/ppermute | solution.py:197
  76.7 35.0 %collective-permute-start.2 = (f32[1280,128]{1,0:T(8,128)S(1)}, f32[1280,128]{1,0:T(8,128)S(1)}, u32[]{:S(2)}, u32[]{:S(2)}) collective-permute-start(f32[1280,128]{1,0:T(8,128)S(1)} %slice.32), channel_id=1, source_target_pairs={{0,1},{1,2},{2,3},{3,0},{4,5},{5,6},{6,7},{7,4},{8,9},{9,10},{10,1... | collective-permute-start | bytes 1966088 | tf_op jit(solution)/shard_map/ppermute | solution.py:201
  95.5 31.0 %collective-permute-start.3 = (f32[1288,128]{1,0:T(8,128)S(1)}, f32[1288,128]{1,0:T(8,128)S(1)}, u32[]{:S(2)}, u32[]{:S(2)}) collective-permute-start(f32[1288,128]{1,0:T(8,128)S(1)} %slice.33), channel_id=1, source_target_pairs={{0,3},{1,0},{2,1},{3,2},{4,7},{5,4},{6,5},{7,6},{8,11},{9,8},{10,9... | collective-permute-start | bytes 1978376 | tf_op jit(solution)/shard_map/ppermute | solution.py:205
  98.3 41.3 %collective-permute-start.6 = (f32[2568,128]{1,0:T(8,128)S(1)}, f32[2568,128]{1,0:T(8,128)S(1)}, u32[]{:S(2)}, u32[]{:S(2)}) collective-permute-start(f32[2568,128]{1,0:T(8,128)S(1)} %collective-permute-done.4.refs_5_), channel_id=1, source_target_pairs={{0,3},{1,0},{2,1},{3,2},{4,7},{5,4},{6,5},{7,6},{8,11},{9,8},{10,9... | collective-permute-start | bytes 3944456 | tf_op jit(solution)/shard_map/ppermute | solution.py:205
  108.4 33.2 %collective-permute-start.5 = (f32[2568,128]{1,0:T(8,128)S(1)}, f32[2568,128]{1,0:T(8,128)S(1)}, u32[]{:S(2)}, u32[]{:S(2)}) collective-permute-start(f32[2568,128]{1,0:T(8,128)S(1)} %collective-permute-done.4.refs_5_), channel_id=1, source_target_pairs={{0,1},{1,2},{2,3},{3,0},{4,5},{5,6},{6,7},{7,4},{8,9},{9,10},{10,1... | collective-permute-start | bytes 3944456 | tf_op jit(solution)/shard_map/ppermute | solution.py:201
  110.5 16.0 %collective-permute-start.14 = (f32[1280,128]{1,0:T(8,128)S(1)}, f32[1280,128]{1,0:T(8,128)S(1)}, u32[]{:S(2)}, u32[]{:S(2)}) collective-permute-start(f32[1280,128]{1,0:T(8,128)S(1)} %slice.36), channel_id=1, source_target_pairs={{0,16},{16,32},{32,48},{48,0},{1,17},{17,33},{33,49},{49,1},{2,18}... | collective-permute-start | bytes 1966088 | tf_op jit(solution)/shard_map/ppermute | solution.py:201
  111.7 14.9 %collective-permute-start.16 = (f32[1288,128]{1,0:T(8,128)S(1)}, f32[1288,128]{1,0:T(8,128)S(1)}, u32[]{:S(2)}, u32[]{:S(2)}) collective-permute-start(f32[1288,128]{1,0:T(8,128)S(1)} %slice.37), channel_id=1, source_target_pairs={{0,48},{16,0},{32,16},{48,32},{1,49},{17,1},{33,17},{49,33},{2,50}... | collective-permute-start | bytes 1978376 | tf_op jit(solution)/shard_map/ppermute | solution.py:205
  126.5 31.4 %collective-permute-start.22 = (f32[2568,128]{1,0:T(8,128)S(1)}, f32[2568,128]{1,0:T(8,128)}, u32[]{:S(2)}, u32[]{:S(2)}) collective-permute-start(f32[2568,128]{1,0:T(8,128)S(1)} %collective-permute-done.18.refs_20_), channel_id=1, source_target_pairs={{0,48},{16,0},{32,16},{48,32},{1,49},{17,1},{33,17},{49,33},{2,50}... | collective-permute-start | bytes 3944456 | tf_op jit(solution)/shard_map/ppermute | solution.py:205
  126.6 32.6 %collective-permute-start.20 = (f32[2568,128]{1,0:T(8,128)S(1)}, f32[2568,128]{1,0:T(8,128)}, u32[]{:S(2)}, u32[]{:S(2)}) collective-permute-start(f32[2568,128]{1,0:T(8,128)S(1)} %collective-permute-done.18.refs_20_), channel_id=1, source_target_pairs={{0,16},{16,32},{32,48},{48,0},{1,17},{17,33},{33,49},{49,1},{2,18}... | collective-permute-start | bytes 3944456 | tf_op jit(solution)/shard_map/ppermute | solution.py:201
  128.6 32.1 %collective-permute-start.19 = (f32[2568,128]{1,0:T(8,128)S(1)}, f32[2568,128]{1,0:T(8,128)S(1)}, u32[]{:S(2)}, u32[]{:S(2)}) collective-permute-start(f32[2568,128]{1,0:T(8,128)S(1)} %collective-permute-done.18.refs_20_), channel_id=1, source_target_pairs={{0,8},{8,0},{1,9},{9,1},{2,10},{10,2},{3,11},{11,3},{4,12},{12,4},... | collective-permute-start | bytes 3944456 | tf_op jit(solution)/shard_map/ppermute | solution.py:197
  139.6 21.3 %collective-permute-start.13 = (f32[2568,128]{1,0:T(8,128)S(1)}, f32[2568,128]{1,0:T(8,128)S(1)}, u32[]{:S(2)}, u32[]{:S(2)}) collective-permute-start(f32[2568,128]{1,0:T(8,128)S(1)} %collective-permute-done.12.refs_14_), channel_id=1, source_target_pairs={{0,8},{8,0},{1,9},{9,1},{2,10},{10,2},{3,11},{11,3},{4,12},{12,4},... | collective-permute-start | bytes 3944456 | tf_op jit(solution)/shard_map/ppermute | solution.py:197
  141.6 19.5 %collective-permute-start.11 = (f32[2568,128]{1,0:T(8,128)S(1)}, f32[2568,128]{1,0:T(8,128)S(1)}, u32[]{:S(2)}, u32[]{:S(2)}) collective-permute-start(f32[2568,128]{1,0:T(8,128)S(1)} %collective-permute-done.10.refs_12_), channel_id=1, source_target_pairs={{0,8},{8,0},{1,9},{9,1},{2,10},{10,2},{3,11},{11,3},{4,12},{12,4},... | collective-permute-start | bytes 3944456 | tf_op jit(solution)/shard_map/ppermute | solution.py:197
  159.2 22.3 %collective-permute-start.26 = (f32[1288,128]{1,0:T(8,128)S(1)}, f32[1288,128]{1,0:T(8,128)}, u32[]{:S(2)}, u32[]{:S(2)}) collective-permute-start(f32[1288,128]{1,0:T(8,128)S(1)} %slice.39), channel_id=1, source_target_pairs={{0,48},{16,0},{32,16},{48,32},{1,49},{17,1},{33,17},{49,33},{2,50}... | collective-permute-start | bytes 1978376 | tf_op jit(solution)/shard_map/ppermute | solution.py:205
  160.7 18.1 %collective-permute-start.7 = (f32[1280,128]{1,0:T(8,128)S(1)}, f32[1280,128]{1,0:T(8,128)S(1)}, u32[]{:S(2)}, u32[]{:S(2)}) collective-permute-start(f32[1280,128]{1,0:T(8,128)S(1)} %slice.34), channel_id=1, source_target_pairs={{0,1},{1,2},{2,3},{3,0},{4,5},{5,6},{6,7},{7,4},{8,9},{9,10},{10,1... | collective-permute-start | bytes 1966088 | tf_op jit(solution)/shard_map/ppermute | solution.py:201
  160.8 35.3 %collective-permute-start.23 = (f32[2568,128]{1,0:T(8,128)}, f32[2568,128]{1,0:T(8,128)}, u32[]{:S(2)}, u32[]{:S(2)}) collective-permute-start(f32[2568,128]{1,0:T(8,128)} %collective-permute-done.22.refs_24_), channel_id=1, source_target_pairs={{0,8},{8,0},{1,9},{9,1},{2,10},{10,2},{3,11},{11,3},{4,12},{12,4},... | collective-permute-start | bytes 3944456 | tf_op jit(solution)/shard_map/ppermute | solution.py:197
  161.2 35.0 %collective-permute-start.21 = (f32[2568,128]{1,0:T(8,128)}, f32[2568,128]{1,0:T(8,128)}, u32[]{:S(2)}, u32[]{:S(2)}) collective-permute-start(f32[2568,128]{1,0:T(8,128)} %collective-permute-done.20.refs_22_), channel_id=1, source_target_pairs={{0,8},{8,0},{1,9},{9,1},{2,10},{10,2},{3,11},{11,3},{4,12},{12,4},... | collective-permute-start | bytes 3944456 | tf_op jit(solution)/shard_map/ppermute | solution.py:197
  163.1 18.5 %collective-permute-start.24 = (f32[1280,128]{1,0:T(8,128)S(1)}, f32[1280,128]{1,0:T(8,128)}, u32[]{:S(2)}, u32[]{:S(2)}) collective-permute-start(f32[1280,128]{1,0:T(8,128)S(1)} %slice.38), channel_id=1, source_target_pairs={{0,16},{16,32},{32,48},{48,0},{1,17},{17,33},{33,49},{49,1},{2,18}... | collective-permute-start | bytes 1966088 | tf_op jit(solution)/shard_map/ppermute | solution.py:201
  179.7 16.4 %collective-permute-start.8 = (f32[1288,128]{1,0:T(8,128)}, f32[1288,128]{1,0:T(8,128)S(1)}, u32[]{:S(2)}, u32[]{:S(2)}) collective-permute-start(f32[1288,128]{1,0:T(8,128)} %slice.35), channel_id=1, source_target_pairs={{0,3},{1,0},{2,1},{3,2},{4,7},{5,4},{6,5},{7,6},{8,11},{9,8},{10,9... | collective-permute-start | bytes 1978376 | tf_op jit(solution)/shard_map/ppermute | solution.py:205
  (22 other events, 508.2 us)

commit v2 on v1

--- a/solution.py
+++ b/solution.py
@@ -69,7 +69,7 @@
         pack_kernel,
         out_shape=(shape, shape),
         in_specs=[smem, smem, hbm, hbm, hbm, hbm],
-        out_specs=(hbm, hbm),
+        out_specs=(pl.BlockSpec(memory_space=pltpu.VMEM), pl.BlockSpec(memory_space=pltpu.VMEM)),
         scratch_shapes=[
             pltpu.SemaphoreType.DMA((32,)),
             pltpu.SemaphoreType.DMA((32,)),
@@ -205,12 +205,11 @@
     return lax.ppermute(x, axis, [(n, (n - 1) % 4) for n in range(4)])
 
 
-def ring(x, axis):
+def ring(x, axis, forward):
     from_left = right(x, axis)
     from_right = left(x, axis)
-    first = right(from_left[:HALF], axis)
-    second = left(from_right[HALF:], axis)
-    return [(3, "whole", from_left), (1, "whole", from_right), (2, "first", first), (2, "second", second)]
+    far = right(from_left, axis) if forward else left(from_right, axis)
+    return [(3, from_left), (1, from_right), (2, far)]
 
 
 def slots_of(mask):
@@ -243,15 +242,15 @@
     b_pieces = []
     for z, own_a, own_b in ((0, a, b), (1, a_other, b_other)):
         add("a", "whole", (zh ^ z) * 4 + x, own_a)
-        for shift, part, piece in ring(own_a, "x"):
-            add("a", part, (zh ^ z) * 4 + (x + shift) % 4, piece)
-        b_pieces.append((z, 0, "whole", own_b))
-        for shift, part, piece in ring(own_b, "y"):
-            b_pieces.append((z, shift, part, piece))
-    for z, shift, part, piece in b_pieces:
+        for shift, piece in ring(own_a, "x", z == 0):
+            add("a", "whole", (zh ^ z) * 4 + (x + shift) % 4, piece)
+        b_pieces.append((z, 0, own_b))
+        for shift, piece in ring(own_b, "y", z == 0):
+            b_pieces.append((z, shift, piece))
+    for z, shift, piece in b_pieces:
         chip = (zl ^ z) * 8 + ((y + shift) % 4) * 2
-        add("b", part, chip + core, piece)
-        add("b", part, chip + 1 - core, swap(piece, "core"))
+        add("b", "whole", chip + core, piece)
+        add("b", "whole", chip + 1 - core, swap(piece, "core"))
     return product(tuple(plan), jnp.stack(where).astype(jnp.int32), keep_tile, pieces)
 
 

time: 229 us -> 198 us (0.86)
  the two profiles are of different devices: /device:TPU:32 before, /device:TPU:63 now
where the time goes in v2:
time: 198 us; the launch traced here: 197 us
  waiting for transfers between devices  128 us (65%)
  Pallas kernels  33.7 us (17%)
  starting transfers between devices  27.8 us (14%)
  local copies, waits for them, and re-layouts  5.79 us (3%)
  other arithmetic  2.21 us (1%)
    ppermute x6, waiting for transfers between devices, right(): return lax.ppermute(x, axis, [(n, (n + 1) % 4) for n in range(4)])  67.7 us
    ppermute x10, waiting for transfers between devices, swap(): return lax.ppermute(x, axis, [(0, 1), (1, 0)])  51.5 us
    pallas_call x1, Pallas kernels, product(): pl.pallas_call(functools.partial(product_kernel, plan), out_shape=jax.Sha...  29.6 us
    ppermute x10, starting transfers between devices, swap(): return lax.ppermute(x, axis, [(0, 1), (1, 0)])  17.9 us
    ppermute x6, waiting for transfers between devices, left(): return lax.ppermute(x, axis, [(n, (n - 1) % 4) for n in range(4)])  8.57 us
    ppermute x6, starting transfers between devices, right(): return lax.ppermute(x, axis, [(n, (n + 1) % 4) for n in range(4)])  6.26 us
    pallas_call x1, Pallas kernels, pack(): pl.pallas_call(pack_kernel, out_shape=(shape, shape), in_specs=[smem, sme...  4.18 us
  transfers between devices with their start and end apart: 22, of which 10 were waited for; matrix products, arithmetic and copies ran while one was open for 0% of the time, Pallas kernels for 0%

profile of v2, /device:TPU:63, one launch (start us, length us, event | category | flops | bytes accessed | tf_op | source)
XLA Modules:
  0.0 197.3 jit_solution(4955358956082340022)
XLA Ops:
  4.1 4.2 %pack.1 = (f32[2568,128]{1,0:T(8,128)}, f32[2568,128]{1,0:T(8,128)}) custom-call(s32[4,8]{1,0:T(4,128)} %am_ref.1, s32[4,8]{1,0:T(4,128)} %bm_ref.1, f32[512,1024]{1,0:T(8,128)} %a_ref.1, f32[512,1024]{1,0:T(8,128)} %b_ref.1, f32[8,128]{1,0:T(8,128)} %pad.13.am_tile, f32[8,128]{1,0:T(8,128)} %pad.14.bm_tile), custom_call_target="tpu_custom_call" | custom-call | tf_op jit(solution)/shard_map/pack/pallas_call | solution.py:68
  8.3 2.8 %collective-permute-start.3 = (f32[2568,128]{1,0:T(8,128)}, f32[2568,128]{1,0:T(8,128)S(1)}, u32[]{:S(2)}, u32[]{:S(2)}) collective-permute-start(f32[2568,128]{1,0:T(8,128)} %get-tuple-element.7.refs_0_), channel_id=1, source_target_pairs={{0,4},{4,0},{1,5},{5,1},{2,6},{6,2},{3,7},{7,3},{8,12},{12,8},{9,1... | collective-permute-start | bytes 3944456 | tf_op jit(solution)/shard_map/ppermute | solution.py:197
  11.5 2.2 %collective-permute-start = (f32[2568,128]{1,0:T(8,128)}, f32[2568,128]{1,0:T(8,128)S(1)}, u32[]{:S(2)}, u32[]{:S(2)}) collective-permute-start(f32[2568,128]{1,0:T(8,128)} %get-tuple-element.7.refs_0_), channel_id=1, source_target_pairs={{0,1},{1,2},{2,3},{3,0},{4,5},{5,6},{6,7},{7,4},{8,9},{9,10},{10,1... | collective-permute-start | bytes 3944456 | tf_op jit(solution)/shard_map/ppermute | solution.py:201
  15.0 24.8 %collective-permute-done.3.refs_4_ = f32[2568,128]{1,0:T(8,128)S(1)} collective-permute-done((f32[2568,128]{1,0:T(8,128)}, f32[2568,128]{1,0:T(8,128)S(1)}, u32[]{:S(2)}, u32[]{:S(2)}) %collective-permute-start.3) | collective-permute-done | bytes 1314848 | tf_op jit(solution)/shard_map/ppermute | solution.py:197
  40.0 1.8 collective-permute-done.1.refs_2_
  41.8 2.0 %collective-permute-start.7 = (f32[2568,128]{1,0:T(8,128)}, f32[2568,128]{1,0:T(8,128)S(1)}, u32[]{:S(2)}, u32[]{:S(2)}) collective-permute-start(f32[2568,128]{1,0:T(8,128)} %get-tuple-element.8.refs_8_), channel_id=1, source_target_pairs={{0,8},{8,0},{1,9},{9,1},{2,10},{10,2},{3,11},{11,3},{4,12},{12,4},... | collective-permute-start | bytes 3944456 | tf_op jit(solution)/shard_map/ppermute | solution.py:197
  43.8 24.7 %collective-permute-done.14.refs_16_ = f32[2568,128]{1,0:T(8,128)S(1)} collective-permute-done((f32[2568,128]{1,0:T(8,128)}, f32[2568,128]{1,0:T(8,128)S(1)}, u32[]{:S(2)}, u32[]{:S(2)}) %collective-permute-start.14) | collective-permute-done | bytes 1314848 | tf_op jit(solution)/shard_map/ppermute | solution.py:197
  68.8 1.4 collective-permute-start.2
  70.7 2.2 %collective-permute-start.16 = (f32[2568,128]{1,0:T(8,128)S(1)}, f32[2568,128]{1,0:T(8,128)}, u32[]{:S(2)}, u32[]{:S(2)}) collective-permute-start(f32[2568,128]{1,0:T(8,128)S(1)} %collective-permute-done.14.refs_16_), channel_id=1, source_target_pairs={{0,16},{16,32},{32,48},{48,0},{1,17},{17,33},{33,49},{49,1},{2,18}... | collective-permute-start | bytes 3944456 | tf_op jit(solution)/shard_map/ppermute | solution.py:201
  72.8 2.8 %collective-permute-done.5.refs_6_ = f32[2568,128]{1,0:T(8,128)} collective-permute-done((f32[2568,128]{1,0:T(8,128)S(1)}, f32[2568,128]{1,0:T(8,128)}, u32[]{:S(2)}, u32[]{:S(2)}) %collective-permute-start.5) | collective-permute-done | bytes 1314848 | tf_op jit(solution)/shard_map/ppermute | solution.py:205
  76.4 21.1 %collective-permute-done.4.refs_5_ = f32[2568,128]{1,0:T(8,128)S(1)} collective-permute-done((f32[2568,128]{1,0:T(8,128)S(1)}, f32[2568,128]{1,0:T(8,128)S(1)}, u32[]{:S(2)}, u32[]{:S(2)}) %collective-permute-start.4) | collective-permute-done | bytes 1314848 | tf_op jit(solution)/shard_map/ppermute | solution.py:201
  97.5 4.3 %collective-permute-start.11 = (f32[2568,128]{1,0:T(8,128)S(1)}, f32[2568,128]{1,0:T(8,128)S(1)}, u32[]{:S(2)}, u32[]{:S(2)}) collective-permute-start(f32[2568,128]{1,0:T(8,128)S(1)} %collective-permute-done.10.refs_12_), channel_id=1, source_target_pairs={{0,8},{8,0},{1,9},{9,1},{2,10},{10,2},{3,11},{11,3},{4,12},{12,4},... | collective-permute-start | bytes 3944456 | tf_op jit(solution)/shard_map/ppermute | solution.py:197
  101.8 23.8 %collective-permute-done.2.refs_3_ = f32[2568,128]{1,0:T(8,128)S(1)} collective-permute-done((f32[2568,128]{1,0:T(8,128)S(1)}, f32[2568,128]{1,0:T(8,128)S(1)}, u32[]{:S(2)}, u32[]{:S(2)}) %collective-permute-start.2) | collective-permute-done | bytes 1314848 | tf_op jit(solution)/shard_map/ppermute | solution.py:201
  125.6 1.0 copy-done.1
  126.6 2.7 %collective-permute-start.9 = (f32[2568,128]{1,0:T(8,128)S(1)}, f32[2568,128]{1,0:T(8,128)S(1)}, u32[]{:S(2)}, u32[]{:S(2)}) collective-permute-start(f32[2568,128]{1,0:T(8,128)S(1)} %collective-permute-done.8.refs_10_), channel_id=1, source_target_pairs={{0,8},{8,0},{1,9},{9,1},{2,10},{10,2},{3,11},{11,3},{4,12},{12,4},... | collective-permute-start | bytes 3944456 | tf_op jit(solution)/shard_map/ppermute | solution.py:197
  129.3 1.5 collective-permute-start.20
  131.9 22.8 %collective-permute-done.12.refs_14_ = f32[2568,128]{1,0:T(8,128)} collective-permute-done((f32[2568,128]{1,0:T(8,128)S(1)}, f32[2568,128]{1,0:T(8,128)}, u32[]{:S(2)}, u32[]{:S(2)}) %collective-permute-start.12) | collective-permute-done | bytes 1314848 | tf_op jit(solution)/shard_map/ppermute | solution.py:201
  154.7 3.3 %collective-permute-start.17 = (f32[2568,128]{1,0:T(8,128)}, f32[2568,128]{1,0:T(8,128)}, u32[]{:S(2)}, u32[]{:S(2)}) collective-permute-start(f32[2568,128]{1,0:T(8,128)} %collective-permute-done.16.refs_18_), channel_id=1, source_target_pairs={{0,8},{8,0},{1,9},{9,1},{2,10},{10,2},{3,11},{11,3},{4,12},{12,4},... | collective-permute-start | bytes 3944456 | tf_op jit(solution)/shard_map/ppermute | solution.py:197
  158.1 3.2 %collective-permute-done.20.refs_22_ = f32[2568,128]{1,0:T(8,128)} collective-permute-done((f32[2568,128]{1,0:T(8,128)}, f32[2568,128]{1,0:T(8,128)}, u32[]{:S(2)}, u32[]{:S(2)}) %collective-permute-start.20) | collective-permute-done | bytes 1314848 | tf_op jit(solution)/shard_map/ppermute | solution.py:205
  161.3 0.9 collective-permute-start.21
  163.1 2.0 %collective-permute-done.21.refs_23_ = f32[2568,128]{1,0:T(8,128)} collective-permute-done((f32[2568,128]{1,0:T(8,128)}, f32[2568,128]{1,0:T(8,128)}, u32[]{:S(2)}, u32[]{:S(2)}) %collective-permute-start.21) | collective-permute-done | bytes 1314848 | tf_op jit(solution)/shard_map/ppermute | solution.py:197
  165.2 1.3 copy-done
  166.5 1.3 copy-done.2
  167.8 29.6 %product.1 = f32[512,1024]{1,0:T(8,128)} custom-call(s32[24]{0:T(128)S(1)} %stack.99.where_ref, s32[64,128]{1,0:T(8,128)S(1)} %pad.12.keep_ref, f32[2568,128]{1,0:T(8,128)S(1)} %copy-done, f32[2568,128]{1,0:T(8,128)S(1)} %collective-permute-done.refs_1_, f32[2568,128]{1,0:T(8,128)S(1)} %collective-permute-done.1.refs_2_, f32[2568,128]{1,0:T(8,128)S(1)} %copy-done.2, ...), custom_call_target="tpu_custom_call" | custom-call | tf_op jit(solution)/shard_map/product/pallas_call | solution.py:174
  (67 shorter events, 9.7 us)
Async XLA Ops:
  4.1 158.1 %copy-start.12 = (s32[4,64,8]{1,2,0:T(8,128)S(1)}, s32[4,64,8]{1,2,0:T(8,128)}, u32[]{:S(2)}) copy-start(s32[4,64,8]{1,2,0:T(8,128)} %param.11) | copy-start | bytes 24580
  8.3 31.5 %collective-permute-start.3 = (f32[2568,128]{1,0:T(8,128)}, f32[2568,128]{1,0:T(8,128)S(1)}, u32[]{:S(2)}, u32[]{:S(2)}) collective-permute-start(f32[2568,128]{1,0:T(8,128)} %get-tuple-element.7.refs_0_), channel_id=1, source_target_pairs={{0,4},{4,0},{1,5},{5,1},{2,6},{6,2},{3,7},{7,3},{8,12},{12,8},{9,1... | collective-permute-start | bytes 3944456 | tf_op jit(solution)/shard_map/ppermute | solution.py:197
  11.1 30.7 %collective-permute-start.1 = (f32[2568,128]{1,0:T(8,128)}, f32[2568,128]{1,0:T(8,128)S(1)}, u32[]{:S(2)}, u32[]{:S(2)}) collective-permute-start(f32[2568,128]{1,0:T(8,128)} %get-tuple-element.7.refs_0_), channel_id=1, source_target_pairs={{0,3},{1,0},{2,1},{3,2},{4,7},{5,4},{6,5},{7,6},{8,11},{9,8},{10,9... | collective-permute-start | bytes 3944456 | tf_op jit(solution)/shard_map/ppermute | solution.py:205
  11.5 32.3 %collective-permute-start = (f32[2568,128]{1,0:T(8,128)}, f32[2568,128]{1,0:T(8,128)S(1)}, u32[]{:S(2)}, u32[]{:S(2)}) collective-permute-start(f32[2568,128]{1,0:T(8,128)} %get-tuple-element.7.refs_0_), channel_id=1, source_target_pairs={{0,1},{1,2},{2,3},{3,0},{4,5},{5,6},{6,7},{7,4},{8,9},{9,10},{10,1... | collective-permute-start | bytes 3944456 | tf_op jit(solution)/shard_map/ppermute | solution.py:201
  13.8 54.7 %collective-permute-start.14 = (f32[2568,128]{1,0:T(8,128)}, f32[2568,128]{1,0:T(8,128)S(1)}, u32[]{:S(2)}, u32[]{:S(2)}) collective-permute-start(f32[2568,128]{1,0:T(8,128)} %get-tuple-element.8.refs_8_), channel_id=1, source_target_pairs={{0,64},{64,0},{1,65},{65,1},{2,66},{66,2},{3,67},{67,3},{4,68},{68... | collective-permute-start | bytes 3944456 | tf_op jit(solution)/shard_map/ppermute | solution.py:197
  14.4 54.3 %collective-permute-start.10 = (f32[2568,128]{1,0:T(8,128)}, f32[2568,128]{1,0:T(8,128)S(1)}, u32[]{:S(2)}, u32[]{:S(2)}) collective-permute-start(f32[2568,128]{1,0:T(8,128)} %get-tuple-element.8.refs_8_), channel_id=1, source_target_pairs={{0,48},{16,0},{32,16},{48,32},{1,49},{17,1},{33,17},{49,33},{2,50}... | collective-permute-start | bytes 3944456 | tf_op jit(solution)/shard_map/ppermute | solution.py:205
  39.8 30.4 %collective-permute-start.8 = (f32[2568,128]{1,0:T(8,128)}, f32[2568,128]{1,0:T(8,128)S(1)}, u32[]{:S(2)}, u32[]{:S(2)}) collective-permute-start(f32[2568,128]{1,0:T(8,128)} %get-tuple-element.8.refs_8_), channel_id=1, source_target_pairs={{0,16},{16,32},{32,48},{48,0},{1,17},{17,33},{33,49},{49,1},{2,18}... | collective-permute-start | bytes 3944456 | tf_op jit(solution)/shard_map/ppermute | solution.py:201
  41.8 28.9 %collective-permute-start.7 = (f32[2568,128]{1,0:T(8,128)}, f32[2568,128]{1,0:T(8,128)S(1)}, u32[]{:S(2)}, u32[]{:S(2)}) collective-permute-start(f32[2568,128]{1,0:T(8,128)} %get-tuple-element.8.refs_8_), channel_id=1, source_target_pairs={{0,8},{8,0},{1,9},{9,1},{2,10},{10,2},{3,11},{11,3},{4,12},{12,4},... | collective-permute-start | bytes 3944456 | tf_op jit(solution)/shard_map/ppermute | solution.py:197
  43.8 31.8 %collective-permute-start.5 = (f32[2568,128]{1,0:T(8,128)S(1)}, f32[2568,128]{1,0:T(8,128)}, u32[]{:S(2)}, u32[]{:S(2)}) collective-permute-start(f32[2568,128]{1,0:T(8,128)S(1)} %collective-permute-done.3.refs_4_), channel_id=1, source_target_pairs={{0,3},{1,0},{2,1},{3,2},{4,7},{5,4},{6,5},{7,6},{8,11},{9,8},{10,9... | collective-permute-start | bytes 3944456 | tf_op jit(solution)/shard_map/ppermute | solution.py:205
  68.5 29.0 %collective-permute-start.4 = (f32[2568,128]{1,0:T(8,128)S(1)}, f32[2568,128]{1,0:T(8,128)S(1)}, u32[]{:S(2)}, u32[]{:S(2)}) collective-permute-start(f32[2568,128]{1,0:T(8,128)S(1)} %collective-permute-done.3.refs_4_), channel_id=1, source_target_pairs={{0,1},{1,2},{2,3},{3,0},{4,5},{5,6},{6,7},{7,4},{8,9},{9,10},{10,1... | collective-permute-start | bytes 3944456 | tf_op jit(solution)/shard_map/ppermute | solution.py:201
  68.8 56.8 %collective-permute-start.2 = (f32[2568,128]{1,0:T(8,128)S(1)}, f32[2568,128]{1,0:T(8,128)S(1)}, u32[]{:S(2)}, u32[]{:S(2)}) collective-permute-start(f32[2568,128]{1,0:T(8,128)S(1)} %collective-permute-done.refs_1_), channel_id=1, source_target_pairs={{0,1},{1,2},{2,3},{3,0},{4,5},{5,6},{6,7},{7,4},{8,9},{9,10},{10,1... | collective-permute-start | bytes 3944456 | tf_op jit(solution)/shard_map/ppermute | solution.py:201
  70.2 56.5 %collective-permute-start.18 = (f32[2568,128]{1,0:T(8,128)S(1)}, f32[2568,128]{1,0:T(8,128)}, u32[]{:S(2)}, u32[]{:S(2)}) collective-permute-start(f32[2568,128]{1,0:T(8,128)S(1)} %collective-permute-done.14.refs_16_), channel_id=1, source_target_pairs={{0,48},{16,0},{32,16},{48,32},{1,49},{17,1},{33,17},{49,33},{2,50}... | collective-permute-start | bytes 3944456 | tf_op jit(solution)/shard_map/ppermute | solution.py:205
  70.7 87.3 %copy-start.7 = (f32[2568,128]{1,0:T(8,128)}, f32[2568,128]{1,0:T(8,128)S(1)}, u32[]{:S(2)}) copy-start(f32[2568,128]{1,0:T(8,128)S(1)} %collective-permute-done.7.refs_9_) | copy-start | bytes 3944452
  70.7 58.6 %collective-permute-start.16 = (f32[2568,128]{1,0:T(8,128)S(1)}, f32[2568,128]{1,0:T(8,128)}, u32[]{:S(2)}, u32[]{:S(2)}) collective-permute-start(f32[2568,128]{1,0:T(8,128)S(1)} %collective-permute-done.14.refs_16_), channel_id=1, source_target_pairs={{0,16},{16,32},{32,48},{48,0},{1,17},{17,33},{33,49},{49,1},{2,18}... | collective-permute-start | bytes 3944456 | tf_op jit(solution)/shard_map/ppermute | solution.py:201
  75.6 55.2 %collective-permute-start.15 = (f32[2568,128]{1,0:T(8,128)S(1)}, f32[2568,128]{1,0:T(8,128)S(1)}, u32[]{:S(2)}, u32[]{:S(2)}) collective-permute-start(f32[2568,128]{1,0:T(8,128)S(1)} %collective-permute-done.14.refs_16_), channel_id=1, source_target_pairs={{0,8},{8,0},{1,9},{9,1},{2,10},{10,2},{3,11},{11,3},{4,12},{12,4},... | collective-permute-start | bytes 3944456 | tf_op jit(solution)/shard_map/ppermute | solution.py:197
  97.5 33.7 %collective-permute-start.11 = (f32[2568,128]{1,0:T(8,128)S(1)}, f32[2568,128]{1,0:T(8,128)S(1)}, u32[]{:S(2)}, u32[]{:S(2)}) collective-permute-start(f32[2568,128]{1,0:T(8,128)S(1)} %collective-permute-done.10.refs_12_), channel_id=1, source_target_pairs={{0,8},{8,0},{1,9},{9,1},{2,10},{10,2},{3,11},{11,3},{4,12},{12,4},... | collective-permute-start | bytes 3944456 | tf_op jit(solution)/shard_map/ppermute | solution.py:197
  126.6 28.1 %collective-permute-start.12 = (f32[2568,128]{1,0:T(8,128)S(1)}, f32[2568,128]{1,0:T(8,128)}, u32[]{:S(2)}, u32[]{:S(2)}) collective-permute-start(f32[2568,128]{1,0:T(8,128)S(1)} %collective-permute-done.8.refs_10_), channel_id=1, source_target_pairs={{0,16},{16,32},{32,48},{48,0},{1,17},{17,33},{33,49},{49,1},{2,18}... | collective-permute-start | bytes 3944456 | tf_op jit(solution)/shard_map/ppermute | solution.py:201
  126.6 31.4 %collective-permute-start.9 = (f32[2568,128]{1,0:T(8,128)S(1)}, f32[2568,128]{1,0:T(8,128)S(1)}, u32[]{:S(2)}, u32[]{:S(2)}) collective-permute-start(f32[2568,128]{1,0:T(8,128)S(1)} %collective-permute-done.8.refs_10_), channel_id=1, source_target_pairs={{0,8},{8,0},{1,9},{9,1},{2,10},{10,2},{3,11},{11,3},{4,12},{12,4},... | collective-permute-start | bytes 3944456 | tf_op jit(solution)/shard_map/ppermute | solution.py:197
  129.3 32.0 %collective-permute-start.20 = (f32[2568,128]{1,0:T(8,128)}, f32[2568,128]{1,0:T(8,128)}, u32[]{:S(2)}, u32[]{:S(2)}) collective-permute-start(f32[2568,128]{1,0:T(8,128)} %collective-permute-done.18.refs_20_), channel_id=1, source_target_pairs={{0,48},{16,0},{32,16},{48,32},{1,49},{17,1},{33,17},{49,33},{2,50}... | collective-permute-start | bytes 3944456 | tf_op jit(solution)/shard_map/ppermute | solution.py:205
  130.8 32.3 %collective-permute-start.19 = (f32[2568,128]{1,0:T(8,128)}, f32[2568,128]{1,0:T(8,128)}, u32[]{:S(2)}, u32[]{:S(2)}) collective-permute-start(f32[2568,128]{1,0:T(8,128)} %collective-permute-done.18.refs_20_), channel_id=1, source_target_pairs={{0,8},{8,0},{1,9},{9,1},{2,10},{10,2},{3,11},{11,3},{4,12},{12,4},... | collective-permute-start | bytes 3944456 | tf_op jit(solution)/shard_map/ppermute | solution.py:197
  131.2 31.9 %collective-permute-start.6 = (f32[2568,128]{1,0:T(8,128)}, f32[2568,128]{1,0:T(8,128)}, u32[]{:S(2)}, u32[]{:S(2)}) collective-permute-start(f32[2568,128]{1,0:T(8,128)} %collective-permute-done.5.refs_6_), channel_id=1, source_target_pairs={{0,3},{1,0},{2,1},{3,2},{4,7},{5,4},{6,5},{7,6},{8,11},{9,8},{10,9... | collective-permute-start | bytes 3944456 | tf_op jit(solution)/shard_map/ppermute | solution.py:205
  154.7 8.4 %collective-permute-start.17 = (f32[2568,128]{1,0:T(8,128)}, f32[2568,128]{1,0:T(8,128)}, u32[]{:S(2)}, u32[]{:S(2)}) collective-permute-start(f32[2568,128]{1,0:T(8,128)} %collective-permute-done.16.refs_18_), channel_id=1, source_target_pairs={{0,8},{8,0},{1,9},{9,1},{2,10},{10,2},{3,11},{11,3},{4,12},{12,4},... | collective-permute-start | bytes 3944456 | tf_op jit(solution)/shard_map/ppermute | solution.py:197
  158.0 5.1 %collective-permute-start.13 = (f32[2568,128]{1,0:T(8,128)}, f32[2568,128]{1,0:T(8,128)}, u32[]{:S(2)}, u32[]{:S(2)}) collective-permute-start(f32[2568,128]{1,0:T(8,128)} %collective-permute-done.12.refs_14_), channel_id=1, source_target_pairs={{0,8},{8,0},{1,9},{9,1},{2,10},{10,2},{3,11},{11,3},{4,12},{12,4},... | collective-permute-start | bytes 3944456 | tf_op jit(solution)/shard_map/ppermute | solution.py:197
  161.3 3.9 %collective-permute-start.21 = (f32[2568,128]{1,0:T(8,128)}, f32[2568,128]{1,0:T(8,128)}, u32[]{:S(2)}, u32[]{:S(2)}) collective-permute-start(f32[2568,128]{1,0:T(8,128)} %collective-permute-done.20.refs_22_), channel_id=1, source_target_pairs={{0,8},{8,0},{1,9},{9,1},{2,10},{10,2},{3,11},{11,3},{4,12},{12,4},... | collective-permute-start | bytes 3944456 | tf_op jit(solution)/shard_map/ppermute | solution.py:197
  (11 other events, 396.9 us)

commit v3 on v2

--- a/solution.py
+++ b/solution.py
@@ -205,11 +205,17 @@
     return lax.ppermute(x, axis, [(n, (n - 1) % 4) for n in range(4)])
 
 
-def ring(x, axis, forward):
-    from_left = right(x, axis)
-    from_right = left(x, axis)
-    far = right(from_left, axis) if forward else left(from_right, axis)
-    return [(3, from_left), (1, from_right), (2, far)]
+def opposite(from_left, from_right, core, axis):
+    if axis == "x":
+        axes, at = ("core", "x"), lambda n, c: c * 4 + n % 4
+    else:
+        axes, at = ("y", "core"), lambda n, c: n % 4 * 2 + c
+    pairs = [(at(n, c), at(n + 1 - 2 * c, c)) for n in range(4) for c in range(2)]
+    return lax.ppermute(jnp.where(core == 0, from_left, from_right), axes, pairs)
+
+
+def after(x, *others):
+    return lax.optimization_barrier((x, *others))[0]
 
 
 def slots_of(mask):
@@ -237,20 +243,37 @@
         where.append(at)
         pieces.append(piece)
 
-    a_other = swap(a, "zh")
-    b_other = swap(b, "zl")
-    b_pieces = []
-    for z, own_a, own_b in ((0, a, b), (1, a_other, b_other)):
-        add("a", "whole", (zh ^ z) * 4 + x, own_a)
-        for shift, piece in ring(own_a, "x", z == 0):
+    az = swap(a, "zh")
+    ar, al = right(a, "x"), left(a, "x")
+    br, bl = right(b, "y"), left(b, "y")
+    phase = (az, ar, al, br, bl)
+    ao = opposite(ar, al, core, "x")
+    bo = opposite(br, bl, core, "y")
+    bz = swap(after(b, *phase), "zl")
+    azr, azl = right(after(az, *phase), "x"), left(after(az, *phase), "x")
+    cb = swap(after(b, ao, bo), "core")
+    cr = swap(after(br, ao, bo), "core")
+    cl = swap(after(bl, cb, cr), "core")
+    co = swap(after(bo, cb, cr), "core")
+    phase = (bz, cl, co)
+    bzr, bzl = right(after(bz, *phase), "y"), left(after(bz, *phase), "y")
+    azo = opposite(after(azr, azl, *phase), after(azl, azr, *phase), core, "x")
+    cz = swap(after(bz, *phase), "core")
+    phase = (bzr, bzl, cz)
+    bzo = opposite(after(bzr, *phase), after(bzl, *phase), core, "y")
+    czr = swap(after(bzr, *phase), "core")
+    czl = swap(after(bzl, *phase), "core")
+    czo = swap(bzo, "core")
+    for z, group in ((0, ((0, a), (3, ar), (1, al), (2, ao))), (1, ((0, az), (3, azr), (1, azl), (2, azo)))):
+        for shift, piece in group:
             add("a", "whole", (zh ^ z) * 4 + (x + shift) % 4, piece)
-        b_pieces.append((z, 0, own_b))
-        for shift, piece in ring(own_b, "y", z == 0):
-            b_pieces.append((z, shift, piece))
-    for z, shift, piece in b_pieces:
-        chip = (zl ^ z) * 8 + ((y + shift) % 4) * 2
-        add("b", "whole", chip + core, piece)
-        add("b", "whole", chip + 1 - core, swap(piece, "core"))
+    near = ((0, b, cb), (3, br, cr), (1, bl, cl), (2, bo, co))
+    far = ((0, bz, cz), (3, bzr, czr), (1, bzl, czl), (2, bzo, czo))
+    for z, group in ((0, near), (1, far)):
+        for shift, mine, other in group:
+            chip = (zl ^ z) * 8 + ((y + shift) % 4) * 2
+            add("b", "whole", chip + core, mine)
+            add("b", "whole", chip + 1 - core, other)
     return product(tuple(plan), jnp.stack(where).astype(jnp.int32), keep_tile, pieces)
 
 

time: 198 us -> 197 us (level)
  the two profiles are of different devices: /device:TPU:63 before, /device:TPU:72 now
where the time goes in v3:
time: 197 us
  waiting for transfers between devices  136 us (69%)
  Pallas kernels  33.9 us (17%)
  starting transfers between devices  15.4 us (8%)
  other arithmetic  6.75 us (3%)
  local copies, waits for them, and re-layouts  4.91 us (2%)
    ppermute x4, waiting for transfers between devices, left(): return lax.ppermute(x, axis, [(n, (n - 1) % 4) for n in range(4)])  51.9 us
    ppermute x10, waiting for transfers between devices, swap(): return lax.ppermute(x, axis, [(0, 1), (1, 0)])  41 us
    ppermute x4, waiting for transfers between devices, opposite(): lax.ppermute(jnp.where(core == 0, from_left, from_right), axes, pairs)  35.3 us
    pallas_call x1, Pallas kernels, product(): pl.pallas_call(functools.partial(product_kernel, plan), out_shape=jax.Sha...  29.7 us
    ppermute x4, waiting for transfers between devices, right(): return lax.ppermute(x, axis, [(n, (n + 1) % 4) for n in range(4)])  7.5 us
    ppermute x4, starting transfers between devices, left(): return lax.ppermute(x, axis, [(n, (n - 1) % 4) for n in range(4)])  6.98 us
    select_n x4, other arithmetic, opposite(): jnp.where(core == 0, from_left, from_right)  4.54 us
    pallas_call x1, Pallas kernels, pack(): pl.pallas_call(pack_kernel, out_shape=(shape, shape), in_specs=[smem, sme...  4.17 us
  transfers between devices with their start and end apart: 22, of which 13 were waited for; matrix products, arithmetic and copies ran while one was open for 2% of the time, Pallas kernels for 0%

profile of v3, /device:TPU:72, one launch (start us, length us, event | category | flops | bytes accessed | tf_op | source)
XLA Modules:
  0.0 196.9 jit_solution(18280646077501917386)
XLA Ops:
  4.1 4.2 %pack.1 = (f32[2568,128]{1,0:T(8,128)}, f32[2568,128]{1,0:T(8,128)}) custom-call(s32[4,8]{1,0:T(4,128)} %am_ref.1, s32[4,8]{1,0:T(4,128)} %bm_ref.1, f32[512,1024]{1,0:T(8,128)} %a_ref.1, f32[512,1024]{1,0:T(8,128)} %b_ref.1, f32[8,128]{1,0:T(8,128)} %pad.13.am_tile, f32[8,128]{1,0:T(8,128)} %pad.14.bm_tile), custom_call_target="tpu_custom_call" | custom-call | tf_op jit(solution)/shard_map/pack/pallas_call | solution.py:68
  8.3 2.8 %collective-permute-start.1 = (f32[2568,128]{1,0:T(8,128)}, f32[2568,128]{1,0:T(8,128)S(1)}, u32[]{:S(2)}, u32[]{:S(2)}) collective-permute-start(f32[2568,128]{1,0:T(8,128)} %get-tuple-element.18.refs_0_), channel_id=1, source_target_pairs={{0,3},{1,0},{2,1},{3,2},{4,7},{5,4},{6,5},{7,6},{8,11},{9,8},{10,9... | collective-permute-start | bytes 3944456 | tf_op jit(solution)/shard_map/ppermute | solution.py:205
  11.5 1.6 collective-permute-start.4
  13.1 26.3 %collective-permute-done.1.refs_2_ = f32[2568,128]{1,0:T(8,128)S(1)} collective-permute-done((f32[2568,128]{1,0:T(8,128)}, f32[2568,128]{1,0:T(8,128)S(1)}, u32[]{:S(2)}, u32[]{:S(2)}) %collective-permute-start.1) | collective-permute-done | bytes 1314848 | tf_op jit(solution)/shard_map/ppermute | solution.py:205
  39.4 3.3 %collective-permute-done.refs_1_ = f32[2568,128]{1,0:T(8,128)S(1)} collective-permute-done((f32[2568,128]{1,0:T(8,128)}, f32[2568,128]{1,0:T(8,128)S(1)}, u32[]{:S(2)}, u32[]{:S(2)}) %collective-permute-start) | collective-permute-done | bytes 1314848 | tf_op jit(solution)/shard_map/ppermute | solution.py:201
  43.1 1.6 broadcast_select_fusion.2
  44.7 1.6 collective-permute-start.9
  46.3 15.5 %collective-permute-done.2.refs_3_ = f32[2568,128]{1,0:T(8,128)S(1)} collective-permute-done((f32[2568,128]{1,0:T(8,128)S(1)}, f32[2568,128]{1,0:T(8,128)S(1)}, u32[]{:S(2)}, u32[]{:S(2)}) %collective-permute-start.2) | collective-permute-done | bytes 1314848 | tf_op jit(solution)/shard_map/ppermute | solution.py:214
  61.8 1.3 collective-permute-done.9.refs_14_
  63.7 14.1 %collective-permute-done.3.refs_4_ = f32[2568,128]{1,0:T(8,128)S(1)} collective-permute-done((f32[2568,128]{1,0:T(8,128)S(1)}, f32[2568,128]{1,0:T(8,128)S(1)}, u32[]{:S(2)}, u32[]{:S(2)}) %collective-permute-start.3) | collective-permute-done | bytes 1314848 | tf_op jit(solution)/shard_map/ppermute | solution.py:197
  77.7 1.9 collective-permute-start.8
  80.2 26.9 %collective-permute-done.8.refs_16_ = f32[2568,128]{1,0:T(8,128)S(1)} collective-permute-done((f32[2568,128]{1,0:T(8,128)S(1)}, f32[2568,128]{1,0:T(8,128)S(1)}, u32[]{:S(2)}, u32[]{:S(2)}) %collective-permute-start.8) | collective-permute-done | bytes 1314848 | tf_op jit(solution)/shard_map/ppermute | solution.py:197
  107.1 1.3 collective-permute-start.17
  109.2 2.4 %collective-permute-start.7 = (f32[2568,128]{1,0:T(8,128)S(1)}, f32[2568,128]{1,0:T(8,128)S(1)}, u32[]{:S(2)}, u32[]{:S(2)}) collective-permute-start(f32[2568,128]{1,0:T(8,128)S(1)} %collective-permute-done.3.refs_4_), channel_id=1, source_target_pairs={{0,3},{1,0},{2,1},{3,2},{4,7},{5,4},{6,5},{7,6},{8,11},{9,8},{10,9... | collective-permute-start | bytes 3944456 | tf_op jit(solution)/shard_map/ppermute | solution.py:205
  111.6 24.2 %collective-permute-done.17.refs_20_ = f32[2568,128]{1,0:T(8,128)} collective-permute-done((f32[2568,128]{1,0:T(8,128)S(1)}, f32[2568,128]{1,0:T(8,128)}, u32[]{:S(2)}, u32[]{:S(2)}) %collective-permute-start.17) | collective-permute-done | bytes 1314848 | tf_op jit(solution)/shard_map/ppermute | solution.py:205
  136.7 1.5 broadcast_select_fusion
  139.1 1.4 collective-permute-done.7.refs_6_
  140.5 3.2 %collective-permute-done.6.refs_5_ = f32[2568,128]{1,0:T(8,128)S(1)} collective-permute-done((f32[2568,128]{1,0:T(8,128)S(1)}, f32[2568,128]{1,0:T(8,128)S(1)}, u32[]{:S(2)}, u32[]{:S(2)}) %collective-permute-start.6) | collective-permute-done | bytes 1314848 | tf_op jit(solution)/shard_map/ppermute | solution.py:201
  143.8 1.4 broadcast_select_fusion.1
  145.8 10.2 %collective-permute-done.20.refs_22_ = f32[2568,128]{1,0:T(8,128)} collective-permute-done((f32[2568,128]{1,0:T(8,128)S(1)}, f32[2568,128]{1,0:T(8,128)}, u32[]{:S(2)}, u32[]{:S(2)}) %collective-permute-start.20) | collective-permute-done | bytes 1314848 | tf_op jit(solution)/shard_map/ppermute | solution.py:214
  156.2 8.2 %collective-permute-done.14.refs_7_ = f32[2568,128]{1,0:T(8,128)} collective-permute-done((f32[2568,128]{1,0:T(8,128)}, f32[2568,128]{1,0:T(8,128)}, u32[]{:S(2)}, u32[]{:S(2)}) %collective-permute-start.14) | collective-permute-done | bytes 1314848 | tf_op jit(solution)/shard_map/ppermute | solution.py:214
  164.5 1.3 copy-done.1
  165.8 1.3 copy-done.3
  167.1 29.7 %product.1 = f32[512,1024]{1,0:T(8,128)} custom-call(s32[24]{0:T(128)S(1)} %stack.99.where_ref, s32[64,128]{1,0:T(8,128)S(1)} %pad.12.keep_ref, f32[2568,128]{1,0:T(8,128)S(1)} %copy-done.1, f32[2568,128]{1,0:T(8,128)S(1)} %collective-permute-done.refs_1_, f32[2568,128]{1,0:T(8,128)S(1)} %collective-permute-done.1.refs_2_, f32[2568,128]{1,0:T(8,128)S(1)} %copy-done.3, ...), custom_call_target="tpu_custom_call" | custom-call | tf_op jit(solution)/shard_map/product/pallas_call | solution.py:174
  (75 shorter events, 9.4 us)
Async XLA Ops:
  8.3 31.2 %collective-permute-start.1 = (f32[2568,128]{1,0:T(8,128)}, f32[2568,128]{1,0:T(8,128)S(1)}, u32[]{:S(2)}, u32[]{:S(2)}) collective-permute-start(f32[2568,128]{1,0:T(8,128)} %get-tuple-element.18.refs_0_), channel_id=1, source_target_pairs={{0,3},{1,0},{2,1},{3,2},{4,7},{5,4},{6,5},{7,6},{8,11},{9,8},{10,9... | collective-permute-start | bytes 3944456 | tf_op jit(solution)/shard_map/ppermute | solution.py:205
  11.1 31.7 %collective-permute-start = (f32[2568,128]{1,0:T(8,128)}, f32[2568,128]{1,0:T(8,128)S(1)}, u32[]{:S(2)}, u32[]{:S(2)}) collective-permute-start(f32[2568,128]{1,0:T(8,128)} %get-tuple-element.18.refs_0_), channel_id=1, source_target_pairs={{0,1},{1,2},{2,3},{3,0},{4,5},{5,6},{6,7},{7,4},{8,9},{9,10},{10,1... | collective-permute-start | bytes 3944456 | tf_op jit(solution)/shard_map/ppermute | solution.py:201
  11.1 31.9 %collective-permute-start.5 = (f32[2568,128]{1,0:T(8,128)}, f32[2568,128]{1,0:T(8,128)}, u32[]{:S(2)}, u32[]{:S(2)}) collective-permute-start(f32[2568,128]{1,0:T(8,128)} %get-tuple-element.22.refs_8_), channel_id=1, source_target_pairs={{0,48},{16,0},{32,16},{48,32},{1,49},{17,1},{33,17},{49,33},{2,50}... | collective-permute-start | bytes 3944456 | tf_op jit(solution)/shard_map/ppermute | solution.py:205
  11.5 31.5 %collective-permute-start.4 = (f32[2568,128]{1,0:T(8,128)}, f32[2568,128]{1,0:T(8,128)}, u32[]{:S(2)}, u32[]{:S(2)}) collective-permute-start(f32[2568,128]{1,0:T(8,128)} %get-tuple-element.22.refs_8_), channel_id=1, source_target_pairs={{0,16},{16,32},{32,48},{48,0},{1,17},{17,33},{33,49},{49,1},{2,18}... | collective-permute-start | bytes 3944456 | tf_op jit(solution)/shard_map/ppermute | solution.py:201
  42.9 18.9 %collective-permute-start.2 = (f32[2568,128]{1,0:T(8,128)S(1)}, f32[2568,128]{1,0:T(8,128)S(1)}, u32[]{:S(2)}, u32[]{:S(2)}) collective-permute-start(f32[2568,128]{1,0:T(8,128)S(1)} %broadcast_select_fusion.3), channel_id=1, source_target_pairs={{0,1},{8,11},{1,2},{9,8},{2,3},{10,9},{3,0},{11,10},{4,5},{12,15},... | collective-permute-start | bytes 3944456 | tf_op jit(solution)/shard_map/ppermute | solution.py:214
  44.7 18.5 %collective-permute-start.9 = (f32[2568,128]{1,0:T(8,128)S(1)}, f32[2568,128]{1,0:T(8,128)S(1)}, u32[]{:S(2)}, u32[]{:S(2)}) collective-permute-start(f32[2568,128]{1,0:T(8,128)S(1)} %broadcast_select_fusion.2), channel_id=1, source_target_pairs={{0,16},{8,56},{16,32},{24,8},{32,48},{40,24},{48,0},{56,40},{1,17}... | collective-permute-start | bytes 3944456 | tf_op jit(solution)/shard_map/ppermute | solution.py:214
  46.3 31.4 %collective-permute-start.3 = (f32[2568,128]{1,0:T(8,128)S(1)}, f32[2568,128]{1,0:T(8,128)S(1)}, u32[]{:S(2)}, u32[]{:S(2)}) collective-permute-start(f32[2568,128]{1,0:T(8,128)S(1)} %copy-done), channel_id=1, source_target_pairs={{0,4},{4,0},{1,5},{5,1},{2,6},{6,2},{3,7},{7,3},{8,12},{12,8},{9,1... | collective-permute-start | bytes 3944456 | tf_op jit(solution)/shard_map/ppermute | solution.py:197
  61.8 76.3 %copy-start.2 = (f32[2568,128]{1,0:T(8,128)}, f32[2568,128]{1,0:T(8,128)S(1)}, u32[]{:S(2)}) copy-start(f32[2568,128]{1,0:T(8,128)S(1)} %collective-permute-done.2.refs_3_) | copy-start | bytes 3944452
  63.1 16.5 %collective-permute-start.10 = (f32[2568,128]{1,0:T(8,128)S(1)}, f32[2568,128]{1,0:T(8,128)S(1)}, u32[]{:S(2)}, u32[]{:S(2)}) collective-permute-start(f32[2568,128]{1,0:T(8,128)S(1)} %copy-done.6), channel_id=1, source_target_pairs={{0,8},{8,0},{1,9},{9,1},{2,10},{10,2},{3,11},{11,3},{4,12},{12,4},... | collective-permute-start | bytes 3944456 | tf_op jit(solution)/shard_map/ppermute | solution.py:197
  63.1 16.5 %collective-permute-start.11 = (f32[2568,128]{1,0:T(8,128)}, f32[2568,128]{1,0:T(8,128)S(1)}, u32[]{:S(2)}, u32[]{:S(2)}) collective-permute-start(f32[2568,128]{1,0:T(8,128)} %collective-permute-done.4.refs_10_), channel_id=1, source_target_pairs={{0,8},{8,0},{1,9},{9,1},{2,10},{10,2},{3,11},{11,3},{4,12},{12,4},... | collective-permute-start | bytes 3944456 | tf_op jit(solution)/shard_map/ppermute | solution.py:197
  77.7 60.5 %copy-start.8 = (f32[2568,128]{1,0:T(8,128)}, f32[2568,128]{1,0:T(8,128)S(1)}, u32[]{:S(2)}) copy-start(f32[2568,128]{1,0:T(8,128)S(1)} %collective-permute-done.3.refs_4_) | copy-start | bytes 3944452
  77.7 29.4 %collective-permute-start.8 = (f32[2568,128]{1,0:T(8,128)S(1)}, f32[2568,128]{1,0:T(8,128)S(1)}, u32[]{:S(2)}, u32[]{:S(2)}) collective-permute-start(f32[2568,128]{1,0:T(8,128)S(1)} %copy-done.6), channel_id=1, source_target_pairs={{0,64},{64,0},{1,65},{65,1},{2,66},{66,2},{3,67},{67,3},{4,68},{68... | collective-permute-start | bytes 3944456 | tf_op jit(solution)/shard_map/ppermute | solution.py:197
  79.6 27.5 %collective-permute-start.12 = (f32[2568,128]{1,0:T(8,128)}, f32[2568,128]{1,0:T(8,128)S(1)}, u32[]{:S(2)}, u32[]{:S(2)}) collective-permute-start(f32[2568,128]{1,0:T(8,128)} %collective-permute-done.5.refs_12_), channel_id=1, source_target_pairs={{0,8},{8,0},{1,9},{9,1},{2,10},{10,2},{3,11},{11,3},{4,12},{12,4},... | collective-permute-start | bytes 3944456 | tf_op jit(solution)/shard_map/ppermute | solution.py:197
  79.7 27.4 %collective-permute-start.13 = (f32[2568,128]{1,0:T(8,128)S(1)}, f32[2568,128]{1,0:T(8,128)S(1)}, u32[]{:S(2)}, u32[]{:S(2)}) collective-permute-start(f32[2568,128]{1,0:T(8,128)S(1)} %collective-permute-done.9.refs_14_), channel_id=1, source_target_pairs={{0,8},{8,0},{1,9},{9,1},{2,10},{10,2},{3,11},{11,3},{4,12},{12,4},... | collective-permute-start | bytes 3944456 | tf_op jit(solution)/shard_map/ppermute | solution.py:197
  107.1 28.6 %collective-permute-start.17 = (f32[2568,128]{1,0:T(8,128)S(1)}, f32[2568,128]{1,0:T(8,128)}, u32[]{:S(2)}, u32[]{:S(2)}) collective-permute-start(f32[2568,128]{1,0:T(8,128)S(1)} %collective-permute-done.8.refs_16_), channel_id=1, source_target_pairs={{0,48},{16,0},{32,16},{48,32},{1,49},{17,1},{33,17},{49,33},{2,50}... | collective-permute-start | bytes 3944456 | tf_op jit(solution)/shard_map/ppermute | solution.py:205
  108.5 28.2 %collective-permute-start.16 = (f32[2568,128]{1,0:T(8,128)S(1)}, f32[2568,128]{1,0:T(8,128)}, u32[]{:S(2)}, u32[]{:S(2)}) collective-permute-start(f32[2568,128]{1,0:T(8,128)S(1)} %collective-permute-done.8.refs_16_), channel_id=1, source_target_pairs={{0,16},{16,32},{32,48},{48,0},{1,17},{17,33},{33,49},{49,1},{2,18}... | collective-permute-start | bytes 3944456 | tf_op jit(solution)/shard_map/ppermute | solution.py:201
  109.2 27.5 %collective-permute-start.15 = (f32[2568,128]{1,0:T(8,128)S(1)}, f32[2568,128]{1,0:T(8,128)}, u32[]{:S(2)}, u32[]{:S(2)}) collective-permute-start(f32[2568,128]{1,0:T(8,128)S(1)} %collective-permute-done.8.refs_16_), channel_id=1, source_target_pairs={{0,8},{8,0},{1,9},{9,1},{2,10},{10,2},{3,11},{11,3},{4,12},{12,4},... | collective-permute-start | bytes 3944456 | tf_op jit(solution)/shard_map/ppermute | solution.py:197
  109.2 31.3 %collective-permute-start.7 = (f32[2568,128]{1,0:T(8,128)S(1)}, f32[2568,128]{1,0:T(8,128)S(1)}, u32[]{:S(2)}, u32[]{:S(2)}) collective-permute-start(f32[2568,128]{1,0:T(8,128)S(1)} %collective-permute-done.3.refs_4_), channel_id=1, source_target_pairs={{0,3},{1,0},{2,1},{3,2},{4,7},{5,4},{6,5},{7,6},{8,11},{9,8},{10,9... | collective-permute-start | bytes 3944456 | tf_op jit(solution)/shard_map/ppermute | solution.py:205
  111.6 32.1 %collective-permute-start.6 = (f32[2568,128]{1,0:T(8,128)S(1)}, f32[2568,128]{1,0:T(8,128)S(1)}, u32[]{:S(2)}, u32[]{:S(2)}) collective-permute-start(f32[2568,128]{1,0:T(8,128)S(1)} %collective-permute-done.3.refs_4_), channel_id=1, source_target_pairs={{0,1},{1,2},{2,3},{3,0},{4,5},{5,6},{6,7},{7,4},{8,9},{9,10},{10,1... | collective-permute-start | bytes 3944456 | tf_op jit(solution)/shard_map/ppermute | solution.py:201
  138.2 17.8 %collective-permute-start.20 = (f32[2568,128]{1,0:T(8,128)S(1)}, f32[2568,128]{1,0:T(8,128)}, u32[]{:S(2)}, u32[]{:S(2)}) collective-permute-start(f32[2568,128]{1,0:T(8,128)S(1)} %broadcast_select_fusion), channel_id=1, source_target_pairs={{0,16},{8,56},{16,32},{24,8},{32,48},{40,24},{48,0},{56,40},{1,17}... | collective-permute-start | bytes 3944456 | tf_op jit(solution)/shard_map/ppermute | solution.py:214
  145.3 19.2 %collective-permute-start.14 = (f32[2568,128]{1,0:T(8,128)}, f32[2568,128]{1,0:T(8,128)}, u32[]{:S(2)}, u32[]{:S(2)}) collective-permute-start(f32[2568,128]{1,0:T(8,128)} %broadcast_select_fusion.1), channel_id=1, source_target_pairs={{0,1},{8,11},{1,2},{9,8},{2,3},{10,9},{3,0},{11,10},{4,5},{12,15},... | collective-permute-start | bytes 3944456 | tf_op jit(solution)/shard_map/ppermute | solution.py:214
  145.3 19.2 %collective-permute-start.18 = (f32[2568,128]{1,0:T(8,128)}, f32[2568,128]{1,0:T(8,128)}, u32[]{:S(2)}, u32[]{:S(2)}) collective-permute-start(f32[2568,128]{1,0:T(8,128)} %collective-permute-done.16.refs_18_), channel_id=1, source_target_pairs={{0,8},{8,0},{1,9},{9,1},{2,10},{10,2},{3,11},{11,3},{4,12},{12,4},... | collective-permute-start | bytes 3944456 | tf_op jit(solution)/shard_map/ppermute | solution.py:197
  145.3 19.2 %collective-permute-start.19 = (f32[2568,128]{1,0:T(8,128)}, f32[2568,128]{1,0:T(8,128)}, u32[]{:S(2)}, u32[]{:S(2)}) collective-permute-start(f32[2568,128]{1,0:T(8,128)} %collective-permute-done.17.refs_20_), channel_id=1, source_target_pairs={{0,8},{8,0},{1,9},{9,1},{2,10},{10,2},{3,11},{11,3},{4,12},{12,4},... | collective-permute-start | bytes 3944456 | tf_op jit(solution)/shard_map/ppermute | solution.py:197
  156.0 8.5 %collective-permute-start.21 = (f32[2568,128]{1,0:T(8,128)}, f32[2568,128]{1,0:T(8,128)}, u32[]{:S(2)}, u32[]{:S(2)}) collective-permute-start(f32[2568,128]{1,0:T(8,128)} %collective-permute-done.20.refs_22_), channel_id=1, source_target_pairs={{0,8},{8,0},{1,9},{9,1},{2,10},{10,2},{3,11},{11,3},{4,12},{12,4},... | collective-permute-start | bytes 3944456 | tf_op jit(solution)/shard_map/ppermute | solution.py:197
  (13 other events, 220.8 us)

commit v4 on v2

v4 whole, which is shorter than its diff:
```python
import functools

import jax
import jax.numpy as jnp
import numpy as np
from jax import lax
from jax.experimental import pallas as pl
from jax.experimental.pallas import tpu as pltpu
from jax.sharding import Mesh
from jax.sharding import PartitionSpec as P

W = 128
SLOTS = 10
DATA = SLOTS * W
ROWS = DATA + 8
HALF = DATA // 2
ROW = ("zl", "y", "core")
COL = ("zh", "x")


def pack_kernel(am_ref, bm_ref, a_ref, b_ref, am_tile, bm_tile, pa_ref, pb_ref, qa_ref, qb_ref, sem_a, sem_b):
    pa_ref[pl.ds(DATA, 8), :] = am_tile[...]
    pb_ref[pl.ds(DATA, 8), :] = bm_tile[...]

    def copy(src, dst, sem, r, c, cols, at):
        return pltpu.make_async_copy(
            src.at[pl.ds(r * W, W), pl.ds(c * W, W)], dst.at[pl.ds(at, W), :], sem.at[r * cols + c]
        )

    def move(mask, src, main, rest, sem):
        rows, cols = mask.shape
        slot = jnp.int32(0)
        for r in range(rows):
            for c in range(cols):
                on = mask[r, c] != 0

                @pl.when(on & (slot < SLOTS))
                def _():
                    copy(src, main, sem, r, c, cols, pl.multiple_of(slot * W, W)).start()

                @pl.when(on & (slot >= SLOTS) & (slot < 2 * SLOTS))
                def _():
                    copy(src, rest, sem, r, c, cols, pl.multiple_of((slot - SLOTS) * W, W)).start()

                slot = slot + on.astype(jnp.int32)

    def finish(mask, src, main, sem):
        rows, cols = mask.shape
        for r in range(rows):
            for c in range(cols):

                @pl.when(mask[r, c] != 0)
                def _():
                    copy(src, main, sem, r, c, cols, 0).wait()

    move(am_ref, a_ref, pa_ref, qa_ref, sem_a)
    move(bm_ref, b_ref, pb_ref, qb_ref, sem_b)
    finish(am_ref, a_ref, pa_ref, sem_a)
    finish(bm_ref, b_ref, pb_ref, sem_b)


def pack(a_mask, b_mask, a_values, b_values, a_tile, b_tile):
    smem = pl.BlockSpec(memory_space=pltpu.SMEM)
    vmem = pl.BlockSpec(memory_space=pltpu.VMEM)
    hbm = pl.BlockSpec(memory_space=pl.ANY)
    main = jax.ShapeDtypeStruct((ROWS, W), jnp.float32)
    rest = jax.ShapeDtypeStruct((DATA, W), jnp.float32)
    return pl.pallas_call(
        pack_kernel,
        out_shape=(main, main, rest, rest),
        in_specs=[smem, smem, hbm, hbm, vmem, vmem],
        out_specs=(vmem,) * 4,
        scratch_shapes=[pltpu.SemaphoreType.DMA((32,)), pltpu.SemaphoreType.DMA((32,))],
        name="pack",
    )(a_mask, b_mask, a_values, b_values, a_tile, b_tile)


def split(x):
    high = x.astype(jnp.bfloat16)
    low = (x - high.astype(jnp.float32)).astype(jnp.bfloat16)
    return high, low


def product_kernel(plan, spread, where_ref, keep_ref, *refs):
    count = len(plan)
    pieces = refs[:count]
    out_ref, a_all, b_all, a_meta, b_meta, table, words, table_s, words_s, sem, sem_t = refs[count:]
    copies = []
    for n, (data, meta, first, rows) in enumerate(plan):
        at = where_ref[n]
        data = a_all if data == "a" else b_all
        copies.append((pieces[n].at[pl.ds(0, rows), :], data.at[pl.ds(first * W + at * rows, rows), :]))
        if meta:
            meta = a_meta if meta == "a" else b_meta
            copies.append((pieces[n].at[pl.ds(rows, 8), :], meta.at[pl.ds(at * 8, 8), :]))
    copies = [pltpu.make_async_copy(src, dst, sem.at[n]) for n, (src, dst) in enumerate(copies)]
    for copy in copies:
        copy.start()
    for copy in copies:
        copy.wait()

    def address(piece, rank, pieces):
        rest = pieces * SLOTS + rank - (SLOTS + 1)
        if spread:
            rest = rest + piece * SLOTS
        return jnp.where(rank <= SLOTS, piece * SLOTS + rank - 1, rest)

    k8 = lax.broadcasted_iota(jnp.int32, (8, W), 0)
    one = jnp.ones((8, W), jnp.int32)
    low = jnp.zeros((8, W), jnp.int32)
    high = jnp.zeros((8, W), jnp.int32)
    for c in range(8):
        a_slot = a_meta[pl.ds(c * 8, 8), :].astype(jnp.int32)
        b0 = b_meta[pl.ds(c * 16, 8), :].astype(jnp.int32)
        b1 = pltpu.roll(b_meta[pl.ds(c * 16 + 8, 8), :], 4, 0).astype(jnp.int32)
        b_slot = jnp.where(k8 < 4, b0, b1)
        live = (keep_ref[pl.ds(c * 8, 8), :] != 0) & (a_slot > 0) & (b_slot > 0)
        a_at = address(c, a_slot, 8)
        b_at = address(jnp.where(k8 < 4, 2 * c, 2 * c + 1), b_slot, 16)
        table[pl.ds(c * 8, 8), :] = jnp.where(live, a_at + b_at * 65536, 0)
        bit = jnp.where(live, lax.shift_left(one, k8 + 8 * (c % 4)), 0)
        if c < 4:
            low = low | bit
        else:
            high = high | bit
    for n, word in enumerate((low, high)):
        word = word | pltpu.roll(word, 4, 0)
        word = word | pltpu.roll(word, 2, 0)
        word = word | pltpu.roll(word, 1, 0)
        words[pl.ds(8 * n, 8), :] = jnp.where(k8 == 0, word, lax.population_count(word))
    t0 = pltpu.make_async_copy(table, table_s, sem_t.at[0])
    t1 = pltpu.make_async_copy(words, words_s, sem_t.at[1])
    t0.start()
    t1.start()
    t0.wait()
    t1.wait()

    def block(p, _):
        acc = jnp.zeros((W, W), jnp.float32)
        for n in range(2):
            bits = words_s[8 * n, p]

            def step(_, state):
                bits, acc = state
                lowest = bits & -bits
                k = 31 - lax.clz(lowest) + 32 * n
                entry = table_s[k, p]
                a_at = pl.multiple_of((entry & 65535) * W, W)
                b_at = pl.multiple_of(lax.shift_right_logical(entry, 16) * W, W)
                a_high, a_low = split(a_all[pl.ds(a_at, W), :])
                b_high, b_low = split(b_all[pl.ds(b_at, W), :])
                left = jnp.concatenate([a_high, a_low], axis=1)
                right = jnp.concatenate(
                    [jnp.concatenate([b_high, b_low], axis=1), jnp.concatenate([b_low, b_high], axis=1)], axis=0
                )
                both = jnp.dot(left, right, preferred_element_type=jnp.float32)
                return bits ^ lowest, acc + (both[:, :W] + both[:, W:])

            bits, acc = lax.fori_loop(0, words_s[8 * n + 1, p], step, (bits, acc))
        i = p // 8
        j = p - i * 8
        out_ref[pl.ds(pl.multiple_of(i * W, W), W), pl.ds(pl.multiple_of(j * W, W), W)] = acc
        return 0

    lax.fori_loop(0, 32, block, 0)


def product(spread, keep_tile, entries):
    hbm = pl.BlockSpec(memory_space=pl.ANY)
    plan = tuple(entry[:4] for entry in entries)
    where = jnp.stack([jnp.asarray(entry[4], jnp.int32) for entry in entries])
    pieces = [entry[5] for entry in entries]
    more = (8, 16) if spread else (1, 1)
    return pl.pallas_call(
        functools.partial(product_kernel, plan, spread),
        out_shape=jax.ShapeDtypeStruct((512, 1024), jnp.float32),
        in_specs=[pl.BlockSpec(memory_space=pltpu.SMEM), pl.BlockSpec(memory_space=pltpu.VMEM)] + [hbm] * len(pieces),
        out_specs=pl.BlockSpec(memory_space=pltpu.VMEM),
        scratch_shapes=[
            pltpu.VMEM(((8 + more[0]) * DATA, W), jnp.float32),
            pltpu.VMEM(((16 + more[1]) * DATA, W), jnp.float32),
            pltpu.VMEM((64, W), jnp.float32),
            pltpu.VMEM((128, W), jnp.float32),
            pltpu.VMEM((64, W), jnp.int32),
            pltpu.VMEM((16, W), jnp.int32),
            pltpu.SMEM((64, W), jnp.int32),
            pltpu.SMEM((16, W), jnp.int32),
            pltpu.SemaphoreType.DMA((2 * len(pieces),)),
            pltpu.SemaphoreType.DMA((2,)),
        ],
        compiler_params=pltpu.CompilerParams(vmem_limit_bytes=48 * 1024 * 1024),
        name="product",
    )(where, keep_tile, *pieces)


def swap(x, axis):
    return lax.ppermute(x, axis, [(0, 1), (1, 0)])


def right(x, axis):
    return lax.ppermute(x, axis, [(n, (n + 1) % 4) for n in range(4)])


def left(x, axis):
    return lax.ppermute(x, axis, [(n, (n - 1) % 4) for n in range(4)])


def opposite(from_left, from_right, core, axis):
    if axis == "x":
        axes, at = ("core", "x"), lambda n, c: c * 4 + n % 4
    else:
        axes, at = ("y", "core"), lambda n, c: n % 4 * 2 + c
    pairs = [(at(n, c), at(n + 1 - 2 * c, c)) for n in range(4) for c in range(2)]
    return lax.ppermute(jnp.where(core == 0, from_left, from_right), axes, pairs)


def gate(*done):
    return lambda x: lax.optimization_barrier((x, *done))[0]


def pair(x, axis, distance):
    return lax.ppermute(x, axis, [(n, n ^ distance) for n in range(4)])


def around(own, z, axis, core):
    other = swap(own, z)
    found = []
    for x in (own, other):
        r, l = right(x, axis), left(x, axis)
        found.append((x, r, l, opposite(r, l, core, axis)))
    return found


def slots_of(mask):
    flat = (mask.reshape(-1) != 0).astype(jnp.float32)
    n = flat.shape[0]
    upto = jnp.asarray(np.tril(np.ones((n, n), np.float32)))
    rank = jnp.sum(upto * flat[None, :], axis=1)
    return (flat * rank).reshape(mask.shape)


def per_device(a_values, a_mask, b_values, b_mask, keep):
    a_slot = slots_of(a_mask)
    b_slot = slots_of(b_mask)
    a_tile = jnp.pad(jnp.repeat(a_slot.T, 8, axis=1), ((0, 0), (0, W - 32)))
    b_tile = jnp.pad(jnp.tile(b_slot, (1, 4)), ((0, 4), (0, W - 32)))
    keep_tile = jnp.pad(jnp.transpose(keep, (1, 0, 2)).reshape(64, 32), ((0, 0), (0, W - 32)))
    a, b, a_rest, b_rest = pack(a_mask, b_mask, a_values, b_values, a_tile, b_tile)
    zl, y, core = (lax.axis_index(n) for n in ROW)
    zh, x = (lax.axis_index(n) for n in COL)

    az, ar, al, br, bl = swap(a, "zh"), right(a, "x"), left(a, "x"), right(b, "y"), left(b, "y")

    over = [(jnp.sum((m != 0).astype(jnp.int32)) > SLOTS).astype(jnp.float32) for m in (a_mask, b_mask)]
    flags = jnp.concatenate([jnp.full((4, W), n) for n in over])
    mine = [lax.dynamic_slice_in_dim(q, core * HALF, HALF) for q in (a_rest, b_rest)]
    theirs = [lax.dynamic_slice_in_dim(q, (1 - core) * HALF, HALF) for q in (a_rest, b_rest)]

    g = gate(az, ar, al, br, bl)
    bz, azr, azl = swap(g(b), "zl"), right(g(az), "x"), left(g(az), "x")
    bo = opposite(g(br), g(bl), core, "y")
    ec = swap(g(jnp.concatenate([*theirs, flags])), "core")
    cb = swap(gate(ec)(g(b)), "core")
    cr = swap(gate(cb)(g(br)), "core")
    cl = swap(gate(cr)(g(bl)), "core")

    excess = []
    for n in range(2):
        also = ec[2 * HALF + 4 * n, 0]
        piece = jnp.where(over[n] > 0, mine[n], jnp.where(also > 0, ec[n * HALF : (n + 1) * HALF], 0.0))
        excess.append(jnp.concatenate([piece, jnp.full((8, W), over[n] + also)]))
    ea, eb = excess

    g = gate(bz, azr, azl, bo, cl)
    bzr, bzl = right(g(bz), "y"), left(g(bz), "y")
    ao, azo = opposite(g(ar), g(al), core, "x"), opposite(g(azr), g(azl), core, "x")
    cz = swap(g(bz), "core")
    co = swap(gate(cz)(g(bo)), "core")
    eaz = swap(gate(cz)(g(ea)), "zh")
    ebz = swap(gate(co)(g(eb)), "zl")
    ea, eb = ea + eaz, eb + ebz

    g = gate(bzr, bzl, ao, azo, co, eaz, ebz)
    bzo = opposite(g(bzr), g(bzl), core, "y")
    czr = swap(g(bzr), "core")
    czl = swap(gate(czr)(g(bzl)), "core")
    eax, ebx = pair(g(ea), "x", 1), pair(g(eb), "y", 1)
    ea, eb = ea + eax, eb + ebx

    g = gate(bzo, czl, eax, ebx)
    czo = swap(g(bzo), "core")
    eax, ebx = pair(g(ea), "x", 2), pair(g(eb), "y", 2)
    ea, eb = ea + eax, eb + ebx
    last = swap(jnp.concatenate([ea[:HALF], eb[:HALF]]), "core")
    fa, fb = last[:HALF], last[HALF:]

    entries = []
    for z, group in ((0, (a, ar, al, ao)), (1, (az, azr, azl, azo))):
        for shift, piece in zip((0, 3, 1, 2), group):
            entries.append(("a", "a", 0, DATA, (zh ^ z) * 4 + (x + shift) % 4, piece))
    near = ((b, cb), (br, cr), (bl, cl), (bo, co))
    far = ((bz, cz), (bzr, czr), (bzl, czl), (bzo, czo))
    for z, group in ((0, near), (1, far)):
        for shift, both in zip((0, 3, 1, 2), group):
            chip = (zl ^ z) * 8 + ((y + shift) % 4) * 2
            entries.append(("b", "b", 0, DATA, chip + core, both[0]))
            entries.append(("b", "b", 0, DATA, chip + 1 - core, both[1]))
    crowded = [e[HALF, 0] > 1.5 for e in (ea, eb)]

    def few(_):
        more = [
            ("a", "", 8 * SLOTS, HALF, core, ea),
            ("a", "", 8 * SLOTS, HALF, 1 - core, fa),
            ("b", "", 16 * SLOTS, HALF, core, eb),
            ("b", "", 16 * SLOTS, HALF, 1 - core, fb),
        ]
        return product(False, keep_tile, entries + more)

    def many(_):
        def whole(e, f):
            e = e[:HALF]
            return jnp.where(core == 0, jnp.concatenate([e, f]), jnp.concatenate([f, e]))

        def all_a(_):
            near, far = around(a_rest, "zh", "x", core)
            return near + far

        def all_b(_):
            near, far = around(b_rest, "zl", "y", core)
            return near + far + tuple(swap(p, "core") for p in near + far)

        rest_a = lax.cond(crowded[0], all_a, lambda _: (whole(ea, fa),) * 8, 0)
        rest_b = lax.cond(crowded[1], all_b, lambda _: (whole(eb, fb),) * 16, 0)
        more = []
        for n, piece in enumerate(rest_a):
            more.append(("a", "", 8 * SLOTS, DATA, (zh ^ (n // 4)) * 4 + (x + (0, 3, 1, 2)[n % 4]) % 4, piece))
        for n, piece in enumerate(rest_b):
            chip = (zl ^ (n // 4 % 2)) * 8 + ((y + (0, 3, 1, 2)[n % 4]) % 4) * 2
            more.append(("b", "", 16 * SLOTS, DATA, chip + (core if n < 8 else 1 - core), piece))
        return product(True, keep_tile, entries + more)

    return lax.cond(crowded[0] | crowded[1], many, few, 0)


def solution(mesh):
    fine = Mesh(mesh.devices.reshape(2, 4, 2, 2, 4), ROW + COL)
    return jax.shard_map(
        per_device,
        mesh=fine,
        in_specs=(P(ROW, COL), P(ROW, COL), P(ROW, COL), P(ROW, COL), P(ROW, None, COL)),
        out_specs=P(ROW, COL),
        check_vma=False,
    )
```

time: 198 us -> 159 us (0.80)
  the two profiles are of different devices: /device:TPU:63 before, /device:TPU:2 now
where the time goes in v4:
time: 159 us; the launch traced here: 160 us
  waiting for transfers between devices  61.8 us (39%)
  Pallas kernels  33.5 us (21%)
  starting transfers between devices  31.3 us (20%)
  local copies, waits for them, and re-layouts  18.9 us (12%)
  other arithmetic  9.1 us (6%)
  between operations  5.34 us (3%)
    pallas_call x1, Pallas kernels, product(): pl.pallas_call(functools.partial(product_kernel, plan, spread), out_shape...  29.6 us
    ppermute x4, waiting for transfers between devices, pair(): return lax.ppermute(x, axis, [(n, n ^ distance) for n in range(4)])  22 us
    ppermute x14, waiting for transfers between devices, swap(): return lax.ppermute(x, axis, [(0, 1), (1, 0)])  18.4 us
    ppermute x4, waiting for transfers between devices, opposite(): lax.ppermute(jnp.where(core == 0, from_left, from_right), axes, pairs)  15.4 us
    ppermute x14, starting transfers between devices, swap(): return lax.ppermute(x, axis, [(0, 1), (1, 0)])  10.3 us
    ppermute x4, starting transfers between devices, right(): return lax.ppermute(x, axis, [(n, (n + 1) % 4) for n in range(4)])  6.17 us
    ppermute x4, starting transfers between devices, pair(): return lax.ppermute(x, axis, [(n, n ^ distance) for n in range(4)])  5.31 us
    unnamed x22, local copies, waits for them, and re-layouts  5.16 us
  transfers between devices with their start and end apart: 30, of which 17 were waited for; matrix products, arithmetic and copies ran while one was open for 10% of the time, Pallas kernels for 0%

profile of v4, /device:TPU:2, one launch (start us, length us, event | category | flops | bytes accessed | tf_op | source)
XLA Modules:
  0.0 160.0 jit_solution(2982815038817777523)
XLA Ops:
  5.4 3.8 %pack.1 = (f32[1288,128]{1,0:T(8,128)S(1)}, f32[1288,128]{1,0:T(8,128)}, f32[1280,128]{1,0:T(8,128)}, f32[1280,128]{1,0:T(8,128)}) custom-call(s32[4,8]{1,0:T(4,128)} %am_ref.1, s32[4,8]{1,0:T(4,128)} %bm_ref.1, f32[512,1024]{1,0:T(8,128)} %a_ref.1, f32[512,1024]{1,0:T(8,128)} %b_ref.1, f32[8,128]{1,0:T(8,128)} %pad.14.am_tile, f32[8,128]{1,0:T(8,128)} %pad.15.bm_tile), custom_call_target="tpu_custom_call" | custom-call | tf_op jit(solution)/shard_map/pack/pallas_call | solution.py:68
  9.3 1.6 %collective-permute-start.23 = (f32[1288,128]{1,0:T(8,128)S(1)}, f32[1288,128]{1,0:T(8,128)S(1)}, u32[]{:S(2)}, u32[]{:S(2)}) collective-permute-start(f32[1288,128]{1,0:T(8,128)S(1)} %get-tuple-element.443), channel_id=1, source_target_pairs={{0,1},{1,2},{2,3},{3,0},{4,5},{5,6},{6,7},{7,4},{8,9},{9,10},{10,1... | collective-permute-start | bytes 1978376 | tf_op jit(solution)/shard_map/ppermute | solution.py:201
  11.4 3.9 %collective-permute-start.22 = (f32[1288,128]{1,0:T(8,128)S(1)}, f32[1288,128]{1,0:T(8,128)}, u32[]{:S(2)}, u32[]{:S(2)}) collective-permute-start(f32[1288,128]{1,0:T(8,128)S(1)} %get-tuple-element.443), channel_id=1, source_target_pairs={{0,4},{4,0},{1,5},{5,1},{2,6},{6,2},{3,7},{7,3},{8,12},{12,8},{9,1... | collective-permute-start | bytes 1978376 | tf_op jit(solution)/shard_map/ppermute | solution.py:197
  16.8 1.7 %collective-permute-start.26 = (f32[1288,128]{1,0:T(8,128)}, f32[1288,128]{1,0:T(8,128)S(1)}, u32[]{:S(2)}, u32[]{:S(2)}) collective-permute-start(f32[1288,128]{1,0:T(8,128)} %get-tuple-element.450), channel_id=1, source_target_pairs={{0,48},{16,0},{32,16},{48,32},{1,49},{17,1},{33,17},{49,33},{2,50}... | collective-permute-start | bytes 1978376 | tf_op jit(solution)/shard_map/ppermute | solution.py:205
  19.8 2.0 %constant_dynamic-slice_fusion = (f32[640,128]{1,0:T(8,128)}, f32[640,128]{1,0:T(8,128)}) fusion(f32[1280,128]{1,0:T(8,128)} %get-tuple-element.442, s32[]{:T(128)S(6)} %select_n.207, f32[1280,128]{1,0:T(8,128)} %get-tuple-element.441), kind=kLoop, calls=%fused_computation.23 | loop fusion | bytes 1310724 | tf_op jit(solution)/shard_map/dynamic_slice | solution.py:257
  21.8 4.0 %concatenate.24 = f32[1288,128]{1,0:T(8,128)} concatenate(f32[640,128]{1,0:T(8,128)} %get-tuple-element.718, f32[640,128]{1,0:T(8,128)} %get-tuple-element.717, f32[4,128]{1,0:T(4,128)S(1)} %broadcast_in_dim.19, f32[4,128]{1,0:T(4,128)S(1)} %broadcast_in_dim.20), dimensions={0} | concatenate | bytes 1318912 | tf_op jit(solution)/shard_map/concatenate | solution.py:262
  27.2 2.5 %collective-permute-done.22 = f32[1288,128]{1,0:T(8,128)} collective-permute-done((f32[1288,128]{1,0:T(8,128)S(1)}, f32[1288,128]{1,0:T(8,128)}, u32[]{:S(2)}, u32[]{:S(2)}) %collective-permute-start.22) | collective-permute-done | bytes 659488 | tf_op jit(solution)/shard_map/ppermute | solution.py:197
  29.7 3.0 %collective-permute-done.25 = f32[1288,128]{1,0:T(8,128)S(1)} collective-permute-done((f32[1288,128]{1,0:T(8,128)}, f32[1288,128]{1,0:T(8,128)S(1)}, u32[]{:S(2)}, u32[]{:S(2)}) %collective-permute-start.25) | collective-permute-done | bytes 659488 | tf_op jit(solution)/shard_map/ppermute | solution.py:201
  32.6 2.3 %collective-permute-done.27 = f32[1288,128]{1,0:T(8,128)S(1)} collective-permute-done((f32[1288,128]{1,0:T(8,128)}, f32[1288,128]{1,0:T(8,128)S(1)}, u32[]{:S(2)}, u32[]{:S(2)}) %collective-permute-start.27) | collective-permute-done | bytes 659488 | tf_op jit(solution)/shard_map/ppermute | solution.py:197
  35.8 1.6 collective-permute-done.32
  40.6 1.6 %collective-permute-start.31 = (f32[1288,128]{1,0:T(8,128)S(1)}, f32[1288,128]{1,0:T(8,128)S(1)}, u32[]{:S(2)}, u32[]{:S(2)}) collective-permute-start(f32[1288,128]{1,0:T(8,128)S(1)} %broadcast_select_fusion.7), channel_id=1, source_target_pairs={{0,16},{8,56},{16,32},{24,8},{32,48},{40,24},{48,0},{56,40},{1,17}... | collective-permute-start | bytes 1978376 | tf_op jit(solution)/shard_map/ppermute | solution.py:214
  42.8 9.6 %collective-permute-done.31 = f32[1288,128]{1,0:T(8,128)S(1)} collective-permute-done((f32[1288,128]{1,0:T(8,128)S(1)}, f32[1288,128]{1,0:T(8,128)S(1)}, u32[]{:S(2)}, u32[]{:S(2)}) %collective-permute-start.31) | collective-permute-done | bytes 659488 | tf_op jit(solution)/shard_map/ppermute | solution.py:214
  52.5 2.4 %collective-permute-done.28 = f32[1288,128]{1,0:T(8,128)} collective-permute-done((f32[1288,128]{1,0:T(8,128)}, f32[1288,128]{1,0:T(8,128)}, u32[]{:S(2)}, u32[]{:S(2)}) %collective-permute-start.28) | collective-permute-done | bytes 659488 | tf_op jit(solution)/shard_map/ppermute | solution.py:197
  59.9 1.6 %collective-permute-start.38 = (f32[1288,128]{1,0:T(8,128)}, f32[1288,128]{1,0:T(8,128)}, u32[]{:S(2)}, u32[]{:S(2)}) collective-permute-start(f32[1288,128]{1,0:T(8,128)} %collective-permute-done.28), channel_id=1, source_target_pairs={{0,48},{16,0},{32,16},{48,32},{1,49},{17,1},{33,17},{49,33},{2,50}... | collective-permute-start | bytes 1978376 | tf_op jit(solution)/shard_map/ppermute | solution.py:205
  66.0 1.6 collective-permute-start.39
  74.7 5.7 %collective-permute-done.39 = f32[1288,128]{1,0:T(8,128)} collective-permute-done((f32[1288,128]{1,0:T(8,128)}, f32[1288,128]{1,0:T(8,128)}, u32[]{:S(2)}, u32[]{:S(2)}) %collective-permute-start.39) | collective-permute-done | bytes 659488 | tf_op jit(solution)/shard_map/ppermute | solution.py:214
  80.5 4.7 %collective-permute-done.36 = f32[648,128]{1,0:T(8,128)S(1)} collective-permute-done((f32[648,128]{1,0:T(8,128)S(1)}, f32[648,128]{1,0:T(8,128)S(1)}, u32[]{:S(2)}, u32[]{:S(2)}) %collective-permute-start.36) | collective-permute-done | bytes 331808 | tf_op jit(solution)/shard_map/ppermute | solution.py:197
  85.2 4.4 %collective-permute-done.42 = f32[648,128]{1,0:T(8,128)S(1)} collective-permute-done((f32[648,128]{1,0:T(8,128)S(1)}, f32[648,128]{1,0:T(8,128)S(1)}, u32[]{:S(2)}, u32[]{:S(2)}) %collective-permute-start.42) | collective-permute-done | bytes 331808 | tf_op jit(solution)/shard_map/ppermute | solution.py:197
  94.2 12.5 %collective-permute-done.47 = f32[648,128]{1,0:T(8,128)S(1)} collective-permute-done((f32[648,128]{1,0:T(8,128)S(1)}, f32[648,128]{1,0:T(8,128)S(1)}, u32[]{:S(2)}, u32[]{:S(2)}) %collective-permute-start.47) | collective-permute-done | bytes 331808 | tf_op jit(solution)/shard_map/ppermute | solution.py:222
  106.8 2.8 %collective-permute-start.49 = (f32[648,128]{1,0:T(8,128)S(1)}, f32[648,128]{1,0:T(8,128)S(1)}, u32[]{:S(2)}, u32[]{:S(2)}) collective-permute-start(f32[648,128]{1,0:T(8,128)S(1)} %add.377), channel_id=1, source_target_pairs={{0,32},{16,48},{32,0},{48,16},{1,33},{17,49},{33,1},{49,17},{2,34}... | collective-permute-start | bytes 995336 | tf_op jit(solution)/shard_map/ppermute | solution.py:222
  110.7 8.1 %collective-permute-done.49 = f32[648,128]{1,0:T(8,128)S(1)} collective-permute-done((f32[648,128]{1,0:T(8,128)S(1)}, f32[648,128]{1,0:T(8,128)S(1)}, u32[]{:S(2)}, u32[]{:S(2)}) %collective-permute-start.49) | collective-permute-done | bytes 331808 | tf_op jit(solution)/shard_map/ppermute | solution.py:222
  126.9 1.9 %fusion.3 = (f32[640,128]{1,0:T(8,128)}, f32[640,128]{1,0:T(8,128)}) fusion(f32[1280,128]{1,0:T(8,128)} %collective-permute-done.51), kind=kLoop, calls=%fused_computation.28 | loop fusion | bytes 1310720 | tf_op jit(solution)/shard_map/slice | solution.py:295
  128.8 29.8 %conditional.3 = (f32[512,1024]{1,0:T(8,128)S(1)}) conditional(s32[]{:T(128)} %convert_element_type.53, (s32[]{:T(128)}, s32[]{:T(128)}, s32[]{:T(128)}, s32[]{:T(128)}, s32[]{:T(128)}, /*index=5*/s32[]{:T(128)}, s32[]{:T(128)}, s32[]{:T(128)}, s32[]{:T(128)}, s32[]{:T(128)}, /*index=10*/s32[]{:T(128)}, s32[]{:T(128)}, s32[]{:T(128)}, s32[]{:T(128)}, ...), branch_computations={%region_4.5_spmd, %region_5.10_spmd} | conditional | flops 983181 | bytes 78744648 | solution.py:342
  129.0 29.6 %product.2 = f32[512,1024]{1,0:T(8,128)S(1)} custom-call(s32[28]{0:T(128)S(1)} %stack.180.where_ref, s32[64,128]{1,0:T(8,128)S(1)} %copy.16.keep_ref, f32[1288,128]{1,0:T(8,128)} %get-tuple-element.286.refs_0_, f32[1288,128]{1,0:T(8,128)S(1)} %get-tuple-element.287.refs_1_, f32[1288,128]{1,0:T(8,128)S(1)} %get-tuple-element.288.refs_2_, ...), custom_call_target="tpu_custom_call" | custom-call | tf_op jit(solution)/shard_map/cond/branch_0_fun/product/pallas_call | solution.py:174
  (106 shorter events, 41.6 us)
Async XLA Ops:
  9.3 16.6 %collective-permute-start.23 = (f32[1288,128]{1,0:T(8,128)S(1)}, f32[1288,128]{1,0:T(8,128)S(1)}, u32[]{:S(2)}, u32[]{:S(2)}) collective-permute-start(f32[1288,128]{1,0:T(8,128)S(1)} %get-tuple-element.443), channel_id=1, source_target_pairs={{0,1},{1,2},{2,3},{3,0},{4,5},{5,6},{6,7},{7,4},{8,9},{9,10},{10,1... | collective-permute-start | bytes 1978376 | tf_op jit(solution)/shard_map/ppermute | solution.py:201
  10.9 16.3 %collective-permute-start.24 = (f32[1288,128]{1,0:T(8,128)S(1)}, f32[1288,128]{1,0:T(8,128)S(1)}, u32[]{:S(2)}, u32[]{:S(2)}) collective-permute-start(f32[1288,128]{1,0:T(8,128)S(1)} %get-tuple-element.443), channel_id=1, source_target_pairs={{0,3},{1,0},{2,1},{3,2},{4,7},{5,4},{6,5},{7,6},{8,11},{9,8},{10,9... | collective-permute-start | bytes 1978376 | tf_op jit(solution)/shard_map/ppermute | solution.py:205
  11.4 18.3 %collective-permute-start.22 = (f32[1288,128]{1,0:T(8,128)S(1)}, f32[1288,128]{1,0:T(8,128)}, u32[]{:S(2)}, u32[]{:S(2)}) collective-permute-start(f32[1288,128]{1,0:T(8,128)S(1)} %get-tuple-element.443), channel_id=1, source_target_pairs={{0,4},{4,0},{1,5},{5,1},{2,6},{6,2},{3,7},{7,3},{8,12},{12,8},{9,1... | collective-permute-start | bytes 1978376 | tf_op jit(solution)/shard_map/ppermute | solution.py:197
  15.3 17.3 %collective-permute-start.25 = (f32[1288,128]{1,0:T(8,128)}, f32[1288,128]{1,0:T(8,128)S(1)}, u32[]{:S(2)}, u32[]{:S(2)}) collective-permute-start(f32[1288,128]{1,0:T(8,128)} %get-tuple-element.450), channel_id=1, source_target_pairs={{0,16},{16,32},{32,48},{48,0},{1,17},{17,33},{33,49},{49,1},{2,18}... | collective-permute-start | bytes 1978376 | tf_op jit(solution)/shard_map/ppermute | solution.py:201
  16.8 15.8 %collective-permute-start.26 = (f32[1288,128]{1,0:T(8,128)}, f32[1288,128]{1,0:T(8,128)S(1)}, u32[]{:S(2)}, u32[]{:S(2)}) collective-permute-start(f32[1288,128]{1,0:T(8,128)} %get-tuple-element.450), channel_id=1, source_target_pairs={{0,48},{16,0},{32,16},{48,32},{1,49},{17,1},{33,17},{49,33},{2,50}... | collective-permute-start | bytes 1978376 | tf_op jit(solution)/shard_map/ppermute | solution.py:205
  37.5 17.4 %collective-permute-start.28 = (f32[1288,128]{1,0:T(8,128)}, f32[1288,128]{1,0:T(8,128)}, u32[]{:S(2)}, u32[]{:S(2)}) collective-permute-start(f32[1288,128]{1,0:T(8,128)} %get-tuple-element.450), channel_id=1, source_target_pairs={{0,64},{64,0},{1,65},{65,1},{2,66},{66,2},{3,67},{67,3},{4,68},{68... | collective-permute-start | bytes 1978376 | tf_op jit(solution)/shard_map/ppermute | solution.py:197
  38.5 17.1 %collective-permute-start.29 = (f32[1288,128]{1,0:T(8,128)}, f32[1288,128]{1,0:T(8,128)S(1)}, u32[]{:S(2)}, u32[]{:S(2)}) collective-permute-start(f32[1288,128]{1,0:T(8,128)} %collective-permute-done.22), channel_id=1, source_target_pairs={{0,1},{1,2},{2,3},{3,0},{4,5},{5,6},{6,7},{7,4},{8,9},{9,10},{10,1... | collective-permute-start | bytes 1978376 | tf_op jit(solution)/shard_map/ppermute | solution.py:201
  39.9 16.7 %collective-permute-start.30 = (f32[1288,128]{1,0:T(8,128)}, f32[1288,128]{1,0:T(8,128)S(1)}, u32[]{:S(2)}, u32[]{:S(2)}) collective-permute-start(f32[1288,128]{1,0:T(8,128)} %collective-permute-done.22), channel_id=1, source_target_pairs={{0,3},{1,0},{2,1},{3,2},{4,7},{5,4},{6,5},{7,6},{8,11},{9,8},{10,9... | collective-permute-start | bytes 1978376 | tf_op jit(solution)/shard_map/ppermute | solution.py:205
  40.6 11.9 %collective-permute-start.31 = (f32[1288,128]{1,0:T(8,128)S(1)}, f32[1288,128]{1,0:T(8,128)S(1)}, u32[]{:S(2)}, u32[]{:S(2)}) collective-permute-start(f32[1288,128]{1,0:T(8,128)S(1)} %broadcast_select_fusion.7), channel_id=1, source_target_pairs={{0,16},{8,56},{16,32},{24,8},{32,48},{40,24},{48,0},{56,40},{1,17}... | collective-permute-start | bytes 1978376 | tf_op jit(solution)/shard_map/ppermute | solution.py:214
  42.2 14.4 %collective-permute-start.34 = (f32[1288,128]{1,0:T(8,128)S(1)}, f32[1288,128]{1,0:T(8,128)S(1)}, u32[]{:S(2)}, u32[]{:S(2)}) collective-permute-start(f32[1288,128]{1,0:T(8,128)S(1)} %collective-permute-done.26), channel_id=1, source_target_pairs={{0,8},{8,0},{1,9},{9,1},{2,10},{10,2},{3,11},{11,3},{4,12},{12,4},... | collective-permute-start | bytes 1978376 | tf_op jit(solution)/shard_map/ppermute | solution.py:197
  58.3 22.2 %collective-permute-start.37 = (f32[1288,128]{1,0:T(8,128)}, f32[1288,128]{1,0:T(8,128)}, u32[]{:S(2)}, u32[]{:S(2)}) collective-permute-start(f32[1288,128]{1,0:T(8,128)} %collective-permute-done.28), channel_id=1, source_target_pairs={{0,16},{16,32},{32,48},{48,0},{1,17},{17,33},{33,49},{49,1},{2,18}... | collective-permute-start | bytes 1978376 | tf_op jit(solution)/shard_map/ppermute | solution.py:201
  59.9 20.6 %collective-permute-start.38 = (f32[1288,128]{1,0:T(8,128)}, f32[1288,128]{1,0:T(8,128)}, u32[]{:S(2)}, u32[]{:S(2)}) collective-permute-start(f32[1288,128]{1,0:T(8,128)} %collective-permute-done.28), channel_id=1, source_target_pairs={{0,48},{16,0},{32,16},{48,32},{1,49},{17,1},{33,17},{49,33},{2,50}... | collective-permute-start | bytes 1978376 | tf_op jit(solution)/shard_map/ppermute | solution.py:205
  62.4 11.7 %collective-permute-start.40 = (f32[1288,128]{1,0:T(8,128)}, f32[1288,128]{1,0:T(8,128)}, u32[]{:S(2)}, u32[]{:S(2)}) collective-permute-start(f32[1288,128]{1,0:T(8,128)} %broadcast_select_fusion.5), channel_id=1, source_target_pairs={{0,1},{8,11},{1,2},{9,8},{2,3},{10,9},{3,0},{11,10},{4,5},{12,15},... | collective-permute-start | bytes 1978376 | tf_op jit(solution)/shard_map/ppermute | solution.py:214
  63.7 9.3 %collective-permute-start.41 = (f32[1288,128]{1,0:T(8,128)}, f32[1288,128]{1,0:T(8,128)}, u32[]{:S(2)}, u32[]{:S(2)}) collective-permute-start(f32[1288,128]{1,0:T(8,128)} %copy-done.6), channel_id=1, source_target_pairs={{0,8},{8,0},{1,9},{9,1},{2,10},{10,2},{3,11},{11,3},{4,12},{12,4},... | collective-permute-start | bytes 1978376 | tf_op jit(solution)/shard_map/ppermute | solution.py:197
  66.0 14.4 %collective-permute-start.39 = (f32[1288,128]{1,0:T(8,128)}, f32[1288,128]{1,0:T(8,128)}, u32[]{:S(2)}, u32[]{:S(2)}) collective-permute-start(f32[1288,128]{1,0:T(8,128)} %broadcast_select_fusion.6), channel_id=1, source_target_pairs={{0,1},{8,11},{1,2},{9,8},{2,3},{10,9},{3,0},{11,10},{4,5},{12,15},... | collective-permute-start | bytes 1978376 | tf_op jit(solution)/shard_map/ppermute | solution.py:214
  73.0 12.1 %collective-permute-start.36 = (f32[648,128]{1,0:T(8,128)S(1)}, f32[648,128]{1,0:T(8,128)S(1)}, u32[]{:S(2)}, u32[]{:S(2)}) collective-permute-start(f32[648,128]{1,0:T(8,128)S(1)} %concatenate.25), channel_id=1, source_target_pairs={{0,4},{4,0},{1,5},{5,1},{2,6},{6,2},{3,7},{7,3},{8,12},{12,8},{9,1... | collective-permute-start | bytes 995336 | tf_op jit(solution)/shard_map/ppermute | solution.py:197
  74.2 15.4 %collective-permute-start.42 = (f32[648,128]{1,0:T(8,128)S(1)}, f32[648,128]{1,0:T(8,128)S(1)}, u32[]{:S(2)}, u32[]{:S(2)}) collective-permute-start(f32[648,128]{1,0:T(8,128)S(1)} %concatenate.26), channel_id=1, source_target_pairs={{0,64},{64,0},{1,65},{65,1},{2,66},{66,2},{3,67},{67,3},{4,68},{68... | collective-permute-start | bytes 995336 | tf_op jit(solution)/shard_map/ppermute | solution.py:197
  90.8 15.9 %collective-permute-start.44 = (f32[1288,128]{1,0:T(8,128)S(1)}, f32[1288,128]{1,0:T(8,128)}, u32[]{:S(2)}, u32[]{:S(2)}) collective-permute-start(f32[1288,128]{1,0:T(8,128)S(1)} %broadcast_select_fusion.4), channel_id=1, source_target_pairs={{0,16},{8,56},{16,32},{24,8},{32,48},{40,24},{48,0},{56,40},{1,17}... | collective-permute-start | bytes 1978376 | tf_op jit(solution)/shard_map/ppermute | solution.py:214
  91.8 14.9 %collective-permute-start.46 = (f32[1288,128]{1,0:T(8,128)}, f32[1288,128]{1,0:T(8,128)S(1)}, u32[]{:S(2)}, u32[]{:S(2)}) collective-permute-start(f32[1288,128]{1,0:T(8,128)} %collective-permute-done.38), channel_id=1, source_target_pairs={{0,8},{8,0},{1,9},{9,1},{2,10},{10,2},{3,11},{11,3},{4,12},{12,4},... | collective-permute-start | bytes 1978376 | tf_op jit(solution)/shard_map/ppermute | solution.py:197
  92.8 13.9 %collective-permute-start.47 = (f32[648,128]{1,0:T(8,128)S(1)}, f32[648,128]{1,0:T(8,128)S(1)}, u32[]{:S(2)}, u32[]{:S(2)}) collective-permute-start(f32[648,128]{1,0:T(8,128)S(1)} %pad_add_fusion), channel_id=1, source_target_pairs={{0,16},{16,0},{32,48},{48,32},{1,17},{17,1},{33,49},{49,33},{2,18}... | collective-permute-start | bytes 995336 | tf_op jit(solution)/shard_map/ppermute | solution.py:222
  93.2 13.5 %collective-permute-start.43 = (f32[648,128]{1,0:T(8,128)S(1)}, f32[648,128]{1,0:T(8,128)S(1)}, u32[]{:S(2)}, u32[]{:S(2)}) collective-permute-start(f32[648,128]{1,0:T(8,128)S(1)} %pad_add_fusion.1), channel_id=1, source_target_pairs={{0,1},{1,0},{2,3},{3,2},{4,5},{5,4},{6,7},{7,6},{8,9},{9,8},{10,11... | collective-permute-start | bytes 995336 | tf_op jit(solution)/shard_map/ppermute | solution.py:222
  106.8 12.0 %collective-permute-start.49 = (f32[648,128]{1,0:T(8,128)S(1)}, f32[648,128]{1,0:T(8,128)S(1)}, u32[]{:S(2)}, u32[]{:S(2)}) collective-permute-start(f32[648,128]{1,0:T(8,128)S(1)} %add.377), channel_id=1, source_target_pairs={{0,32},{16,48},{32,0},{48,16},{1,33},{17,49},{33,1},{49,17},{2,34}... | collective-permute-start | bytes 995336 | tf_op jit(solution)/shard_map/ppermute | solution.py:222
  109.5 11.5 %collective-permute-start.48 = (f32[648,128]{1,0:T(8,128)S(1)}, f32[648,128]{1,0:T(8,128)S(1)}, u32[]{:S(2)}, u32[]{:S(2)}) collective-permute-start(f32[648,128]{1,0:T(8,128)S(1)} %add.374), channel_id=1, source_target_pairs={{0,2},{1,3},{2,0},{3,1},{4,6},{5,7},{6,4},{7,5},{8,10},{9,11},{10,... | collective-permute-start | bytes 995336 | tf_op jit(solution)/shard_map/ppermute | solution.py:222
  122.7 6.1 %collective-permute-start.50 = (f32[1288,128]{1,0:T(8,128)}, f32[1288,128]{1,0:T(8,128)}, u32[]{:S(2)}, u32[]{:S(2)}) collective-permute-start(f32[1288,128]{1,0:T(8,128)} %collective-permute-done.44), channel_id=1, source_target_pairs={{0,8},{8,0},{1,9},{9,1},{2,10},{10,2},{3,11},{11,3},{4,12},{12,4},... | collective-permute-start | bytes 1978376 | tf_op jit(solution)/shard_map/ppermute | solution.py:197
  (17 other events, 93.8 us)

commit v5 on v4

--- a/solution.py
+++ b/solution.py
@@ -2,7 +2,6 @@
 
 import jax
 import jax.numpy as jnp
-import numpy as np
 from jax import lax
 from jax.experimental import pallas as pl
 from jax.experimental.pallas import tpu as pltpu
@@ -18,31 +17,45 @@
 COL = ("zh", "x")
 
 
-def pack_kernel(am_ref, bm_ref, a_ref, b_ref, am_tile, bm_tile, pa_ref, pb_ref, qa_ref, qb_ref, sem_a, sem_b):
-    pa_ref[pl.ds(DATA, 8), :] = am_tile[...]
-    pb_ref[pl.ds(DATA, 8), :] = bm_tile[...]
+def pack_kernel(core_ref, am_ref, bm_ref, a_ref, b_ref, pa_ref, pb_ref, mine_ref, theirs_ref, sem_a, sem_b):
+    core = core_ref[0]
+    row = lax.broadcasted_iota(jnp.int32, (8, W), 0)
+    lane = lax.broadcasted_iota(jnp.int32, (8, W), 1)
 
     def copy(src, dst, sem, r, c, cols, at):
         return pltpu.make_async_copy(
             src.at[pl.ds(r * W, W), pl.ds(c * W, W)], dst.at[pl.ds(at, W), :], sem.at[r * cols + c]
         )
 
-    def move(mask, src, main, rest, sem):
+    def move(mask, src, main, base, sem, spot):
         rows, cols = mask.shape
         slot = jnp.int32(0)
+        tile = jnp.zeros((8, W), jnp.float32)
         for r in range(rows):
             for c in range(cols):
                 on = mask[r, c] != 0
-
-                @pl.when(on & (slot < SLOTS))
+                rest = slot - SLOTS
+                second = rest >= SLOTS // 2
+                inside = (rest >= 0) & (rest < SLOTS)
+                half = second.astype(jnp.int32)
+                at = base + (rest - half * (SLOTS // 2)) * W
+
+                @pl.when(on & (rest < 0))
                 def _():
                     copy(src, main, sem, r, c, cols, pl.multiple_of(slot * W, W)).start()
 
-                @pl.when(on & (slot >= SLOTS) & (slot < 2 * SLOTS))
+                @pl.when(on & inside & (half == core))
                 def _():
-                    copy(src, rest, sem, r, c, cols, pl.multiple_of((slot - SLOTS) * W, W)).start()
+                    copy(src, mine_ref, sem, r, c, cols, pl.multiple_of(at, W)).start()
+
+                @pl.when(on & inside & (half != core))
+                def _():
+                    copy(src, theirs_ref, sem, r, c, cols, pl.multiple_of(at, W)).start()
 
                 slot = slot + on.astype(jnp.int32)
+                tile = jnp.where(spot(r, c), jnp.where(on, slot, 0).astype(jnp.float32), tile)
+        main[pl.ds(DATA, 8), :] = tile
+        return slot > SLOTS
 
     def finish(mask, src, main, sem):
         rows, cols = mask.shape
@@ -53,26 +66,47 @@
                 def _():
                     copy(src, main, sem, r, c, cols, 0).wait()
 
-    move(am_ref, a_ref, pa_ref, qa_ref, sem_a)
-    move(bm_ref, b_ref, pb_ref, qb_ref, sem_b)
+    over_a = move(am_ref, a_ref, pa_ref, 0, sem_a, lambda r, c: (row == c) & (lane // 8 == r))
+    over_b = move(bm_ref, b_ref, pb_ref, HALF, sem_b, lambda r, c: (row == r) & (lane % 8 == c))
+    flags = jnp.where(row < 4, over_a.astype(jnp.float32), over_b.astype(jnp.float32))
+    mine_ref[pl.ds(DATA, 8), :] = flags
+    theirs_ref[pl.ds(DATA, 8), :] = flags
     finish(am_ref, a_ref, pa_ref, sem_a)
     finish(bm_ref, b_ref, pb_ref, sem_b)
 
 
-def pack(a_mask, b_mask, a_values, b_values, a_tile, b_tile):
+def pack(core, a_mask, b_mask, a_values, b_values):
     smem = pl.BlockSpec(memory_space=pltpu.SMEM)
     vmem = pl.BlockSpec(memory_space=pltpu.VMEM)
     hbm = pl.BlockSpec(memory_space=pl.ANY)
-    main = jax.ShapeDtypeStruct((ROWS, W), jnp.float32)
-    rest = jax.ShapeDtypeStruct((DATA, W), jnp.float32)
     return pl.pallas_call(
         pack_kernel,
-        out_shape=(main, main, rest, rest),
-        in_specs=[smem, smem, hbm, hbm, vmem, vmem],
+        out_shape=(jax.ShapeDtypeStruct((ROWS, W), jnp.float32),) * 4,
+        in_specs=[smem, smem, smem, hbm, hbm],
         out_specs=(vmem,) * 4,
         scratch_shapes=[pltpu.SemaphoreType.DMA((32,)), pltpu.SemaphoreType.DMA((32,))],
         name="pack",
-    )(a_mask, b_mask, a_values, b_values, a_tile, b_tile)
+    )(core.reshape(1).astype(jnp.int32), a_mask, b_mask, a_values, b_values)
+
+
+def merge_kernel(mine_ref, theirs_ref, a_ref, b_ref):
+    for n, out_ref in enumerate((a_ref, b_ref)):
+        own = mine_ref[pl.ds(DATA + 4 * n, 1), :]
+        also = theirs_ref[pl.ds(DATA + 4 * n, 1), :]
+        kept = jnp.where(also > 0, theirs_ref[pl.ds(n * HALF, HALF), :], 0.0)
+        out_ref[pl.ds(0, HALF), :] = jnp.where(own > 0, mine_ref[pl.ds(n * HALF, HALF), :], kept)
+        out_ref[pl.ds(HALF, 8), :] = jnp.broadcast_to(own + also, (8, W))
+
+
+def merge(mine, theirs):
+    vmem = pl.BlockSpec(memory_space=pltpu.VMEM)
+    return pl.pallas_call(
+        merge_kernel,
+        out_shape=(jax.ShapeDtypeStruct((HALF + 8, W), jnp.float32),) * 2,
+        in_specs=[vmem, vmem],
+        out_specs=(vmem, vmem),
+        name="merge",
+    )(mine, theirs)
 
 
 def split(x):
@@ -84,7 +118,7 @@
 def product_kernel(plan, spread, where_ref, keep_ref, *refs):
     count = len(plan)
     pieces = refs[:count]
-    out_ref, a_all, b_all, a_meta, b_meta, table, words, table_s, words_s, sem, sem_t = refs[count:]
+    out_ref, acc, a_all, b_all, a_meta, b_meta, table, words, table_s, words_s, list_s, sem, sem_t, sem_o = refs[count:]
     copies = []
     for n, (data, meta, first, rows) in enumerate(plan):
         at = where_ref[n]
@@ -96,6 +130,7 @@
     copies = [pltpu.make_async_copy(src, dst, sem.at[n]) for n, (src, dst) in enumerate(copies)]
     for copy in copies:
         copy.start()
+    acc[...] = jnp.zeros(acc.shape, jnp.float32)
     for copy in copies:
         copy.wait()
 
@@ -135,34 +170,55 @@
     t0.wait()
     t1.wait()
 
-    def block(p, _):
-        acc = jnp.zeros((W, W), jnp.float32)
+    def gather(p, total):
         for n in range(2):
-            bits = words_s[8 * n, p]
-
-            def step(_, state):
-                bits, acc = state
+
+            def one(m, bits):
                 lowest = bits & -bits
                 k = 31 - lax.clz(lowest) + 32 * n
-                entry = table_s[k, p]
-                a_at = pl.multiple_of((entry & 65535) * W, W)
-                b_at = pl.multiple_of(lax.shift_right_logical(entry, 16) * W, W)
-                a_high, a_low = split(a_all[pl.ds(a_at, W), :])
-                b_high, b_low = split(b_all[pl.ds(b_at, W), :])
-                left = jnp.concatenate([a_high, a_low], axis=1)
-                right = jnp.concatenate(
-                    [jnp.concatenate([b_high, b_low], axis=1), jnp.concatenate([b_low, b_high], axis=1)], axis=0
-                )
-                both = jnp.dot(left, right, preferred_element_type=jnp.float32)
-                return bits ^ lowest, acc + (both[:, :W] + both[:, W:])
-
-            bits, acc = lax.fori_loop(0, words_s[8 * n + 1, p], step, (bits, acc))
-        i = p // 8
-        j = p - i * 8
-        out_ref[pl.ds(pl.multiple_of(i * W, W), W), pl.ds(pl.multiple_of(j * W, W), W)] = acc
+                list_s[0, total + m] = table_s[k, p]
+                list_s[1, total + m] = p
+                return bits ^ lowest
+
+            found = words_s[8 * n + 1, p]
+            lax.fori_loop(0, found, one, words_s[8 * n, p])
+            total = total + found
+        return total
+
+    def term(entry):
+        a_at = pl.multiple_of((entry & 65535) * W, W)
+        b_at = pl.multiple_of(lax.shift_right_logical(entry, 16) * W, W)
+        a_high, a_low = split(a_all[pl.ds(a_at, W), :])
+        b_high, b_low = split(b_all[pl.ds(b_at, W), :])
+        left = jnp.concatenate([a_high, a_low], axis=1)
+        right = jnp.concatenate(
+            [jnp.concatenate([b_high, b_low], axis=1), jnp.concatenate([b_low, b_high], axis=1)], axis=0
+        )
+        both = jnp.dot(left, right, preferred_element_type=jnp.float32)
+        return both[:, :W] + both[:, W:]
+
+    def place(p):
+        return pl.ds(pl.multiple_of(p // 8 * W, W), W), pl.ds(pl.multiple_of(p % 8 * W, W), W)
+
+    total = lax.fori_loop(0, 32, gather, jnp.int32(0))
+
+    def four(t, _):
+        terms = [term(list_s[0, 4 * t + n]) for n in range(4)]
+        for n in range(4):
+            rows, cols = place(list_s[1, 4 * t + n])
+            acc[rows, cols] = acc[rows, cols] + terms[n]
         return 0
 
-    lax.fori_loop(0, 32, block, 0)
+    def single(t, _):
+        rows, cols = place(list_s[1, t])
+        acc[rows, cols] = acc[rows, cols] + term(list_s[0, t])
+        return 0
+
+    lax.fori_loop(0, total // 4, four, 0)
+    lax.fori_loop(total // 4 * 4, total, single, 0)
+    out = pltpu.make_async_copy(acc, out_ref, sem_o)
+    out.start()
+    out.wait()
 
 
 def product(spread, keep_tile, entries):
@@ -175,8 +231,9 @@
         functools.partial(product_kernel, plan, spread),
         out_shape=jax.ShapeDtypeStruct((512, 1024), jnp.float32),
         in_specs=[pl.BlockSpec(memory_space=pltpu.SMEM), pl.BlockSpec(memory_space=pltpu.VMEM)] + [hbm] * len(pieces),
-        out_specs=pl.BlockSpec(memory_space=pltpu.VMEM),
+        out_specs=hbm,
         scratch_shapes=[
+            pltpu.VMEM((512, 1024), jnp.float32),
             pltpu.VMEM(((8 + more[0]) * DATA, W), jnp.float32),
             pltpu.VMEM(((16 + more[1]) * DATA, W), jnp.float32),
             pltpu.VMEM((64, W), jnp.float32),
@@ -185,8 +242,10 @@
             pltpu.VMEM((16, W), jnp.int32),
             pltpu.SMEM((64, W), jnp.int32),
             pltpu.SMEM((16, W), jnp.int32),
+            pltpu.SMEM((2, 2048), jnp.int32),
             pltpu.SemaphoreType.DMA((2 * len(pieces),)),
             pltpu.SemaphoreType.DMA((2,)),
+            pltpu.SemaphoreType.DMA,
         ],
         compiler_params=pltpu.CompilerParams(vmem_limit_bytes=48 * 1024 * 1024),
         name="product",
@@ -231,68 +290,42 @@
     return found
 
 
-def slots_of(mask):
-    flat = (mask.reshape(-1) != 0).astype(jnp.float32)
-    n = flat.shape[0]
-    upto = jnp.asarray(np.tril(np.ones((n, n), np.float32)))
-    rank = jnp.sum(upto * flat[None, :], axis=1)
-    return (flat * rank).reshape(mask.shape)
-
-
 def per_device(a_values, a_mask, b_values, b_mask, keep):
-    a_slot = slots_of(a_mask)
-    b_slot = slots_of(b_mask)
-    a_tile = jnp.pad(jnp.repeat(a_slot.T, 8, axis=1), ((0, 0), (0, W - 32)))
-    b_tile = jnp.pad(jnp.tile(b_slot, (1, 4)), ((0, 4), (0, W - 32)))
-    keep_tile = jnp.pad(jnp.transpose(keep, (1, 0, 2)).reshape(64, 32), ((0, 0), (0, W - 32)))
-    a, b, a_rest, b_rest = pack(a_mask, b_mask, a_values, b_values, a_tile, b_tile)
     zl, y, core = (lax.axis_index(n) for n in ROW)
     zh, x = (lax.axis_index(n) for n in COL)
-
-    az, ar, al, br, bl = swap(a, "zh"), right(a, "x"), left(a, "x"), right(b, "y"), left(b, "y")
-
-    over = [(jnp.sum((m != 0).astype(jnp.int32)) > SLOTS).astype(jnp.float32) for m in (a_mask, b_mask)]
-    flags = jnp.concatenate([jnp.full((4, W), n) for n in over])
-    mine = [lax.dynamic_slice_in_dim(q, core * HALF, HALF) for q in (a_rest, b_rest)]
-    theirs = [lax.dynamic_slice_in_dim(q, (1 - core) * HALF, HALF) for q in (a_rest, b_rest)]
-
-    g = gate(az, ar, al, br, bl)
-    bz, azr, azl = swap(g(b), "zl"), right(g(az), "x"), left(g(az), "x")
-    bo = opposite(g(br), g(bl), core, "y")
-    ec = swap(g(jnp.concatenate([*theirs, flags])), "core")
-    cb = swap(gate(ec)(g(b)), "core")
-    cr = swap(gate(cb)(g(br)), "core")
-    cl = swap(gate(cr)(g(bl)), "core")
-
-    excess = []
-    for n in range(2):
-        also = ec[2 * HALF + 4 * n, 0]
-        piece = jnp.where(over[n] > 0, mine[n], jnp.where(also > 0, ec[n * HALF : (n + 1) * HALF], 0.0))
-        excess.append(jnp.concatenate([piece, jnp.full((8, W), over[n] + also)]))
-    ea, eb = excess
-
-    g = gate(bz, azr, azl, bo, cl)
-    bzr, bzl = right(g(bz), "y"), left(g(bz), "y")
-    ao, azo = opposite(g(ar), g(al), core, "x"), opposite(g(azr), g(azl), core, "x")
-    cz = swap(g(bz), "core")
-    co = swap(gate(cz)(g(bo)), "core")
-    eaz = swap(gate(cz)(g(ea)), "zh")
-    ebz = swap(gate(co)(g(eb)), "zl")
+    keep_tile = jnp.pad(jnp.transpose(keep, (1, 0, 2)).reshape(64, 32), ((0, 0), (0, W - 32)))
+    a, b, mine, theirs = pack(core, a_mask, b_mask, a_values, b_values)
+
+    ar, al, br, bl = right(a, "x"), left(a, "x"), right(b, "y"), left(b, "y")
+    az = swap(a, "zh")
+    ea, eb = merge(mine, swap(theirs, "core"))
+    eaz, ebz = swap(ea, "zh"), swap(eb, "zl")
+
+    ga, gb = gate(az, ar, al, eaz), gate(az, br, bl, ebz)
+    azr, azl = right(ga(az), "x"), left(ga(az), "x")
+    bz = swap(gb(b), "zl")
+    bo = opposite(gb(br), gb(bl), core, "y")
     ea, eb = ea + eaz, eb + ebz
-
-    g = gate(bzr, bzl, ao, azo, co, eaz, ebz)
-    bzo = opposite(g(bzr), g(bzl), core, "y")
-    czr = swap(g(bzr), "core")
-    czl = swap(gate(czr)(g(bzl)), "core")
-    eax, ebx = pair(g(ea), "x", 1), pair(g(eb), "y", 1)
+    eax, ebx = pair(ga(ea), "x", 1), pair(gb(eb), "y", 1)
+    cb = swap(gb(b), "core")
+    cr = swap(gate(cb)(gb(br)), "core")
+    cl = swap(gate(cr)(gb(bl)), "core")
+
+    ga, gb = gate(azr, azl, eax), gate(bz, bo, cl, ebx)
+    bzr, bzl = right(gb(bz), "y"), left(gb(bz), "y")
+    ao, azo = opposite(ga(ar), ga(al), core, "x"), opposite(ga(azr), ga(azl), core, "x")
     ea, eb = ea + eax, eb + ebx
-
-    g = gate(bzo, czl, eax, ebx)
-    czo = swap(g(bzo), "core")
-    eax, ebx = pair(g(ea), "x", 2), pair(g(eb), "y", 2)
+    eax, ebx = pair(ga(ea), "x", 2), pair(gb(eb), "y", 2)
+    cz = swap(gb(bz), "core")
+    co = swap(gate(cz)(gb(bo)), "core")
+
     ea, eb = ea + eax, eb + ebx
-    last = swap(jnp.concatenate([ea[:HALF], eb[:HALF]]), "core")
-    fa, fb = last[:HALF], last[HALF:]
+    gb = gate(bzr, bzl, co, ao, azo, eax, ebx)
+    bzo = opposite(gb(bzr), gb(bzl), core, "y")
+    czr = swap(gb(bzr), "core")
+    fa, fb = swap(gb(ea), "core"), swap(gate(czr)(gb(eb)), "core")
+    czl = swap(gate(fb)(gb(bzl)), "core")
+    czo = swap(bzo, "core")
 
     entries = []
     for z, group in ((0, (a, ar, al, ao)), (1, (az, azr, azl, azo))):
@@ -318,16 +351,20 @@
 
     def many(_):
         def whole(e, f):
-            e = e[:HALF]
+            e, f = e[:HALF], f[:HALF]
             return jnp.where(core == 0, jnp.concatenate([e, f]), jnp.concatenate([f, e]))
 
         def all_a(_):
-            near, far = around(a_rest, "zh", "x", core)
+            near, far = around(rest(0), "zh", "x", core)
             return near + far
 
         def all_b(_):
-            near, far = around(b_rest, "zl", "y", core)
+            near, far = around(rest(1), "zl", "y", core)
             return near + far + tuple(swap(p, "core") for p in near + far)
+
+        def rest(n):
+            parts = [q[n * HALF : (n + 1) * HALF] for q in (mine, theirs)]
+            return jnp.where(core == 0, jnp.concatenate(parts), jnp.concatenate(parts[::-1]))
 
         rest_a = lax.cond(crowded[0], all_a, lambda _: (whole(ea, fa),) * 8, 0)
         rest_b = lax.cond(crowded[1], all_b, lambda _: (whole(eb, fb),) * 16, 0)

time: 159 us -> 152 us (0.956)
  the two profiles are of different devices: /device:TPU:2 before, /device:TPU:1 now
where the time goes in v5:
time: 152 us; the launch traced here: 149 us
  waiting for transfers between devices  75.2 us (49%)
  starting transfers between devices  45.3 us (30%)
  Pallas kernels  17.4 us (11%)
  local copies, waits for them, and re-layouts  5.9 us (4%)
  other arithmetic  3.49 us (2%)
  between operations  1.57 us (1%)
    ppermute x4, waiting for transfers between devices, pair(): return lax.ppermute(x, axis, [(n, n ^ distance) for n in range(4)])  36 us
    ppermute x15, starting transfers between devices, swap(): return lax.ppermute(x, axis, [(0, 1), (1, 0)])  20.1 us
    ppermute x4, waiting for transfers between devices, right(): return lax.ppermute(x, axis, [(n, (n + 1) % 4) for n in range(4)])  15.8 us
    ppermute x15, waiting for transfers between devices, swap(): return lax.ppermute(x, axis, [(0, 1), (1, 0)])  14.7 us
    pallas_call x1, Pallas kernels, product(): pl.pallas_call(functools.partial(product_kernel, plan, spread), out_shape...  11.5 us
    ppermute x4, waiting for transfers between devices, opposite(): lax.ppermute(jnp.where(core == 0, from_left, from_right), axes, pairs)  8.65 us
    ppermute x4, starting transfers between devices, opposite(): lax.ppermute(jnp.where(core == 0, from_left, from_right), axes, pairs)  8.44 us
    ppermute x4, starting transfers between devices, left(): return lax.ppermute(x, axis, [(n, (n - 1) % 4) for n in range(4)])  6.28 us
  transfers between devices with their start and end apart: 31, of which 10 were waited for; matrix products, arithmetic and copies ran while one was open for 4% of the time, Pallas kernels for 1%

profile of v5, /device:TPU:1, one launch (start us, length us, event | category | flops | bytes accessed | tf_op | source)
XLA Modules:
  0.0 149.0 jit_solution(14532175154570749944)
XLA Ops:
  0.0 3.8 %pack.1 = (f32[1288,128]{1,0:T(8,128)S(1)}, f32[1288,128]{1,0:T(8,128)}, f32[1288,128]{1,0:T(8,128)S(1)}, f32[1288,128]{1,0:T(8,128)}) custom-call(s32[1]{0:T(128)} %bitcast.74.core_ref, s32[4,8]{1,0:T(4,128)} %am_ref.1, s32[4,8]{1,0:T(4,128)} %bm_ref.1, f32[512,1024]{1,0:T(8,128)} %a_ref.1, f32[512,1024]{1,0:T(8,128)} %b_ref.1), custom_call_target="tpu_custom_call" | custom-call | tf_op jit(solution)/shard_map/pack/pallas_call | solution.py:82
  3.8 1.5 %collective-permute-start.22 = (f32[1288,128]{1,0:T(8,128)}, f32[1288,128]{1,0:T(8,128)}, u32[]{:S(2)}, u32[]{:S(2)}) collective-permute-start(f32[1288,128]{1,0:T(8,128)} %get-tuple-element.446), channel_id=1, source_target_pairs={{0,8},{8,0},{1,9},{9,1},{2,10},{10,2},{3,11},{11,3},{4,12},{12,4},... | collective-permute-start | bytes 1978376 | tf_op jit(solution)/shard_map/ppermute | solution.py:256
  5.4 3.7 %collective-permute-start.24 = (f32[1288,128]{1,0:T(8,128)S(1)}, f32[1288,128]{1,0:T(8,128)S(1)}, u32[]{:S(2)}, u32[]{:S(2)}) collective-permute-start(f32[1288,128]{1,0:T(8,128)S(1)} %get-tuple-element.448), channel_id=1, source_target_pairs={{0,4},{4,0},{1,5},{5,1},{2,6},{6,2},{3,7},{7,3},{8,12},{12,8},{9,1... | collective-permute-start | bytes 1978376 | tf_op jit(solution)/shard_map/ppermute | solution.py:256
  11.8 2.0 %merge.1 = (f32[648,128]{1,0:T(8,128)}, f32[648,128]{1,0:T(8,128)}) custom-call(f32[1288,128]{1,0:T(8,128)S(1)} %get-tuple-element.445.mine_ref, f32[1288,128]{1,0:T(8,128)} %collective-permute-done.22.theirs_ref), custom_call_target="tpu_custom_call" | custom-call | tf_op jit(solution)/shard_map/merge/pallas_call | solution.py:103
  14.6 9.6 %collective-permute-done.24 = f32[1288,128]{1,0:T(8,128)S(1)} collective-permute-done((f32[1288,128]{1,0:T(8,128)S(1)}, f32[1288,128]{1,0:T(8,128)S(1)}, u32[]{:S(2)}, u32[]{:S(2)}) %collective-permute-start.24) | collective-permute-done | bytes 659488 | tf_op jit(solution)/shard_map/ppermute | solution.py:256
  24.2 2.5 %collective-permute-done.32 = f32[1288,128]{1,0:T(8,128)S(1)} collective-permute-done((f32[1288,128]{1,0:T(8,128)}, f32[1288,128]{1,0:T(8,128)S(1)}, u32[]{:S(2)}, u32[]{:S(2)}) %collective-permute-start.32) | collective-permute-done | bytes 659488 | tf_op jit(solution)/shard_map/ppermute | solution.py:260
  26.7 5.1 %collective-permute-done.31 = f32[648,128]{1,0:T(8,128)S(1)} collective-permute-done((f32[648,128]{1,0:T(8,128)}, f32[648,128]{1,0:T(8,128)S(1)}, u32[]{:S(2)}, u32[]{:S(2)}) %collective-permute-start.31) | collective-permute-done | bytes 331808 | tf_op jit(solution)/shard_map/ppermute | solution.py:256
  33.8 1.5 %collective-permute-start.26 = (f32[1288,128]{1,0:T(8,128)S(1)}, f32[1288,128]{1,0:T(8,128)S(1)}, u32[]{:S(2)}, u32[]{:S(2)}) collective-permute-start(f32[1288,128]{1,0:T(8,128)S(1)} %get-tuple-element.448), channel_id=1, source_target_pairs={{0,3},{1,0},{2,1},{3,2},{4,7},{5,4},{6,5},{7,6},{8,11},{9,8},{10,9... | collective-permute-start | bytes 1978376 | tf_op jit(solution)/shard_map/ppermute | solution.py:264
  37.0 13.3 %collective-permute-done.25 = f32[1288,128]{1,0:T(8,128)S(1)} collective-permute-done((f32[1288,128]{1,0:T(8,128)S(1)}, f32[1288,128]{1,0:T(8,128)S(1)}, u32[]{:S(2)}, u32[]{:S(2)}) %collective-permute-start.25) | collective-permute-done | bytes 659488 | tf_op jit(solution)/shard_map/ppermute | solution.py:260
  51.2 1.8 %collective-permute-start.29 = (f32[1288,128]{1,0:T(8,128)}, f32[1288,128]{1,0:T(8,128)S(1)}, u32[]{:S(2)}, u32[]{:S(2)}) collective-permute-start(f32[1288,128]{1,0:T(8,128)} %copy-done.4), channel_id=1, source_target_pairs={{0,3},{1,0},{2,1},{3,2},{4,7},{5,4},{6,5},{7,6},{8,11},{9,8},{10,9... | collective-permute-start | bytes 1978376 | tf_op jit(solution)/shard_map/ppermute | solution.py:264
  54.3 2.9 %collective-permute-start.36 = (f32[1288,128]{1,0:T(8,128)S(1)}, f32[1288,128]{1,0:T(8,128)S(1)}, u32[]{:S(2)}, u32[]{:S(2)}) collective-permute-start(f32[1288,128]{1,0:T(8,128)S(1)} %broadcast_select_fusion.7), channel_id=1, source_target_pairs={{0,16},{8,56},{16,32},{24,8},{32,48},{40,24},{48,0},{56,40},{1,17}... | collective-permute-start | bytes 1978376 | tf_op jit(solution)/shard_map/ppermute | solution.py:273
  57.2 16.2 %collective-permute-done.27 = f32[648,128]{1,0:T(8,128)S(1)} collective-permute-done((f32[648,128]{1,0:T(8,128)S(1)}, f32[648,128]{1,0:T(8,128)S(1)}, u32[]{:S(2)}, u32[]{:S(2)}) %collective-permute-start.27) | collective-permute-done | bytes 331808 | tf_op jit(solution)/shard_map/ppermute | solution.py:281
  73.4 2.4 %collective-permute-start.39 = (f32[1288,128]{1,0:T(8,128)S(1)}, f32[1288,128]{1,0:T(8,128)S(1)}, u32[]{:S(2)}, u32[]{:S(2)}) collective-permute-start(f32[1288,128]{1,0:T(8,128)S(1)} %collective-permute-done.33), channel_id=1, source_target_pairs={{0,8},{8,0},{1,9},{9,1},{2,10},{10,2},{3,11},{11,3},{4,12},{12,4},... | collective-permute-start | bytes 1978376 | tf_op jit(solution)/shard_map/ppermute | solution.py:256
  77.3 8.0 %collective-permute-done.34 = f32[648,128]{1,0:T(8,128)S(1)} collective-permute-done((f32[648,128]{1,0:T(8,128)S(1)}, f32[648,128]{1,0:T(8,128)S(1)}, u32[]{:S(2)}, u32[]{:S(2)}) %collective-permute-start.34) | collective-permute-done | bytes 331808 | tf_op jit(solution)/shard_map/ppermute | solution.py:281
  86.3 1.5 %collective-permute-start.42 = (f32[1288,128]{1,0:T(8,128)S(1)}, f32[1288,128]{1,0:T(8,128)S(1)}, u32[]{:S(2)}, u32[]{:S(2)}) collective-permute-start(f32[1288,128]{1,0:T(8,128)S(1)} %broadcast_select_fusion.5), channel_id=1, source_target_pairs={{0,1},{8,11},{1,2},{9,8},{2,3},{10,9},{3,0},{11,10},{4,5},{12,15},... | collective-permute-start | bytes 1978376 | tf_op jit(solution)/shard_map/ppermute | solution.py:273
  93.2 5.7 %collective-permute-done.30 = f32[648,128]{1,0:T(8,128)S(1)} collective-permute-done((f32[648,128]{1,0:T(8,128)S(1)}, f32[648,128]{1,0:T(8,128)S(1)}, u32[]{:S(2)}, u32[]{:S(2)}) %collective-permute-start.30) | collective-permute-done | bytes 331808 | tf_op jit(solution)/shard_map/ppermute | solution.py:281
  98.9 6.5 %collective-permute-start.44 = (f32[1288,128]{1,0:T(8,128)S(1)}, f32[1288,128]{1,0:T(8,128)S(1)}, u32[]{:S(2)}, u32[]{:S(2)}) collective-permute-start(f32[1288,128]{1,0:T(8,128)S(1)} %collective-permute-done.36), channel_id=1, source_target_pairs={{0,8},{8,0},{1,9},{9,1},{2,10},{10,2},{3,11},{11,3},{4,12},{12,4},... | collective-permute-start | bytes 1978376 | tf_op jit(solution)/shard_map/ppermute | solution.py:256
  105.5 3.0 %collective-permute-start.40 = (f32[648,128]{1,0:T(8,128)S(1)}, f32[648,128]{1,0:T(8,128)S(1)}, u32[]{:S(2)}, u32[]{:S(2)}) collective-permute-start(f32[648,128]{1,0:T(8,128)S(1)} %add.351), channel_id=1, source_target_pairs={{0,32},{16,48},{32,0},{48,16},{1,33},{17,49},{33,1},{49,17},{2,34}... | collective-permute-start | bytes 995336 | tf_op jit(solution)/shard_map/ppermute | solution.py:281
  108.5 1.8 %collective-permute-done.41 = f32[1288,128]{1,0:T(8,128)S(1)} collective-permute-done((f32[1288,128]{1,0:T(8,128)S(1)}, f32[1288,128]{1,0:T(8,128)S(1)}, u32[]{:S(2)}, u32[]{:S(2)}) %collective-permute-start.41) | collective-permute-done | bytes 659488 | tf_op jit(solution)/shard_map/ppermute | solution.py:273
  110.4 6.1 %collective-permute-done.40 = f32[648,128]{1,0:T(8,128)S(1)} collective-permute-done((f32[648,128]{1,0:T(8,128)S(1)}, f32[648,128]{1,0:T(8,128)S(1)}, u32[]{:S(2)}, u32[]{:S(2)}) %collective-permute-start.40) | collective-permute-done | bytes 331808 | tf_op jit(solution)/shard_map/ppermute | solution.py:281
  119.7 2.9 %collective-permute-start.50 = (f32[1288,128]{1,0:T(8,128)S(1)}, f32[1288,128]{1,0:T(8,128)}, u32[]{:S(2)}, u32[]{:S(2)}) collective-permute-start(f32[1288,128]{1,0:T(8,128)S(1)} %broadcast_select_fusion.4), channel_id=1, source_target_pairs={{0,16},{8,56},{16,32},{24,8},{32,48},{40,24},{48,0},{56,40},{1,17}... | collective-permute-start | bytes 1978376 | tf_op jit(solution)/shard_map/ppermute | solution.py:273
  123.3 6.8 %collective-permute-done.50 = f32[1288,128]{1,0:T(8,128)} collective-permute-done((f32[1288,128]{1,0:T(8,128)S(1)}, f32[1288,128]{1,0:T(8,128)}, u32[]{:S(2)}, u32[]{:S(2)}) %collective-permute-start.50) | collective-permute-done | bytes 659488 | tf_op jit(solution)/shard_map/ppermute | solution.py:273
  135.8 11.9 %conditional.3 = (f32[512,1024]{1,0:T(8,128)S(1)}) conditional(s32[]{:T(128)} %convert_element_type.9, (s32[]{:T(128)}, s32[]{:T(128)}, s32[]{:T(128)}, s32[]{:T(128)}, s32[]{:T(128)}, /*index=5*/s32[]{:T(128)}, s32[]{:T(128)}, s32[]{:T(128)}, s32[]{:T(128)}, s32[]{:T(128)}, /*index=10*/s32[]{:T(128)}, s32[]{:T(128)}, s32[]{:T(128)}, s32[]{:T(128)}, ...), branch_computations={%region_0.1_spmd, %region_1.6_spmd} | conditional | flops 1638541 | bytes 70847448 | solution.py:379
  136.0 11.5 %product.2 = f32[512,1024]{1,0:T(8,128)S(1)} custom-call(s32[28]{0:T(128)S(1)} %stack.180.where_ref, s32[64,128]{1,0:T(8,128)S(1)} %copy.9.keep_ref, f32[1288,128]{1,0:T(8,128)} %get-tuple-element.290.refs_0_, f32[1288,128]{1,0:T(8,128)S(1)} %get-tuple-element.291.refs_1_, f32[1288,128]{1,0:T(8,128)S(1)} %get-tuple-element.292.refs_2_, ...), custom_call_target="tpu_custom_call" | custom-call | tf_op jit(solution)/shard_map/cond/branch_0_fun/product/pallas_call | solution.py:230
  (97 shorter events, 27.0 us)
Async XLA Ops:
  3.8 8.0 %collective-permute-start.22 = (f32[1288,128]{1,0:T(8,128)}, f32[1288,128]{1,0:T(8,128)}, u32[]{:S(2)}, u32[]{:S(2)}) collective-permute-start(f32[1288,128]{1,0:T(8,128)} %get-tuple-element.446), channel_id=1, source_target_pairs={{0,8},{8,0},{1,9},{9,1},{2,10},{10,2},{3,11},{11,3},{4,12},{12,4},... | collective-permute-start | bytes 1978376 | tf_op jit(solution)/shard_map/ppermute | solution.py:256
  5.4 18.8 %collective-permute-start.24 = (f32[1288,128]{1,0:T(8,128)S(1)}, f32[1288,128]{1,0:T(8,128)S(1)}, u32[]{:S(2)}, u32[]{:S(2)}) collective-permute-start(f32[1288,128]{1,0:T(8,128)S(1)} %get-tuple-element.448), channel_id=1, source_target_pairs={{0,4},{4,0},{1,5},{5,1},{2,6},{6,2},{3,7},{7,3},{8,12},{12,8},{9,1... | collective-permute-start | bytes 1978376 | tf_op jit(solution)/shard_map/ppermute | solution.py:256
  9.1 17.6 %collective-permute-start.32 = (f32[1288,128]{1,0:T(8,128)}, f32[1288,128]{1,0:T(8,128)S(1)}, u32[]{:S(2)}, u32[]{:S(2)}) collective-permute-start(f32[1288,128]{1,0:T(8,128)} %get-tuple-element.455), channel_id=1, source_target_pairs={{0,16},{16,32},{32,48},{48,0},{1,17},{17,33},{33,49},{49,1},{2,18}... | collective-permute-start | bytes 1978376 | tf_op jit(solution)/shard_map/ppermute | solution.py:260
  10.4 16.3 %collective-permute-start.33 = (f32[1288,128]{1,0:T(8,128)}, f32[1288,128]{1,0:T(8,128)S(1)}, u32[]{:S(2)}, u32[]{:S(2)}) collective-permute-start(f32[1288,128]{1,0:T(8,128)} %get-tuple-element.455), channel_id=1, source_target_pairs={{0,48},{16,0},{32,16},{48,32},{1,49},{17,1},{33,17},{49,33},{2,50}... | collective-permute-start | bytes 1978376 | tf_op jit(solution)/shard_map/ppermute | solution.py:264
  13.9 17.9 %collective-permute-start.31 = (f32[648,128]{1,0:T(8,128)}, f32[648,128]{1,0:T(8,128)S(1)}, u32[]{:S(2)}, u32[]{:S(2)}) collective-permute-start(f32[648,128]{1,0:T(8,128)} %get-tuple-element.452), channel_id=1, source_target_pairs={{0,64},{64,0},{1,65},{65,1},{2,66},{66,2},{3,67},{67,3},{4,68},{68... | collective-permute-start | bytes 995336 | tf_op jit(solution)/shard_map/ppermute | solution.py:256
  32.7 17.6 %collective-permute-start.25 = (f32[1288,128]{1,0:T(8,128)S(1)}, f32[1288,128]{1,0:T(8,128)S(1)}, u32[]{:S(2)}, u32[]{:S(2)}) collective-permute-start(f32[1288,128]{1,0:T(8,128)S(1)} %get-tuple-element.448), channel_id=1, source_target_pairs={{0,1},{1,2},{2,3},{3,0},{4,5},{5,6},{6,7},{7,4},{8,9},{9,10},{10,1... | collective-permute-start | bytes 1978376 | tf_op jit(solution)/shard_map/ppermute | solution.py:260
  33.8 16.4 %collective-permute-start.26 = (f32[1288,128]{1,0:T(8,128)S(1)}, f32[1288,128]{1,0:T(8,128)S(1)}, u32[]{:S(2)}, u32[]{:S(2)}) collective-permute-start(f32[1288,128]{1,0:T(8,128)S(1)} %get-tuple-element.448), channel_id=1, source_target_pairs={{0,3},{1,0},{2,1},{3,2},{4,7},{5,4},{6,5},{7,6},{8,11},{9,8},{10,9... | collective-permute-start | bytes 1978376 | tf_op jit(solution)/shard_map/ppermute | solution.py:264
  35.4 14.9 %collective-permute-start.23 = (f32[648,128]{1,0:T(8,128)}, f32[648,128]{1,0:T(8,128)}, u32[]{:S(2)}, u32[]{:S(2)}) collective-permute-start(f32[648,128]{1,0:T(8,128)} %get-tuple-element.447), channel_id=1, source_target_pairs={{0,4},{4,0},{1,5},{5,1},{2,6},{6,2},{3,7},{7,3},{8,12},{12,8},{9,1... | collective-permute-start | bytes 995336 | tf_op jit(solution)/shard_map/ppermute | solution.py:256
  36.1 18.2 %collective-permute-start.38 = (f32[1288,128]{1,0:T(8,128)S(1)}, f32[1288,128]{1,0:T(8,128)}, u32[]{:S(2)}, u32[]{:S(2)}) collective-permute-start(f32[1288,128]{1,0:T(8,128)S(1)} %collective-permute-done.32), channel_id=1, source_target_pairs={{0,8},{8,0},{1,9},{9,1},{2,10},{10,2},{3,11},{11,3},{4,12},{12,4},... | collective-permute-start | bytes 1978376 | tf_op jit(solution)/shard_map/ppermute | solution.py:256
  37.0 48.3 %collective-permute-start.35 = (f32[1288,128]{1,0:T(8,128)}, f32[1288,128]{1,0:T(8,128)S(1)}, u32[]{:S(2)}, u32[]{:S(2)}) collective-permute-start(f32[1288,128]{1,0:T(8,128)} %get-tuple-element.455), channel_id=1, source_target_pairs={{0,64},{64,0},{1,65},{65,1},{2,66},{66,2},{3,67},{67,3},{4,68},{68... | collective-permute-start | bytes 1978376 | tf_op jit(solution)/shard_map/ppermute | solution.py:256
  50.3 25.5 %collective-permute-start.28 = (f32[1288,128]{1,0:T(8,128)}, f32[1288,128]{1,0:T(8,128)S(1)}, u32[]{:S(2)}, u32[]{:S(2)}) collective-permute-start(f32[1288,128]{1,0:T(8,128)} %copy-done.4), channel_id=1, source_target_pairs={{0,1},{1,2},{2,3},{3,0},{4,5},{5,6},{6,7},{7,4},{8,9},{9,10},{10,1... | collective-permute-start | bytes 1978376 | tf_op jit(solution)/shard_map/ppermute | solution.py:260
  51.2 26.1 %collective-permute-start.29 = (f32[1288,128]{1,0:T(8,128)}, f32[1288,128]{1,0:T(8,128)S(1)}, u32[]{:S(2)}, u32[]{:S(2)}) collective-permute-start(f32[1288,128]{1,0:T(8,128)} %copy-done.4), channel_id=1, source_target_pairs={{0,3},{1,0},{2,1},{3,2},{4,7},{5,4},{6,5},{7,6},{8,11},{9,8},{10,9... | collective-permute-start | bytes 1978376 | tf_op jit(solution)/shard_map/ppermute | solution.py:264
  54.1 19.2 %collective-permute-start.27 = (f32[648,128]{1,0:T(8,128)S(1)}, f32[648,128]{1,0:T(8,128)S(1)}, u32[]{:S(2)}, u32[]{:S(2)}) collective-permute-start(f32[648,128]{1,0:T(8,128)S(1)} %add.347), channel_id=1, source_target_pairs={{0,1},{1,0},{2,3},{3,2},{4,5},{5,4},{6,7},{7,6},{8,9},{9,8},{10,11... | collective-permute-start | bytes 995336 | tf_op jit(solution)/shard_map/ppermute | solution.py:281
  54.3 31.0 %collective-permute-start.36 = (f32[1288,128]{1,0:T(8,128)S(1)}, f32[1288,128]{1,0:T(8,128)S(1)}, u32[]{:S(2)}, u32[]{:S(2)}) collective-permute-start(f32[1288,128]{1,0:T(8,128)S(1)} %broadcast_select_fusion.7), channel_id=1, source_target_pairs={{0,16},{8,56},{16,32},{24,8},{32,48},{40,24},{48,0},{56,40},{1,17}... | collective-permute-start | bytes 1978376 | tf_op jit(solution)/shard_map/ppermute | solution.py:273
  73.4 12.0 %collective-permute-start.39 = (f32[1288,128]{1,0:T(8,128)S(1)}, f32[1288,128]{1,0:T(8,128)S(1)}, u32[]{:S(2)}, u32[]{:S(2)}) collective-permute-start(f32[1288,128]{1,0:T(8,128)S(1)} %collective-permute-done.33), channel_id=1, source_target_pairs={{0,8},{8,0},{1,9},{9,1},{2,10},{10,2},{3,11},{11,3},{4,12},{12,4},... | collective-permute-start | bytes 1978376 | tf_op jit(solution)/shard_map/ppermute | solution.py:256
  75.8 9.5 %collective-permute-start.34 = (f32[648,128]{1,0:T(8,128)S(1)}, f32[648,128]{1,0:T(8,128)S(1)}, u32[]{:S(2)}, u32[]{:S(2)}) collective-permute-start(f32[648,128]{1,0:T(8,128)S(1)} %add.350), channel_id=1, source_target_pairs={{0,16},{16,0},{32,48},{48,32},{1,17},{17,1},{33,49},{49,33},{2,18}... | collective-permute-start | bytes 995336 | tf_op jit(solution)/shard_map/ppermute | solution.py:281
  86.3 19.2 %collective-permute-start.42 = (f32[1288,128]{1,0:T(8,128)S(1)}, f32[1288,128]{1,0:T(8,128)S(1)}, u32[]{:S(2)}, u32[]{:S(2)}) collective-permute-start(f32[1288,128]{1,0:T(8,128)S(1)} %broadcast_select_fusion.5), channel_id=1, source_target_pairs={{0,1},{8,11},{1,2},{9,8},{2,3},{10,9},{3,0},{11,10},{4,5},{12,15},... | collective-permute-start | bytes 1978376 | tf_op jit(solution)/shard_map/ppermute | solution.py:273
  87.8 11.1 %collective-permute-start.30 = (f32[648,128]{1,0:T(8,128)S(1)}, f32[648,128]{1,0:T(8,128)S(1)}, u32[]{:S(2)}, u32[]{:S(2)}) collective-permute-start(f32[648,128]{1,0:T(8,128)S(1)} %add.348), channel_id=1, source_target_pairs={{0,2},{1,3},{2,0},{3,1},{4,6},{5,7},{6,4},{7,5},{8,10},{9,11},{10,... | collective-permute-start | bytes 995336 | tf_op jit(solution)/shard_map/ppermute | solution.py:281
  89.2 21.2 %collective-permute-start.41 = (f32[1288,128]{1,0:T(8,128)S(1)}, f32[1288,128]{1,0:T(8,128)S(1)}, u32[]{:S(2)}, u32[]{:S(2)}) collective-permute-start(f32[1288,128]{1,0:T(8,128)S(1)} %broadcast_select_fusion.6), channel_id=1, source_target_pairs={{0,1},{8,11},{1,2},{9,8},{2,3},{10,9},{3,0},{11,10},{4,5},{12,15},... | collective-permute-start | bytes 1978376 | tf_op jit(solution)/shard_map/ppermute | solution.py:273
  90.4 26.1 %collective-permute-start.45 = (f32[1288,128]{1,0:T(8,128)S(1)}, f32[1288,128]{1,0:T(8,128)S(1)}, u32[]{:S(2)}, u32[]{:S(2)}) collective-permute-start(f32[1288,128]{1,0:T(8,128)S(1)} %collective-permute-done.35), channel_id=1, source_target_pairs={{0,16},{16,32},{32,48},{48,0},{1,17},{17,33},{33,49},{49,1},{2,18}... | collective-permute-start | bytes 1978376 | tf_op jit(solution)/shard_map/ppermute | solution.py:260
  91.7 24.8 %collective-permute-start.46 = (f32[1288,128]{1,0:T(8,128)S(1)}, f32[1288,128]{1,0:T(8,128)}, u32[]{:S(2)}, u32[]{:S(2)}) collective-permute-start(f32[1288,128]{1,0:T(8,128)S(1)} %collective-permute-done.35), channel_id=1, source_target_pairs={{0,48},{16,0},{32,16},{48,32},{1,49},{17,1},{33,17},{49,33},{2,50}... | collective-permute-start | bytes 1978376 | tf_op jit(solution)/shard_map/ppermute | solution.py:264
  98.9 17.6 %collective-permute-start.44 = (f32[1288,128]{1,0:T(8,128)S(1)}, f32[1288,128]{1,0:T(8,128)S(1)}, u32[]{:S(2)}, u32[]{:S(2)}) collective-permute-start(f32[1288,128]{1,0:T(8,128)S(1)} %collective-permute-done.36), channel_id=1, source_target_pairs={{0,8},{8,0},{1,9},{9,1},{2,10},{10,2},{3,11},{11,3},{4,12},{12,4},... | collective-permute-start | bytes 1978376 | tf_op jit(solution)/shard_map/ppermute | solution.py:256
  105.5 11.0 %collective-permute-start.40 = (f32[648,128]{1,0:T(8,128)S(1)}, f32[648,128]{1,0:T(8,128)S(1)}, u32[]{:S(2)}, u32[]{:S(2)}) collective-permute-start(f32[648,128]{1,0:T(8,128)S(1)} %add.351), channel_id=1, source_target_pairs={{0,32},{16,48},{32,0},{48,16},{1,33},{17,49},{33,1},{49,17},{2,34}... | collective-permute-start | bytes 995336 | tf_op jit(solution)/shard_map/ppermute | solution.py:281
  119.7 10.4 %collective-permute-start.50 = (f32[1288,128]{1,0:T(8,128)S(1)}, f32[1288,128]{1,0:T(8,128)}, u32[]{:S(2)}, u32[]{:S(2)}) collective-permute-start(f32[1288,128]{1,0:T(8,128)S(1)} %broadcast_select_fusion.4), channel_id=1, source_target_pairs={{0,16},{8,56},{16,32},{24,8},{32,48},{40,24},{48,0},{56,40},{1,17}... | collective-permute-start | bytes 1978376 | tf_op jit(solution)/shard_map/ppermute | solution.py:273
  (27 other events, 386.0 us)

commit v6 on v5

v6 whole, which is shorter than its diff:
```python
import functools

import jax
import jax.numpy as jnp
import numpy as np
from jax import lax
from jax.experimental import pallas as pl
from jax.experimental.pallas import tpu as pltpu
from jax.sharding import Mesh
from jax.sharding import PartitionSpec as P

W = 128
SLOTS = 10
DATA = SLOTS * W
TILES = 2 * DATA
ROWS = TILES + 16
ROW = ("zl", "y", "core")
COL = ("zh", "x")


def pack_kernel(core_ref, am_ref, bm_ref, a_ref, b_ref, keep_ref, send_ref, sem):
    core = core_ref[0]
    row = lax.broadcasted_iota(jnp.int32, (8, W), 0)
    lane = lax.broadcasted_iota(jnp.int32, (8, W), 1)
    factors = (
        (am_ref, a_ref, lambda r, c: (row == c) & (lane // 8 == r)),
        (bm_ref, b_ref, lambda r, c: (row == r) & (lane % 8 == c)),
    )

    def copy(n, src, dst, r, c, cols, at):
        return pltpu.make_async_copy(
            src.at[pl.ds(r * W, W), pl.ds(c * W, W)], dst.at[pl.ds(at, W), :], sem.at[n * 32 + r * cols + c]
        )

    for n, (mask, src, spot) in enumerate(factors):
        rows, cols = mask.shape
        slot = jnp.int32(0)
        tile = jnp.zeros((8, W), jnp.float32)
        for r in range(rows):
            for c in range(cols):
                on = mask[r, c] != 0
                fits = on & (slot < 2 * SLOTS)
                at = pl.multiple_of(slot * W, W)
                for dst, here in ((keep_ref, core == n), (send_ref, core != n)):

                    @pl.when(fits & here)
                    def _():
                        copy(n, src, dst, r, c, cols, at).start()

                slot = slot + on.astype(jnp.int32)
                tile = jnp.where(spot(r, c), jnp.where(on, slot, 0).astype(jnp.float32), tile)
        flag = jnp.zeros((8, W), jnp.float32) + jnp.where(slot > SLOTS, 1.0, 0.0)
        for dst, here in ((keep_ref, core == n), (send_ref, core != n)):

            @pl.when(here)
            def _():
                dst[pl.ds(TILES, 8), :] = tile
                dst[pl.ds(TILES + 8, 8), :] = flag

    for n, (mask, src, _) in enumerate(factors):
        rows, cols = mask.shape
        for r in range(rows):
            for c in range(cols):

                @pl.when(mask[r, c] != 0)
                def _():
                    copy(n, src, keep_ref, r, c, cols, 0).wait()


def pack(core, a_mask, b_mask, a_values, b_values):
    smem = pl.BlockSpec(memory_space=pltpu.SMEM)
    vmem = pl.BlockSpec(memory_space=pltpu.VMEM)
    hbm = pl.BlockSpec(memory_space=pl.ANY)
    return pl.pallas_call(
        pack_kernel,
        out_shape=(jax.ShapeDtypeStruct((ROWS, W), jnp.float32),) * 2,
        in_specs=[smem, smem, smem, hbm, hbm],
        out_specs=(vmem,) * 2,
        scratch_shapes=[pltpu.SemaphoreType.DMA((64,))],
        name="pack",
    )(core, a_mask, b_mask, a_values, b_values)


def merge_kernel(core_ref, keep_ref, got_ref, main_ref, excess_ref):
    core = core_ref[0]
    for ref, at in ((keep_ref, core), (got_ref, 1 - core)):
        main_ref[pl.ds(pl.multiple_of(at * DATA, DATA), DATA), :] = ref[pl.ds(0, DATA), :]
        main_ref[pl.ds(pl.multiple_of(TILES + at * 8, 8), 8), :] = ref[pl.ds(TILES, 8), :]
    own = keep_ref[pl.ds(TILES + 8, 8), :]
    also = got_ref[pl.ds(TILES + 8, 8), :]
    kept = jnp.where(also[:1] > 0, got_ref[pl.ds(DATA, DATA), :], 0.0)
    excess_ref[pl.ds(0, DATA), :] = jnp.where(own[:1] > 0, keep_ref[pl.ds(DATA, DATA), :], kept)
    excess_ref[pl.ds(DATA, 8), :] = own + also


def merge(core, keep, got):
    vmem = pl.BlockSpec(memory_space=pltpu.VMEM)
    return pl.pallas_call(
        merge_kernel,
        out_shape=(
            jax.ShapeDtypeStruct((ROWS, W), jnp.float32),
            jax.ShapeDtypeStruct((DATA + 8, W), jnp.float32),
        ),
        in_specs=[pl.BlockSpec(memory_space=pltpu.SMEM), vmem, vmem],
        out_specs=(vmem, vmem),
        name="merge",
    )(core, keep, got)


def split(x):
    high = x.astype(jnp.bfloat16)
    low = (x - high.astype(jnp.float32)).astype(jnp.bfloat16)
    return high, low


def product_kernel(shapes, spread, where_ref, keep_ref, *refs):
    count = sum(shapes)
    pieces = list(refs[:count])
    out_ref, acc, a_all, b_all, a_meta, b_meta, table, words, table_s, words_s, list_s, sem, sem_t, sem_o = refs[count:]
    core = where_ref[0]
    groups = []
    for size in shapes:
        groups.append(pieces[:size])
        pieces = pieces[size:]
    lines, extra = groups[:17], groups[17:]

    def parts(piece):
        if len(piece) == 1:
            return [piece[0].at[pl.ds(0, DATA), :], piece[0].at[pl.ds(DATA, DATA), :], piece[0].at[pl.ds(TILES, 16), :]]
        return [piece[0], piece[1].at[pl.ds(0, DATA), :], piece[1].at[pl.ds(DATA, 16), :]]

    def copies(side):
        found = []
        for n in range(8):
            a_at, b_at = where_ref[1 + n], where_ref[9 + n]
            pair = (parts(lines[2 * n]), parts(lines[2 * n + 1]))
            a_parts, b_parts = pair[side], pair[1 - side]
            found.append((a_parts[side], a_all.at[pl.ds(a_at * DATA, DATA), :]))
            found.append((a_parts[2].at[pl.ds(8 * side, 8), :], a_meta.at[pl.ds(a_at * 8, 8), :]))
            for h in range(2):
                found.append((b_parts[h], b_all.at[pl.ds((b_at * 2 + h) * DATA, DATA), :]))
            found.append((b_parts[2], b_meta.at[pl.ds(b_at * 16, 16), :]))
        if not spread:
            e = lines[16]
            found.append((e[side].at[pl.ds(0, DATA), :], a_all.at[pl.ds(8 * DATA, DATA), :]))
            found.append((e[1 - side].at[pl.ds(0, DATA), :], b_all.at[pl.ds(16 * DATA, DATA), :]))
        for n, piece in enumerate(extra):
            if n < 8:
                found.append((piece[0], a_all.at[pl.ds((8 + where_ref[1 + n]) * DATA, DATA), :]))
            else:
                h = side if n < 16 else 1 - side
                at = 16 + where_ref[9 + n % 8] * 2 + h
                found.append((piece[0], b_all.at[pl.ds(at * DATA, DATA), :]))
        return [pltpu.make_async_copy(src, dst, sem.at[n]) for n, (src, dst) in enumerate(found)]

    for side in range(2):

        @pl.when(core == side)
        def _():
            for copy in copies(side):
                copy.start()

    acc[...] = jnp.zeros(acc.shape, jnp.float32)
    for side in range(2):

        @pl.when(core == side)
        def _():
            for copy in copies(side):
                copy.wait()

    def address(piece, rank, pieces):
        rest = pieces * SLOTS + rank - (SLOTS + 1)
        if spread:
            rest = rest + piece * SLOTS
        return jnp.where(rank <= SLOTS, piece * SLOTS + rank - 1, rest)

    k8 = lax.broadcasted_iota(jnp.int32, (8, W), 0)
    one = jnp.ones((8, W), jnp.int32)
    low = jnp.zeros((8, W), jnp.int32)
    high = jnp.zeros((8, W), jnp.int32)
    for c in range(8):
        a_slot = a_meta[pl.ds(c * 8, 8), :].astype(jnp.int32)
        b0 = b_meta[pl.ds(c * 16, 8), :].astype(jnp.int32)
        b1 = pltpu.roll(b_meta[pl.ds(c * 16 + 8, 8), :], 4, 0).astype(jnp.int32)
        b_slot = jnp.where(k8 < 4, b0, b1)
        live = (keep_ref[pl.ds(c * 8, 8), :] != 0) & (a_slot > 0) & (b_slot > 0)
        a_at = address(c, a_slot, 8)
        b_at = address(jnp.where(k8 < 4, 2 * c, 2 * c + 1), b_slot, 16)
        table[pl.ds(c * 8, 8), :] = jnp.where(live, a_at + b_at * 65536, 0)
        bit = jnp.where(live, lax.shift_left(one, k8 + 8 * (c % 4)), 0)
        if c < 4:
            low = low | bit
        else:
            high = high | bit
    for n, word in enumerate((low, high)):
        word = word | pltpu.roll(word, 4, 0)
        word = word | pltpu.roll(word, 2, 0)
        word = word | pltpu.roll(word, 1, 0)
        words[pl.ds(8 * n, 8), :] = jnp.where(k8 == 0, word, lax.population_count(word))
    t0 = pltpu.make_async_copy(table, table_s, sem_t.at[0])
    t1 = pltpu.make_async_copy(words, words_s, sem_t.at[1])
    t0.start()
    t1.start()
    t0.wait()
    t1.wait()

    def gather(p, total):
        for n in range(2):

            def one(m, bits):
                lowest = bits & -bits
                k = 31 - lax.clz(lowest) + 32 * n
                list_s[0, total + m] = table_s[k, p]
                list_s[1, total + m] = p
                return bits ^ lowest

            found = words_s[8 * n + 1, p]
            lax.fori_loop(0, found, one, words_s[8 * n, p])
            total = total + found
        return total

    def term(entry):
        a_at = pl.multiple_of((entry & 65535) * W, W)
        b_at = pl.multiple_of(lax.shift_right_logical(entry, 16) * W, W)
        a_high, a_low = split(a_all[pl.ds(a_at, W), :])
        b_high, b_low = split(b_all[pl.ds(b_at, W), :])
        left = jnp.concatenate([a_high, a_low], axis=1)
        right = jnp.concatenate(
            [jnp.concatenate([b_high, b_low], axis=1), jnp.concatenate([b_low, b_high], axis=1)], axis=0
        )
        both = jnp.dot(left, right, preferred_element_type=jnp.float32)
        return both[:, :W] + both[:, W:]

    def place(p):
        return pl.ds(pl.multiple_of(p // 8 * W, W), W), pl.ds(pl.multiple_of(p % 8 * W, W), W)

    total = lax.fori_loop(0, 32, gather, jnp.int32(0))

    def four(t, _):
        terms = [term(list_s[0, 4 * t + n]) for n in range(4)]
        for n in range(4):
            rows, cols = place(list_s[1, 4 * t + n])
            acc[rows, cols] = acc[rows, cols] + terms[n]
        return 0

    def single(t, _):
        rows, cols = place(list_s[1, t])
        acc[rows, cols] = acc[rows, cols] + term(list_s[0, t])
        return 0

    lax.fori_loop(0, total // 4, four, 0)
    lax.fori_loop(total // 4 * 4, total, single, 0)
    out = pltpu.make_async_copy(acc, out_ref, sem_o)
    out.start()
    out.wait()


def product(spread, where, keep_tile, groups):
    hbm = pl.BlockSpec(memory_space=pl.ANY)
    shapes = tuple(len(group) for group in groups)
    pieces = [piece for group in groups for piece in group]
    more = (8, 16) if spread else (1, 1)
    return pl.pallas_call(
        functools.partial(product_kernel, shapes, spread),
        out_shape=jax.ShapeDtypeStruct((512, 1024), jnp.float32),
        in_specs=[pl.BlockSpec(memory_space=pltpu.SMEM), pl.BlockSpec(memory_space=pltpu.VMEM)] + [hbm] * len(pieces),
        out_specs=hbm,
        scratch_shapes=[
            pltpu.VMEM((512, 1024), jnp.float32),
            pltpu.VMEM(((8 + more[0]) * DATA, W), jnp.float32),
            pltpu.VMEM(((16 + more[1]) * DATA, W), jnp.float32),
            pltpu.VMEM((64, W), jnp.float32),
            pltpu.VMEM((128, W), jnp.float32),
            pltpu.VMEM((64, W), jnp.int32),
            pltpu.VMEM((16, W), jnp.int32),
            pltpu.SMEM((64, W), jnp.int32),
            pltpu.SMEM((16, W), jnp.int32),
            pltpu.SMEM((2, 2048), jnp.int32),
            pltpu.SemaphoreType.DMA((72,)),
            pltpu.SemaphoreType.DMA((2,)),
            pltpu.SemaphoreType.DMA,
        ],
        compiler_params=pltpu.CompilerParams(vmem_limit_bytes=48 * 1024 * 1024),
        name="product",
    )(where, keep_tile, *pieces)


def swap(x, axis):
    return lax.ppermute(x, axis, [(0, 1), (1, 0)])


def right(x, axis):
    return lax.ppermute(x, axis, [(n, (n + 1) % 4) for n in range(4)])


def left(x, axis):
    return lax.ppermute(x, axis, [(n, (n - 1) % 4) for n in range(4)])


def opposite(from_left, from_right, core, axis):
    if axis == "x":
        axes, at = ("core", "x"), lambda n, c: c * 4 + n % 4
    else:
        axes, at = ("y", "core"), lambda n, c: n % 4 * 2 + c
    pairs = [(at(n, c), at(n + 1 - 2 * c, c)) for n in range(4) for c in range(2)]
    return lax.ppermute(jnp.where(core == 0, from_left, from_right), axes, pairs)


def gate(*done):
    return lambda x: lax.optimization_barrier((x, *done))[0]


def around(own, z, axis, core):
    other = swap(own, z)
    found = []
    for x in (own, other):
        r, l = right(x, axis), left(x, axis)
        found.extend((x, r, l, opposite(r, l, core, axis)))
    return found


SIZES = (2, 4, 2, 2, 4)


def route(x, ring, z):
    pairs = []
    for n in range(128):
        zl, y, core, zh, at = (int(i) for i in np.unravel_index(n, SIZES))
        if core == 0:
            to = (zl, y, core, zh ^ z, ring(at))
        else:
            to = (zl ^ z, ring(y), core, zh, at)
        pairs.append((n, int(np.ravel_multi_index(to, SIZES))))
    return lax.ppermute(x, ROW + COL, pairs)


def forth(x):
    return route(x, lambda n: (n + 1) % 4, 0)


def back(x):
    return route(x, lambda n: (n - 1) % 4, 0)


def cross(x):
    return route(x, lambda n: n, 1)


def pair(x, distance):
    return route(x, lambda n: n ^ distance, 0)


def per_device(a_values, a_mask, b_values, b_mask, keep):
    zl, y, core = (lax.axis_index(n) for n in ROW)
    zh, x = (lax.axis_index(n) for n in COL)
    core_s = core.reshape(1).astype(jnp.int32)
    keep_tile = jnp.pad(jnp.transpose(keep, (1, 0, 2)).reshape(64, 32), ((0, 0), (0, W - 32)))
    held, sent = pack(core_s, a_mask, b_mask, a_values, b_values)
    m, e = merge(core_s, held, swap(sent, "core"))

    r, l, z0 = forth(m), back(m), cross(m[:DATA])

    g = gate(r, l, z0)
    z1 = cross(g(m[DATA:]))
    o0, o1 = forth(g(r[:DATA])), back(g(l[DATA:]))
    e1 = pair(g(e), 1)
    cm = swap(g(m), "core")
    cr = swap(gate(cm)(g(r)), "core")
    cl = swap(gate(cr)(g(l)), "core")
    e = e + e1

    g = gate(z1, o0, o1, e1, cl)
    z = jnp.concatenate([g(z0), g(z1)])
    zr, zl_ = forth(z), back(z)
    e2 = cross(g(e))
    cz = swap(z, "core")
    co0 = swap(gate(cz)(g(o0)), "core")
    co1 = swap(gate(co0)(g(o1)), "core")
    e = e + e2

    g = gate(zr, zl_, e2, co1)
    zo0, zo1 = forth(g(zr[:DATA])), back(g(zl_[DATA:]))
    e3 = pair(g(e), 2)
    czr = swap(g(zr), "core")
    czl = swap(gate(czr)(g(zl_)), "core")
    e = e + e3

    g = gate(zo0, zo1, e3, czl)
    ce = swap(g(e), "core")
    czo0, czo1 = swap(g(zo0), "core"), swap(g(zo1), "core")

    shifts = (0, 3, 1, 2)
    groups = [[m], [cm], [r], [cr], [l], [cl], [o0, o1], [co0, co1]]
    groups += [[z], [cz], [zr], [czr], [zl_], [czl], [zo0, zo1], [czo0, czo1], [e, ce]]
    where = [core] + [(zh ^ n) * 4 + (x + s) % 4 for n in range(2) for s in shifts]
    where += [(zl ^ n) * 4 + (y + s) % 4 for n in range(2) for s in shifts]
    where = jnp.stack(where).astype(jnp.int32)
    crowd = [q[DATA, 0] > 1.5 for q in (e, ce)]

    def few(_):
        return product(False, where, keep_tile, groups)

    def many(_):
        first = core == 0
        crowd_a, crowd_b = jnp.where(first, crowd[0], crowd[1]), jnp.where(first, crowd[1], crowd[0])
        rest_a = jnp.where(first, held, sent)[DATA:TILES]
        rest_b = jnp.where(first, sent, held)[DATA:TILES]
        some_a = jnp.where(first, e, ce)[:DATA]
        some_b = jnp.where(first, ce, e)[:DATA]

        def all_b(_):
            found = around(rest_b, "zl", "y", core)
            return tuple(found + [swap(p, "core") for p in found])

        more = lax.cond(crowd_a, lambda _: tuple(around(rest_a, "zh", "x", core)), lambda _: (some_a,) * 8, 0)
        more += lax.cond(crowd_b, all_b, lambda _: (some_b,) * 16, 0)
        return product(True, where, keep_tile, groups + [[p] for p in more])

    return lax.cond(crowd[0] | crowd[1], many, few, 0)


def solution(mesh):
    fine = Mesh(mesh.devices.reshape(2, 4, 2, 2, 4), ROW + COL)
    return jax.shard_map(
        per_device,
        mesh=fine,
        in_specs=(P(ROW, COL), P(ROW, COL), P(ROW, COL), P(ROW, COL), P(ROW, None, COL)),
        out_specs=P(ROW, COL),
        check_vma=False,
    )
```

time: 152 us -> 135 us (0.89)
  starting transfers between devices: 45.3 us -> 31.1 us
  other arithmetic: 3.49 us -> 0.26 us
  local copies, waits for them, and re-layouts: 5.9 us -> 8.7 us
    ppermute x16 -> x13, starting transfers between devices: 25.2 us -> 13.5 us  [route(): return lax.ppermute(x, ROW + COL, pairs)]
    unnamed x40 -> x39, local copies, waits for them, and re-layouts: 3.24 us -> 7.26 us
    ppermute x15 -> x12, starting transfers between devices: 20.1 us -> 17.6 us  [swap(): return lax.ppermute(x, axis, [(0, 1), (1, 0)])]
    add x6 -> x3, other arithmetic: 2.06 us -> 0.26 us  [the longest x1 0.09 us: per_device(): e = e + e1]
    ppermute x16 -> x13, waiting for transfers between devices: 60.5 us -> 59.8 us  [route(): return lax.ppermute(x, ROW + COL, pairs)]
    ppermute x15 -> x12, waiting for transfers between devices: 14.7 us -> 14.3 us  [swap(): return lax.ppermute(x, axis, [(0, 1), (1, 0)])]
  transfers between devices with their start and end apart: 31 -> 25, of which waited for: 10 -> 14; matrix products, arithmetic and copies ran while one was open for 4% -> 1% of each run, Pallas kernels for 1% -> 0%
where the time goes in v6:
time: 135 us; the launch traced here: 133 us
  waiting for transfers between devices  74.1 us (55%)
  starting transfers between devices  31.1 us (23%)
  Pallas kernels  16.8 us (12%)
  local copies, waits for them, and re-layouts  8.7 us (6%)
    ppermute x13, waiting for transfers between devices, route(): return lax.ppermute(x, ROW + COL, pairs)  59.8 us
    ppermute x12, starting transfers between devices, swap(): return lax.ppermute(x, axis, [(0, 1), (1, 0)])  17.6 us
    ppermute x12, waiting for transfers between devices, swap(): return lax.ppermute(x, axis, [(0, 1), (1, 0)])  14.3 us
    ppermute x13, starting transfers between devices, route(): return lax.ppermute(x, ROW + COL, pairs)  13.5 us
    pallas_call x1, Pallas kernels, product(): pl.pallas_call(functools.partial(product_kernel, shapes, spread), out_sha...  10.8 us
    unnamed x39, local copies, waits for them, and re-layouts  7.26 us
    pallas_call x1, Pallas kernels, pack(): pl.pallas_call(pack_kernel, out_shape=(jax.ShapeDtypeStruct((ROWS, W), jn...  3.66 us
  transfers between devices with their start and end apart: 25, of which 14 were waited for; matrix products, arithmetic and copies ran while one was open for 1% of the time, Pallas kernels for 0%

profile of v6, /device:TPU:1, one launch (start us, length us, event | category | flops | bytes accessed | tf_op | source)
XLA Modules:
  0.0 132.5 jit_solution(11649237750874916092)
XLA Ops:
  0.0 3.7 %pack.1 = (f32[2576,128]{1,0:T(8,128)S(1)}, f32[2576,128]{1,0:T(8,128)}) custom-call(s32[1]{0:T(128)} %bitcast.core_ref, s32[4,8]{1,0:T(4,128)} %am_ref.1, s32[4,8]{1,0:T(4,128)} %bm_ref.1, f32[512,1024]{1,0:T(8,128)} %a_ref.1, f32[512,1024]{1,0:T(8,128)} %b_ref.1), custom_call_target="tpu_custom_call" | custom-call | tf_op jit(solution)/shard_map/pack/pallas_call | solution.py:74
  3.7 1.5 %collective-permute-start.22 = (f32[2576,128]{1,0:T(8,128)}, f32[2576,128]{1,0:T(8,128)S(1)}, u32[]{:S(2)}, u32[]{:S(2)}) collective-permute-start(f32[2576,128]{1,0:T(8,128)} %get-tuple-element.275), channel_id=1, source_target_pairs={{0,8},{8,0},{1,9},{9,1},{2,10},{10,2},{3,11},{11,3},{4,12},{12,4},... | collective-permute-start | bytes 3956744 | tf_op jit(solution)/shard_map/ppermute | solution.py:289
  5.1 2.9 %collective-permute-done.22.got_ref = f32[2576,128]{1,0:T(8,128)S(1)} collective-permute-done((f32[2576,128]{1,0:T(8,128)}, f32[2576,128]{1,0:T(8,128)S(1)}, u32[]{:S(2)}, u32[]{:S(2)}) %collective-permute-start.22) | collective-permute-done | bytes 1318944 | tf_op jit(solution)/shard_map/ppermute | solution.py:289
  9.1 2.4 %merge.1 = (f32[2576,128]{1,0:T(8,128)S(1)}, f32[1288,128]{1,0:T(8,128)}) custom-call(s32[1]{0:T(128)} %bitcast.core_ref, f32[2576,128]{1,0:T(8,128)S(1)} %get-tuple-element.274.keep_ref, f32[2576,128]{1,0:T(8,128)} %copy-done.16), custom_call_target="tpu_custom_call" | custom-call | tf_op jit(solution)/shard_map/merge/pallas_call | solution.py:98
  12.9 1.5 %collective-permute-start.24 = (f32[2576,128]{1,0:T(8,128)S(1)}, f32[2576,128]{1,0:T(8,128)S(1)}, u32[]{:S(2)}, u32[]{:S(2)}) collective-permute-start(f32[2576,128]{1,0:T(8,128)S(1)} %get-tuple-element.284), channel_id=1, source_target_pairs={{0,3},{1,0},{2,1},{3,2},{4,7},{5,4},{6,5},{7,6},{8,56},{9,57},{10,... | collective-permute-start | bytes 3956744 | tf_op jit(solution)/shard_map/ppermute | solution.py:334
  14.4 1.7 %collective-permute-start.25 = (f32[1280,128]{1,0:T(8,128)S(1)}, f32[1280,128]{1,0:T(8,128)S(1)}, u32[]{:S(2)}, u32[]{:S(2)}) collective-permute-start(f32[1280,128]{1,0:T(8,128)S(1)} %slice.44), channel_id=1, source_target_pairs={{0,4},{1,5},{2,6},{3,7},{4,0},{5,1},{6,2},{7,3},{8,72},{9,73},{10,... | collective-permute-start | bytes 1966088 | tf_op jit(solution)/shard_map/ppermute | solution.py:334
  16.1 11.1 %collective-permute-done.25 = f32[1280,128]{1,0:T(8,128)S(1)} collective-permute-done((f32[1280,128]{1,0:T(8,128)S(1)}, f32[1280,128]{1,0:T(8,128)S(1)}, u32[]{:S(2)}, u32[]{:S(2)}) %collective-permute-start.25) | collective-permute-done | bytes 655392 | tf_op jit(solution)/shard_map/ppermute | solution.py:334
  27.3 2.5 %collective-permute-done.23 = f32[2576,128]{1,0:T(8,128)S(1)} collective-permute-done((f32[2576,128]{1,0:T(8,128)S(1)}, f32[2576,128]{1,0:T(8,128)S(1)}, u32[]{:S(2)}, u32[]{:S(2)}) %collective-permute-start.23) | collective-permute-done | bytes 1318944 | tf_op jit(solution)/shard_map/ppermute | solution.py:334
  29.7 5.1 %collective-permute-start.30 = (f32[2576,128]{1,0:T(8,128)S(1)}, f32[2576,128]{1,0:T(8,128)S(1)}, u32[]{:S(2)}, u32[]{:S(2)}) collective-permute-start(f32[2576,128]{1,0:T(8,128)S(1)} %get-tuple-element.284), channel_id=1, source_target_pairs={{0,8},{8,0},{1,9},{9,1},{2,10},{10,2},{3,11},{11,3},{4,12},{12,4},... | collective-permute-start | bytes 3956744 | tf_op jit(solution)/shard_map/ppermute | solution.py:289
  34.8 2.7 %collective-permute-done.30 = f32[2576,128]{1,0:T(8,128)S(1)} collective-permute-done((f32[2576,128]{1,0:T(8,128)S(1)}, f32[2576,128]{1,0:T(8,128)S(1)}, u32[]{:S(2)}, u32[]{:S(2)}) %collective-permute-start.30) | collective-permute-done | bytes 1318944 | tf_op jit(solution)/shard_map/ppermute | solution.py:289
  37.9 2.7 %collective-permute-done.31 = f32[2576,128]{1,0:T(8,128)S(1)} collective-permute-done((f32[2576,128]{1,0:T(8,128)S(1)}, f32[2576,128]{1,0:T(8,128)S(1)}, u32[]{:S(2)}, u32[]{:S(2)}) %collective-permute-start.31) | collective-permute-done | bytes 1318944 | tf_op jit(solution)/shard_map/ppermute | solution.py:289
  42.1 2.0 %collective-permute-start.29 = (f32[1296,128]{1,0:T(8,128)S(1)}, f32[1296,128]{1,0:T(8,128)S(1)}, u32[]{:S(2)}, u32[]{:S(2)}) collective-permute-start(f32[1296,128]{1,0:T(8,128)S(1)} %slice.61), channel_id=1, source_target_pairs={{0,3},{1,0},{2,1},{3,2},{4,7},{5,4},{6,5},{7,6},{8,56},{9,57},{10,... | collective-permute-start | bytes 1990664 | tf_op jit(solution)/shard_map/ppermute | solution.py:334
  44.2 1.5 %collective-permute-start.28 = (f32[1280,128]{1,0:T(8,128)S(1)}, f32[1280,128]{1,0:T(8,128)S(1)}, u32[]{:S(2)}, u32[]{:S(2)}) collective-permute-start(f32[1280,128]{1,0:T(8,128)S(1)} %slice.60), channel_id=1, source_target_pairs={{0,1},{1,2},{2,3},{3,0},{4,5},{5,6},{6,7},{7,4},{8,24},{9,25},{10,... | collective-permute-start | bytes 1966088 | tf_op jit(solution)/shard_map/ppermute | solution.py:334
  45.7 13.0 %collective-permute-done.28 = f32[1280,128]{1,0:T(8,128)S(1)} collective-permute-done((f32[1280,128]{1,0:T(8,128)S(1)}, f32[1280,128]{1,0:T(8,128)S(1)}, u32[]{:S(2)}, u32[]{:S(2)}) %collective-permute-start.28) | collective-permute-done | bytes 655392 | tf_op jit(solution)/shard_map/ppermute | solution.py:334
  62.5 2.7 %collective-permute-done.36 = f32[2576,128]{1,0:T(8,128)S(1)} collective-permute-done((f32[2576,128]{1,0:T(8,128)S(1)}, f32[2576,128]{1,0:T(8,128)S(1)}, u32[]{:S(2)}, u32[]{:S(2)}) %collective-permute-start.36) | collective-permute-done | bytes 1318944 | tf_op jit(solution)/shard_map/ppermute | solution.py:289
  67.0 1.9 %collective-permute-start.35 = (f32[2576,128]{1,0:T(8,128)S(1)}, f32[2576,128]{1,0:T(8,128)S(1)}, u32[]{:S(2)}, u32[]{:S(2)}) collective-permute-start(f32[2576,128]{1,0:T(8,128)S(1)} %constant_dynamic-update-slice_fusion), channel_id=1, source_target_pairs={{0,3},{1,0},{2,1},{3,2},{4,7},{5,4},{6,5},{7,6},{8,56},{9,57},{10,... | collective-permute-start | bytes 3956744 | tf_op jit(solution)/shard_map/ppermute | solution.py:334
  71.2 14.3 %collective-permute-done.33 = f32[1288,128]{1,0:T(8,128)S(1)} collective-permute-done((f32[1288,128]{1,0:T(8,128)S(1)}, f32[1288,128]{1,0:T(8,128)S(1)}, u32[]{:S(2)}, u32[]{:S(2)}) %collective-permute-start.33) | collective-permute-done | bytes 659488 | tf_op jit(solution)/shard_map/ppermute | solution.py:334
  85.6 4.3 %collective-permute-start.42 = (f32[2576,128]{1,0:T(8,128)S(1)}, f32[2576,128]{1,0:T(8,128)S(1)}, u32[]{:S(2)}, u32[]{:S(2)}) collective-permute-start(f32[2576,128]{1,0:T(8,128)S(1)} %collective-permute-done.34), channel_id=1, source_target_pairs={{0,8},{8,0},{1,9},{9,1},{2,10},{10,2},{3,11},{11,3},{4,12},{12,4},... | collective-permute-start | bytes 3956744 | tf_op jit(solution)/shard_map/ppermute | solution.py:289
  90.0 2.7 %collective-permute-done.42 = f32[2576,128]{1,0:T(8,128)S(1)} collective-permute-done((f32[2576,128]{1,0:T(8,128)S(1)}, f32[2576,128]{1,0:T(8,128)S(1)}, u32[]{:S(2)}, u32[]{:S(2)}) %collective-permute-start.42) | collective-permute-done | bytes 1318944 | tf_op jit(solution)/shard_map/ppermute | solution.py:289
  94.1 1.4 %collective-permute-start.41 = (f32[1296,128]{1,0:T(8,128)S(1)}, f32[1296,128]{1,0:T(8,128)}, u32[]{:S(2)}, u32[]{:S(2)}) collective-permute-start(f32[1296,128]{1,0:T(8,128)S(1)} %slice.64), channel_id=1, source_target_pairs={{0,3},{1,0},{2,1},{3,2},{4,7},{5,4},{6,5},{7,6},{8,56},{9,57},{10,... | collective-permute-start | bytes 1990664 | tf_op jit(solution)/shard_map/ppermute | solution.py:334
  96.6 17.4 %collective-permute-done.40 = f32[1280,128]{1,0:T(8,128)} collective-permute-done((f32[1280,128]{1,0:T(8,128)S(1)}, f32[1280,128]{1,0:T(8,128)}, u32[]{:S(2)}, u32[]{:S(2)}) %collective-permute-start.40) | collective-permute-done | bytes 655392 | tf_op jit(solution)/shard_map/ppermute | solution.py:334
  114.1 1.9 %collective-permute-start.46 = (f32[1296,128]{1,0:T(8,128)}, f32[1296,128]{1,0:T(8,128)}, u32[]{:S(2)}, u32[]{:S(2)}) collective-permute-start(f32[1296,128]{1,0:T(8,128)} %collective-permute-done.41), channel_id=1, source_target_pairs={{0,8},{8,0},{1,9},{9,1},{2,10},{10,2},{3,11},{11,3},{4,12},{12,4},... | collective-permute-start | bytes 1990664 | tf_op jit(solution)/shard_map/ppermute | solution.py:289
  120.2 11.0 %conditional.3 = (f32[512,1024]{1,0:T(8,128)S(1)}) conditional(s32[]{:T(128)} %convert_element_type.9, (s32[17]{0:T(128)S(1)}, s32[64,128]{0,1:T(8,128)S(1)}, f32[2576,128]{1,0:T(8,128)S(1)}, f32[2576,128]{1,0:T(8,128)}, f32[2576,128]{1,0:T(8,128)}, /*index=5*/f32[2576,128]{1,0:T(8,128)}, f32[2576,128]{1,0:T(8,128)}, f32[2576,128]{1,0:T(8,128)}, ...), branch_computations={%region_0.1_spmd, %region_1.6_spmd} | conditional | flops 983047 | bytes 69534936 | solution.py:419
  120.2 10.8 %product.2 = f32[512,1024]{1,0:T(8,128)S(1)} custom-call(s32[17]{0:T(128)S(1)} %get-tuple-element.154.where_ref, s32[64,128]{1,0:T(8,128)S(1)} %copy.9.keep_ref, f32[2576,128]{1,0:T(8,128)S(1)} %get-tuple-element.156.refs_0_, f32[2576,128]{1,0:T(8,128)} %get-tuple-element.157.refs_1_, f32[2576,128]{1,0:T(8,128)} %get-tuple-element.158.refs_2_, ...), custom_call_target="tpu_custom_call" | custom-call | tf_op jit(solution)/shard_map/cond/branch_0_fun/product/pallas_call | solution.py:263
  (84 shorter events, 19.4 us)
Async XLA Ops:
  3.7 4.4 %collective-permute-start.22 = (f32[2576,128]{1,0:T(8,128)}, f32[2576,128]{1,0:T(8,128)S(1)}, u32[]{:S(2)}, u32[]{:S(2)}) collective-permute-start(f32[2576,128]{1,0:T(8,128)} %get-tuple-element.275), channel_id=1, source_target_pairs={{0,8},{8,0},{1,9},{9,1},{2,10},{10,2},{3,11},{11,3},{4,12},{12,4},... | collective-permute-start | bytes 3956744 | tf_op jit(solution)/shard_map/ppermute | solution.py:289
  11.5 18.2 %collective-permute-start.23 = (f32[2576,128]{1,0:T(8,128)S(1)}, f32[2576,128]{1,0:T(8,128)S(1)}, u32[]{:S(2)}, u32[]{:S(2)}) collective-permute-start(f32[2576,128]{1,0:T(8,128)S(1)} %get-tuple-element.284), channel_id=1, source_target_pairs={{0,1},{1,2},{2,3},{3,0},{4,5},{5,6},{6,7},{7,4},{8,24},{9,25},{10,... | collective-permute-start | bytes 3956744 | tf_op jit(solution)/shard_map/ppermute | solution.py:334
  12.9 16.9 %collective-permute-start.24 = (f32[2576,128]{1,0:T(8,128)S(1)}, f32[2576,128]{1,0:T(8,128)S(1)}, u32[]{:S(2)}, u32[]{:S(2)}) collective-permute-start(f32[2576,128]{1,0:T(8,128)S(1)} %get-tuple-element.284), channel_id=1, source_target_pairs={{0,3},{1,0},{2,1},{3,2},{4,7},{5,4},{6,5},{7,6},{8,56},{9,57},{10,... | collective-permute-start | bytes 3956744 | tf_op jit(solution)/shard_map/ppermute | solution.py:334
  14.4 12.9 %collective-permute-start.25 = (f32[1280,128]{1,0:T(8,128)S(1)}, f32[1280,128]{1,0:T(8,128)S(1)}, u32[]{:S(2)}, u32[]{:S(2)}) collective-permute-start(f32[1280,128]{1,0:T(8,128)S(1)} %slice.44), channel_id=1, source_target_pairs={{0,4},{1,5},{2,6},{3,7},{4,0},{5,1},{6,2},{7,3},{8,72},{9,73},{10,... | collective-permute-start | bytes 1966088 | tf_op jit(solution)/shard_map/ppermute | solution.py:334
  29.7 7.7 %collective-permute-start.30 = (f32[2576,128]{1,0:T(8,128)S(1)}, f32[2576,128]{1,0:T(8,128)S(1)}, u32[]{:S(2)}, u32[]{:S(2)}) collective-permute-start(f32[2576,128]{1,0:T(8,128)S(1)} %get-tuple-element.284), channel_id=1, source_target_pairs={{0,8},{8,0},{1,9},{9,1},{2,10},{10,2},{3,11},{11,3},{4,12},{12,4},... | collective-permute-start | bytes 3956744 | tf_op jit(solution)/shard_map/ppermute | solution.py:289
  37.5 3.0 %collective-permute-start.31 = (f32[2576,128]{1,0:T(8,128)S(1)}, f32[2576,128]{1,0:T(8,128)S(1)}, u32[]{:S(2)}, u32[]{:S(2)}) collective-permute-start(f32[2576,128]{1,0:T(8,128)S(1)} %collective-permute-done.23), channel_id=1, source_target_pairs={{0,8},{8,0},{1,9},{9,1},{2,10},{10,2},{3,11},{11,3},{4,12},{12,4},... | collective-permute-start | bytes 3956744 | tf_op jit(solution)/shard_map/ppermute | solution.py:289
  41.6 18.5 %collective-permute-start.32 = (f32[2576,128]{1,0:T(8,128)S(1)}, f32[2576,128]{1,0:T(8,128)S(1)}, u32[]{:S(2)}, u32[]{:S(2)}) collective-permute-start(f32[2576,128]{1,0:T(8,128)S(1)} %collective-permute-done.24), channel_id=1, source_target_pairs={{0,8},{8,0},{1,9},{9,1},{2,10},{10,2},{3,11},{11,3},{4,12},{12,4},... | collective-permute-start | bytes 3956744 | tf_op jit(solution)/shard_map/ppermute | solution.py:289
  42.1 17.0 %collective-permute-start.29 = (f32[1296,128]{1,0:T(8,128)S(1)}, f32[1296,128]{1,0:T(8,128)S(1)}, u32[]{:S(2)}, u32[]{:S(2)}) collective-permute-start(f32[1296,128]{1,0:T(8,128)S(1)} %slice.61), channel_id=1, source_target_pairs={{0,3},{1,0},{2,1},{3,2},{4,7},{5,4},{6,5},{7,6},{8,56},{9,57},{10,... | collective-permute-start | bytes 1990664 | tf_op jit(solution)/shard_map/ppermute | solution.py:334
  44.1 16.0 %collective-permute-start.27 = (f32[1296,128]{1,0:T(8,128)S(1)}, f32[1296,128]{1,0:T(8,128)S(1)}, u32[]{:S(2)}, u32[]{:S(2)}) collective-permute-start(f32[1296,128]{1,0:T(8,128)S(1)} %slice.45), channel_id=1, source_target_pairs={{0,4},{1,5},{2,6},{3,7},{4,0},{5,1},{6,2},{7,3},{8,72},{9,73},{10,... | collective-permute-start | bytes 1990664 | tf_op jit(solution)/shard_map/ppermute | solution.py:334
  44.1 14.9 %collective-permute-start.26 = (f32[1288,128]{1,0:T(8,128)S(1)}, f32[1288,128]{1,0:T(8,128)S(1)}, u32[]{:S(2)}, u32[]{:S(2)}) collective-permute-start(f32[1288,128]{1,0:T(8,128)S(1)} %copy-done.17), channel_id=1, source_target_pairs={{0,1},{1,0},{2,3},{3,2},{4,5},{5,4},{6,7},{7,6},{8,24},{9,25},{10,... | collective-permute-start | bytes 1978376 | tf_op jit(solution)/shard_map/ppermute | solution.py:334
  44.2 14.5 %collective-permute-start.28 = (f32[1280,128]{1,0:T(8,128)S(1)}, f32[1280,128]{1,0:T(8,128)S(1)}, u32[]{:S(2)}, u32[]{:S(2)}) collective-permute-start(f32[1280,128]{1,0:T(8,128)S(1)} %slice.60), channel_id=1, source_target_pairs={{0,1},{1,2},{2,3},{3,0},{4,5},{5,6},{6,7},{7,4},{8,24},{9,25},{10,... | collective-permute-start | bytes 1966088 | tf_op jit(solution)/shard_map/ppermute | solution.py:334
  61.3 3.9 %collective-permute-start.36 = (f32[2576,128]{1,0:T(8,128)S(1)}, f32[2576,128]{1,0:T(8,128)S(1)}, u32[]{:S(2)}, u32[]{:S(2)}) collective-permute-start(f32[2576,128]{1,0:T(8,128)S(1)} %constant_dynamic-update-slice_fusion), channel_id=1, source_target_pairs={{0,8},{8,0},{1,9},{9,1},{2,10},{10,2},{3,11},{11,3},{4,12},{12,4},... | collective-permute-start | bytes 3956744 | tf_op jit(solution)/shard_map/ppermute | solution.py:289
  65.2 3.8 %collective-permute-start.37 = (f32[1280,128]{1,0:T(8,128)S(1)}, f32[1280,128]{1,0:T(8,128)S(1)}, u32[]{:S(2)}, u32[]{:S(2)}) collective-permute-start(f32[1280,128]{1,0:T(8,128)S(1)} %collective-permute-done.28), channel_id=1, source_target_pairs={{0,8},{8,0},{1,9},{9,1},{2,10},{10,2},{3,11},{11,3},{4,12},{12,4},... | collective-permute-start | bytes 1966088 | tf_op jit(solution)/shard_map/ppermute | solution.py:289
  66.3 19.3 %collective-permute-start.34 = (f32[2576,128]{1,0:T(8,128)S(1)}, f32[2576,128]{1,0:T(8,128)S(1)}, u32[]{:S(2)}, u32[]{:S(2)}) collective-permute-start(f32[2576,128]{1,0:T(8,128)S(1)} %constant_dynamic-update-slice_fusion), channel_id=1, source_target_pairs={{0,1},{1,2},{2,3},{3,0},{4,5},{5,6},{6,7},{7,4},{8,24},{9,25},{10,... | collective-permute-start | bytes 3956744 | tf_op jit(solution)/shard_map/ppermute | solution.py:334
  67.0 18.6 %collective-permute-start.35 = (f32[2576,128]{1,0:T(8,128)S(1)}, f32[2576,128]{1,0:T(8,128)S(1)}, u32[]{:S(2)}, u32[]{:S(2)}) collective-permute-start(f32[2576,128]{1,0:T(8,128)S(1)} %constant_dynamic-update-slice_fusion), channel_id=1, source_target_pairs={{0,3},{1,0},{2,1},{3,2},{4,7},{5,4},{6,5},{7,6},{8,56},{9,57},{10,... | collective-permute-start | bytes 3956744 | tf_op jit(solution)/shard_map/ppermute | solution.py:334
  69.8 15.8 %collective-permute-start.38 = (f32[1296,128]{1,0:T(8,128)S(1)}, f32[1296,128]{1,0:T(8,128)S(1)}, u32[]{:S(2)}, u32[]{:S(2)}) collective-permute-start(f32[1296,128]{1,0:T(8,128)S(1)} %collective-permute-done.29), channel_id=1, source_target_pairs={{0,8},{8,0},{1,9},{9,1},{2,10},{10,2},{3,11},{11,3},{4,12},{12,4},... | collective-permute-start | bytes 1990664 | tf_op jit(solution)/shard_map/ppermute | solution.py:289
  70.8 14.8 %collective-permute-start.33 = (f32[1288,128]{1,0:T(8,128)S(1)}, f32[1288,128]{1,0:T(8,128)S(1)}, u32[]{:S(2)}, u32[]{:S(2)}) collective-permute-start(f32[1288,128]{1,0:T(8,128)S(1)} %add.116), channel_id=1, source_target_pairs={{0,4},{1,5},{2,6},{3,7},{4,0},{5,1},{6,2},{7,3},{8,72},{9,73},{10,... | collective-permute-start | bytes 1978376 | tf_op jit(solution)/shard_map/ppermute | solution.py:334
  85.6 7.0 %collective-permute-start.42 = (f32[2576,128]{1,0:T(8,128)S(1)}, f32[2576,128]{1,0:T(8,128)S(1)}, u32[]{:S(2)}, u32[]{:S(2)}) collective-permute-start(f32[2576,128]{1,0:T(8,128)S(1)} %collective-permute-done.34), channel_id=1, source_target_pairs={{0,8},{8,0},{1,9},{9,1},{2,10},{10,2},{3,11},{11,3},{4,12},{12,4},... | collective-permute-start | bytes 3956744 | tf_op jit(solution)/shard_map/ppermute | solution.py:289
  93.7 20.4 %collective-permute-start.43 = (f32[2576,128]{1,0:T(8,128)S(1)}, f32[2576,128]{1,0:T(8,128)S(1)}, u32[]{:S(2)}, u32[]{:S(2)}) collective-permute-start(f32[2576,128]{1,0:T(8,128)S(1)} %collective-permute-done.35), channel_id=1, source_target_pairs={{0,8},{8,0},{1,9},{9,1},{2,10},{10,2},{3,11},{11,3},{4,12},{12,4},... | collective-permute-start | bytes 3956744 | tf_op jit(solution)/shard_map/ppermute | solution.py:289
  94.1 19.9 %collective-permute-start.41 = (f32[1296,128]{1,0:T(8,128)S(1)}, f32[1296,128]{1,0:T(8,128)}, u32[]{:S(2)}, u32[]{:S(2)}) collective-permute-start(f32[1296,128]{1,0:T(8,128)S(1)} %slice.64), channel_id=1, source_target_pairs={{0,3},{1,0},{2,1},{3,2},{4,7},{5,4},{6,5},{7,6},{8,56},{9,57},{10,... | collective-permute-start | bytes 1990664 | tf_op jit(solution)/shard_map/ppermute | solution.py:334
  95.6 18.5 %collective-permute-start.39 = (f32[1288,128]{1,0:T(8,128)S(1)}, f32[1288,128]{1,0:T(8,128)S(1)}, u32[]{:S(2)}, u32[]{:S(2)}) collective-permute-start(f32[1288,128]{1,0:T(8,128)S(1)} %add.117), channel_id=1, source_target_pairs={{0,2},{1,3},{2,0},{3,1},{4,6},{5,7},{6,4},{7,5},{8,40},{9,41},{10,... | collective-permute-start | bytes 1978376 | tf_op jit(solution)/shard_map/ppermute | solution.py:334
  96.2 17.8 %collective-permute-start.40 = (f32[1280,128]{1,0:T(8,128)S(1)}, f32[1280,128]{1,0:T(8,128)}, u32[]{:S(2)}, u32[]{:S(2)}) collective-permute-start(f32[1280,128]{1,0:T(8,128)S(1)} %slice.63), channel_id=1, source_target_pairs={{0,1},{1,2},{2,3},{3,0},{4,5},{5,6},{6,7},{7,4},{8,24},{9,25},{10,... | collective-permute-start | bytes 1966088 | tf_op jit(solution)/shard_map/ppermute | solution.py:334
  114.1 6.1 %collective-permute-start.46 = (f32[1296,128]{1,0:T(8,128)}, f32[1296,128]{1,0:T(8,128)}, u32[]{:S(2)}, u32[]{:S(2)}) collective-permute-start(f32[1296,128]{1,0:T(8,128)} %collective-permute-done.41), channel_id=1, source_target_pairs={{0,8},{8,0},{1,9},{9,1},{2,10},{10,2},{3,11},{11,3},{4,12},{12,4},... | collective-permute-start | bytes 1990664 | tf_op jit(solution)/shard_map/ppermute | solution.py:289
  117.1 3.0 %collective-permute-start.45 = (f32[1280,128]{1,0:T(8,128)}, f32[1280,128]{1,0:T(8,128)}, u32[]{:S(2)}, u32[]{:S(2)}) collective-permute-start(f32[1280,128]{1,0:T(8,128)} %collective-permute-done.40), channel_id=1, source_target_pairs={{0,8},{8,0},{1,9},{9,1},{2,10},{10,2},{3,11},{11,3},{4,12},{12,4},... | collective-permute-start | bytes 1966088 | tf_op jit(solution)/shard_map/ppermute | solution.py:289
  (20 other events, 165.0 us)

commit v7 on v6

--- a/solution.py
+++ b/solution.py
@@ -280,7 +280,7 @@
             pltpu.SemaphoreType.DMA((2,)),
             pltpu.SemaphoreType.DMA,
         ],
-        compiler_params=pltpu.CompilerParams(vmem_limit_bytes=48 * 1024 * 1024),
+        compiler_params=pltpu.CompilerParams(vmem_limit_bytes=(40 if spread else 24) * 1024 * 1024),
         name="product",
     )(where, keep_tile, *pieces)
 
@@ -358,36 +358,28 @@
     held, sent = pack(core_s, a_mask, b_mask, a_values, b_values)
     m, e = merge(core_s, held, swap(sent, "core"))
 
-    r, l, z0 = forth(m), back(m), cross(m[:DATA])
-
-    g = gate(r, l, z0)
-    z1 = cross(g(m[DATA:]))
-    o0, o1 = forth(g(r[:DATA])), back(g(l[DATA:]))
-    e1 = pair(g(e), 1)
-    cm = swap(g(m), "core")
-    cr = swap(gate(cm)(g(r)), "core")
-    cl = swap(gate(cr)(g(l)), "core")
+    z0 = cross(m[:DATA])
+    r, l = forth(m), back(m)
+    cm = swap(m, "core")
+    z1 = cross(gate(z0, r, l)(m[DATA:]))
+    o0, o1 = forth(r[:DATA]), back(l[DATA:])
+    e1 = pair(gate(r, l)(e), 1)
+    cr, cl = swap(r, "core"), swap(l, "core")
     e = e + e1
 
-    g = gate(z1, o0, o1, e1, cl)
+    g = gate(o0, o1)
     z = jnp.concatenate([g(z0), g(z1)])
     zr, zl_ = forth(z), back(z)
-    e2 = cross(g(e))
-    cz = swap(z, "core")
-    co0 = swap(gate(cz)(g(o0)), "core")
-    co1 = swap(gate(co0)(g(o1)), "core")
+    e2 = cross(gate(z1)(e))
+    cz, co0, co1 = swap(z, "core"), swap(o0, "core"), swap(o1, "core")
     e = e + e2
 
-    g = gate(zr, zl_, e2, co1)
-    zo0, zo1 = forth(g(zr[:DATA])), back(g(zl_[DATA:]))
-    e3 = pair(g(e), 2)
-    czr = swap(g(zr), "core")
-    czl = swap(gate(czr)(g(zl_)), "core")
+    zo0, zo1 = forth(zr[:DATA]), back(zl_[DATA:])
+    e3 = pair(gate(zr, zl_)(e), 2)
+    czr, czl = swap(zr, "core"), swap(zl_, "core")
     e = e + e3
-
-    g = gate(zo0, zo1, e3, czl)
-    ce = swap(g(e), "core")
-    czo0, czo1 = swap(g(zo0), "core"), swap(g(zo1), "core")
+    ce = swap(e, "core")
+    czo0, czo1 = swap(zo0, "core"), swap(zo1, "core")
 
     shifts = (0, 3, 1, 2)
     groups = [[m], [cm], [r], [cr], [l], [cl], [o0, o1], [co0, co1]]

time: 135 us -> 114 us (0.84)
  the two profiles are of different devices: /device:TPU:1 before, /device:TPU:12 now
where the time goes in v7:
time: 114 us; the launch traced here: 115 us
  waiting for transfers between devices  60.6 us (53%)
  Pallas kernels  25 us (22%)
  starting transfers between devices  20.4 us (18%)
  local copies, waits for them, and re-layouts  6.52 us (6%)
  between operations  1.76 us (2%)
    ppermute x13, waiting for transfers between devices, route(): return lax.ppermute(x, ROW + COL, pairs)  54.8 us
    pallas_call x1, Pallas kernels, product(): pl.pallas_call(functools.partial(product_kernel, shapes, spread), out_sha...  18.9 us
    ppermute x13, starting transfers between devices, route(): return lax.ppermute(x, ROW + COL, pairs)  18.3 us
    ppermute x12, waiting for transfers between devices, swap(): return lax.ppermute(x, axis, [(0, 1), (1, 0)])  5.72 us
    pallas_call x1, Pallas kernels, pack(): pl.pallas_call(pack_kernel, out_shape=(jax.ShapeDtypeStruct((ROWS, W), jn...  3.72 us
    pallas_call x1, Pallas kernels, merge(): pl.pallas_call(merge_kernel, out_shape=(jax.ShapeDtypeStruct((ROWS, W), j...  2.34 us
  transfers between devices with their start and end apart: 25, of which 10 were waited for; matrix products, arithmetic and copies ran while one was open for 5% of the time, Pallas kernels for 0%

profile of v7, /device:TPU:12, one launch (start us, length us, event | category | flops | bytes accessed | tf_op | source)
XLA Modules:
  0.0 114.7 jit_solution(1211349886149136510)
XLA Ops:
  0.0 3.7 %pack.1 = (f32[2576,128]{1,0:T(8,128)S(1)}, f32[2576,128]{1,0:T(8,128)}) custom-call(s32[1]{0:T(128)} %bitcast.core_ref, s32[4,8]{1,0:T(4,128)} %am_ref.1, s32[4,8]{1,0:T(4,128)} %bm_ref.1, f32[512,1024]{1,0:T(8,128)} %a_ref.1, f32[512,1024]{1,0:T(8,128)} %b_ref.1), custom_call_target="tpu_custom_call" | custom-call | tf_op jit(solution)/shard_map/pack/pallas_call | solution.py:74
  3.8 3.2 %collective-permute-done.22.got_ref = f32[2576,128]{1,0:T(8,128)S(1)} collective-permute-done((f32[2576,128]{1,0:T(8,128)}, f32[2576,128]{1,0:T(8,128)S(1)}, u32[]{:S(2)}, u32[]{:S(2)}) %collective-permute-start.22) | collective-permute-done | bytes 1318944 | tf_op jit(solution)/shard_map/ppermute | solution.py:289
  7.1 1.1 copy-done.9
  8.1 2.3 %merge.1 = (f32[2576,128]{1,0:T(8,128)S(1)}, f32[1288,128]{1,0:T(8,128)}) custom-call(s32[1]{0:T(128)} %bitcast.core_ref, f32[2576,128]{1,0:T(8,128)S(1)} %get-tuple-element.255.keep_ref, f32[2576,128]{1,0:T(8,128)} %copy-done.9), custom_call_target="tpu_custom_call" | custom-call | tf_op jit(solution)/shard_map/merge/pallas_call | solution.py:98
  10.5 1.2 %collective-permute-start.23 = (f32[2576,128]{1,0:T(8,128)S(1)}, f32[2576,128]{1,0:T(8,128)S(1)}, u32[]{:S(2)}, u32[]{:S(2)}) collective-permute-start(f32[2576,128]{1,0:T(8,128)S(1)} %get-tuple-element.258), channel_id=1, source_target_pairs={{0,1},{1,2},{2,3},{3,0},{4,5},{5,6},{6,7},{7,4},{8,24},{9,25},{10,... | collective-permute-start | bytes 3956744 | tf_op jit(solution)/shard_map/ppermute | solution.py:334
  12.5 4.0 %collective-permute-start.26 = (f32[1280,128]{1,0:T(8,128)S(1)}, f32[1280,128]{1,0:T(8,128)S(1)}, u32[]{:S(2)}, u32[]{:S(2)}) collective-permute-start(f32[1280,128]{1,0:T(8,128)S(1)} %slice.45), channel_id=1, source_target_pairs={{0,4},{1,5},{2,6},{3,7},{4,0},{5,1},{6,2},{7,3},{8,72},{9,73},{10,... | collective-permute-start | bytes 1966088 | tf_op jit(solution)/shard_map/ppermute | solution.py:334
  16.6 15.4 %collective-permute-done.26 = f32[1280,128]{1,0:T(8,128)S(1)} collective-permute-done((f32[1280,128]{1,0:T(8,128)S(1)}, f32[1280,128]{1,0:T(8,128)S(1)}, u32[]{:S(2)}, u32[]{:S(2)}) %collective-permute-start.26) | collective-permute-done | bytes 655392 | tf_op jit(solution)/shard_map/ppermute | solution.py:334
  32.0 1.3 %collective-permute-start.27 = (f32[1296,128]{1,0:T(8,128)S(1)}, f32[1296,128]{1,0:T(8,128)S(1)}, u32[]{:S(2)}, u32[]{:S(2)}) collective-permute-start(f32[1296,128]{1,0:T(8,128)S(1)} %slice.44), channel_id=1, source_target_pairs={{0,4},{1,5},{2,6},{3,7},{4,0},{5,1},{6,2},{7,3},{8,72},{9,73},{10,... | collective-permute-start | bytes 1990664 | tf_op jit(solution)/shard_map/ppermute | solution.py:334
  34.3 1.3 %collective-permute-start.29 = (f32[1280,128]{1,0:T(8,128)S(1)}, f32[1280,128]{1,0:T(8,128)S(1)}, u32[]{:S(2)}, u32[]{:S(2)}) collective-permute-start(f32[1280,128]{1,0:T(8,128)S(1)} %slice.60), channel_id=1, source_target_pairs={{0,1},{1,2},{2,3},{3,0},{4,5},{5,6},{6,7},{7,4},{8,24},{9,25},{10,... | collective-permute-start | bytes 1966088 | tf_op jit(solution)/shard_map/ppermute | solution.py:334
  35.5 2.9 %collective-permute-start.25 = (f32[1288,128]{1,0:T(8,128)S(1)}, f32[1288,128]{1,0:T(8,128)S(1)}, u32[]{:S(2)}, u32[]{:S(2)}) collective-permute-start(f32[1288,128]{1,0:T(8,128)S(1)} %copy-done.10), channel_id=1, source_target_pairs={{0,1},{1,0},{2,3},{3,2},{4,5},{5,4},{6,7},{7,6},{8,24},{9,25},{10,... | collective-permute-start | bytes 1978376 | tf_op jit(solution)/shard_map/ppermute | solution.py:334
  38.4 6.5 %collective-permute-done.29 = f32[1280,128]{1,0:T(8,128)S(1)} collective-permute-done((f32[1280,128]{1,0:T(8,128)S(1)}, f32[1280,128]{1,0:T(8,128)S(1)}, u32[]{:S(2)}, u32[]{:S(2)}) %collective-permute-start.29) | collective-permute-done | bytes 655392 | tf_op jit(solution)/shard_map/ppermute | solution.py:334
  44.9 4.2 %collective-permute-done.27 = f32[1296,128]{1,0:T(8,128)S(1)} collective-permute-done((f32[1296,128]{1,0:T(8,128)S(1)}, f32[1296,128]{1,0:T(8,128)S(1)}, u32[]{:S(2)}, u32[]{:S(2)}) %collective-permute-start.27) | collective-permute-done | bytes 663584 | tf_op jit(solution)/shard_map/ppermute | solution.py:334
  50.9 1.2 %collective-permute-start.31 = (f32[2576,128]{1,0:T(8,128)}, f32[2576,128]{1,0:T(8,128)}, u32[]{:S(2)}, u32[]{:S(2)}) collective-permute-start(f32[2576,128]{1,0:T(8,128)} %constant_dynamic-update-slice_fusion), channel_id=1, source_target_pairs={{0,1},{1,2},{2,3},{3,0},{4,5},{5,6},{6,7},{7,4},{8,24},{9,25},{10,... | collective-permute-start | bytes 3956744 | tf_op jit(solution)/shard_map/ppermute | solution.py:334
  54.1 13.8 %collective-permute-done.28 = f32[1288,128]{1,0:T(8,128)S(1)} collective-permute-done((f32[1288,128]{1,0:T(8,128)S(1)}, f32[1288,128]{1,0:T(8,128)S(1)}, u32[]{:S(2)}, u32[]{:S(2)}) %collective-permute-start.28) | collective-permute-done | bytes 659488 | tf_op jit(solution)/shard_map/ppermute | solution.py:334
  67.9 1.0 collective-permute-done.31
  69.0 1.2 %collective-permute-done.32 = f32[2576,128]{1,0:T(8,128)} collective-permute-done((f32[2576,128]{1,0:T(8,128)}, f32[2576,128]{1,0:T(8,128)}, u32[]{:S(2)}, u32[]{:S(2)}) %collective-permute-start.32) | collective-permute-done | bytes 1318944 | tf_op jit(solution)/shard_map/ppermute | solution.py:334
  71.2 1.1 slice.64
  72.4 2.1 %collective-permute-start.43 = (f32[1280,128]{1,0:T(8,128)S(1)}, f32[1280,128]{1,0:T(8,128)}, u32[]{:S(2)}, u32[]{:S(2)}) collective-permute-start(f32[1280,128]{1,0:T(8,128)S(1)} %slice.64), channel_id=1, source_target_pairs={{0,1},{1,2},{2,3},{3,0},{4,5},{5,6},{6,7},{7,4},{8,24},{9,25},{10,... | collective-permute-start | bytes 1966088 | tf_op jit(solution)/shard_map/ppermute | solution.py:334
  74.5 1.1 slice.65
  76.8 5.8 %collective-permute-done.33 = f32[1288,128]{1,0:T(8,128)S(1)} collective-permute-done((f32[1288,128]{1,0:T(8,128)S(1)}, f32[1288,128]{1,0:T(8,128)S(1)}, u32[]{:S(2)}, u32[]{:S(2)}) %collective-permute-start.33) | collective-permute-done | bytes 659488 | tf_op jit(solution)/shard_map/ppermute | solution.py:334
  82.7 6.9 %collective-permute-done.43 = f32[1280,128]{1,0:T(8,128)} collective-permute-done((f32[1280,128]{1,0:T(8,128)S(1)}, f32[1280,128]{1,0:T(8,128)}, u32[]{:S(2)}, u32[]{:S(2)}) %collective-permute-start.43) | collective-permute-done | bytes 655392 | tf_op jit(solution)/shard_map/ppermute | solution.py:334
  90.1 2.5 %collective-permute-done.34 = f32[1288,128]{1,0:T(8,128)S(1)} collective-permute-done((f32[1288,128]{1,0:T(8,128)S(1)}, f32[1288,128]{1,0:T(8,128)S(1)}, u32[]{:S(2)}, u32[]{:S(2)}) %collective-permute-start.34) | collective-permute-done | bytes 659488 | tf_op jit(solution)/shard_map/ppermute | solution.py:289
  95.3 19.2 %conditional.3 = (f32[512,1024]{1,0:T(8,128)}) conditional(s32[]{:T(128)} %convert_element_type.9, (s32[17]{0:T(128)S(1)}, s32[64,128]{0,1:T(8,128)S(1)}, f32[2576,128]{1,0:T(8,128)S(1)}, f32[2576,128]{1,0:T(8,128)}, f32[2576,128]{1,0:T(8,128)}, /*index=5*/f32[2576,128]{1,0:T(8,128)}, f32[2576,128]{1,0:T(8,128)}, f32[2576,128]{1,0:T(8,128)}, ...), branch_computations={%region_0.1_spmd, %region_1.6_spmd} | conditional | flops 983047 | bytes 69534936 | solution.py:411
  95.4 18.9 %product.2 = f32[512,1024]{1,0:T(8,128)} custom-call(s32[17]{0:T(128)S(1)} %get-tuple-element.154.where_ref, s32[64,128]{1,0:T(8,128)S(1)} %copy.9.keep_ref, f32[2576,128]{1,0:T(8,128)S(1)} %get-tuple-element.156.refs_0_, f32[2576,128]{1,0:T(8,128)} %get-tuple-element.157.refs_1_, f32[2576,128]{1,0:T(8,128)} %get-tuple-element.158.refs_2_, ...), custom_call_target="tpu_custom_call" | custom-call | tf_op jit(solution)/shard_map/cond/branch_0_fun/product/pallas_call | solution.py:263
  (70 shorter events, 9.9 us)
Async XLA Ops:
  3.7 3.3 %collective-permute-start.22 = (f32[2576,128]{1,0:T(8,128)}, f32[2576,128]{1,0:T(8,128)S(1)}, u32[]{:S(2)}, u32[]{:S(2)}) collective-permute-start(f32[2576,128]{1,0:T(8,128)} %get-tuple-element.256), channel_id=1, source_target_pairs={{0,8},{8,0},{1,9},{9,1},{2,10},{10,2},{3,11},{11,3},{4,12},{12,4},... | collective-permute-start | bytes 3956744 | tf_op jit(solution)/shard_map/ppermute | solution.py:289
  10.5 21.5 %collective-permute-start.23 = (f32[2576,128]{1,0:T(8,128)S(1)}, f32[2576,128]{1,0:T(8,128)S(1)}, u32[]{:S(2)}, u32[]{:S(2)}) collective-permute-start(f32[2576,128]{1,0:T(8,128)S(1)} %get-tuple-element.258), channel_id=1, source_target_pairs={{0,1},{1,2},{2,3},{3,0},{4,5},{5,6},{6,7},{7,4},{8,24},{9,25},{10,... | collective-permute-start | bytes 3956744 | tf_op jit(solution)/shard_map/ppermute | solution.py:334
  11.7 20.3 %collective-permute-start.24 = (f32[2576,128]{1,0:T(8,128)S(1)}, f32[2576,128]{1,0:T(8,128)S(1)}, u32[]{:S(2)}, u32[]{:S(2)}) collective-permute-start(f32[2576,128]{1,0:T(8,128)S(1)} %get-tuple-element.258), channel_id=1, source_target_pairs={{0,3},{1,0},{2,1},{3,2},{4,7},{5,4},{6,5},{7,6},{8,56},{9,57},{10,... | collective-permute-start | bytes 3956744 | tf_op jit(solution)/shard_map/ppermute | solution.py:334
  12.5 19.4 %collective-permute-start.26 = (f32[1280,128]{1,0:T(8,128)S(1)}, f32[1280,128]{1,0:T(8,128)S(1)}, u32[]{:S(2)}, u32[]{:S(2)}) collective-permute-start(f32[1280,128]{1,0:T(8,128)S(1)} %slice.45), channel_id=1, source_target_pairs={{0,4},{1,5},{2,6},{3,7},{4,0},{5,1},{6,2},{7,3},{8,72},{9,73},{10,... | collective-permute-start | bytes 1966088 | tf_op jit(solution)/shard_map/ppermute | solution.py:334
  32.0 17.2 %collective-permute-start.27 = (f32[1296,128]{1,0:T(8,128)S(1)}, f32[1296,128]{1,0:T(8,128)S(1)}, u32[]{:S(2)}, u32[]{:S(2)}) collective-permute-start(f32[1296,128]{1,0:T(8,128)S(1)} %slice.44), channel_id=1, source_target_pairs={{0,4},{1,5},{2,6},{3,7},{4,0},{5,1},{6,2},{7,3},{8,72},{9,73},{10,... | collective-permute-start | bytes 1990664 | tf_op jit(solution)/shard_map/ppermute | solution.py:334
  33.3 15.8 %collective-permute-start.30 = (f32[1296,128]{1,0:T(8,128)S(1)}, f32[1296,128]{1,0:T(8,128)S(1)}, u32[]{:S(2)}, u32[]{:S(2)}) collective-permute-start(f32[1296,128]{1,0:T(8,128)S(1)} %slice.61), channel_id=1, source_target_pairs={{0,3},{1,0},{2,1},{3,2},{4,7},{5,4},{6,5},{7,6},{8,56},{9,57},{10,... | collective-permute-start | bytes 1990664 | tf_op jit(solution)/shard_map/ppermute | solution.py:334
  34.3 10.7 %collective-permute-start.29 = (f32[1280,128]{1,0:T(8,128)S(1)}, f32[1280,128]{1,0:T(8,128)S(1)}, u32[]{:S(2)}, u32[]{:S(2)}) collective-permute-start(f32[1280,128]{1,0:T(8,128)S(1)} %slice.60), channel_id=1, source_target_pairs={{0,1},{1,2},{2,3},{3,0},{4,5},{5,6},{6,7},{7,4},{8,24},{9,25},{10,... | collective-permute-start | bytes 1966088 | tf_op jit(solution)/shard_map/ppermute | solution.py:334
  35.5 17.4 %collective-permute-start.25 = (f32[1288,128]{1,0:T(8,128)S(1)}, f32[1288,128]{1,0:T(8,128)S(1)}, u32[]{:S(2)}, u32[]{:S(2)}) collective-permute-start(f32[1288,128]{1,0:T(8,128)S(1)} %copy-done.10), channel_id=1, source_target_pairs={{0,1},{1,0},{2,3},{3,2},{4,5},{5,4},{6,7},{7,6},{8,24},{9,25},{10,... | collective-permute-start | bytes 1978376 | tf_op jit(solution)/shard_map/ppermute | solution.py:334
  50.9 18.0 %collective-permute-start.31 = (f32[2576,128]{1,0:T(8,128)}, f32[2576,128]{1,0:T(8,128)}, u32[]{:S(2)}, u32[]{:S(2)}) collective-permute-start(f32[2576,128]{1,0:T(8,128)} %constant_dynamic-update-slice_fusion), channel_id=1, source_target_pairs={{0,1},{1,2},{2,3},{3,0},{4,5},{5,6},{6,7},{7,4},{8,24},{9,25},{10,... | collective-permute-start | bytes 3956744 | tf_op jit(solution)/shard_map/ppermute | solution.py:334
  52.1 18.0 %collective-permute-start.32 = (f32[2576,128]{1,0:T(8,128)}, f32[2576,128]{1,0:T(8,128)}, u32[]{:S(2)}, u32[]{:S(2)}) collective-permute-start(f32[2576,128]{1,0:T(8,128)} %constant_dynamic-update-slice_fusion), channel_id=1, source_target_pairs={{0,3},{1,0},{2,1},{3,2},{4,7},{5,4},{6,5},{7,6},{8,56},{9,57},{10,... | collective-permute-start | bytes 3956744 | tf_op jit(solution)/shard_map/ppermute | solution.py:334
  53.1 14.8 %collective-permute-start.28 = (f32[1288,128]{1,0:T(8,128)S(1)}, f32[1288,128]{1,0:T(8,128)S(1)}, u32[]{:S(2)}, u32[]{:S(2)}) collective-permute-start(f32[1288,128]{1,0:T(8,128)S(1)} %add.116), channel_id=1, source_target_pairs={{0,4},{1,5},{2,6},{3,7},{4,0},{5,1},{6,2},{7,3},{8,72},{9,73},{10,... | collective-permute-start | bytes 1978376 | tf_op jit(solution)/shard_map/ppermute | solution.py:334
  53.6 16.6 %collective-permute-start.35 = (f32[2576,128]{1,0:T(8,128)S(1)}, f32[2576,128]{1,0:T(8,128)S(1)}, u32[]{:S(2)}, u32[]{:S(2)}) collective-permute-start(f32[2576,128]{1,0:T(8,128)S(1)} %get-tuple-element.258), channel_id=1, source_target_pairs={{0,8},{8,0},{1,9},{9,1},{2,10},{10,2},{3,11},{11,3},{4,12},{12,4},... | collective-permute-start | bytes 3956744 | tf_op jit(solution)/shard_map/ppermute | solution.py:289
  53.6 22.0 %collective-permute-start.36 = (f32[2576,128]{1,0:T(8,128)S(1)}, f32[2576,128]{1,0:T(8,128)S(1)}, u32[]{:S(2)}, u32[]{:S(2)}) collective-permute-start(f32[2576,128]{1,0:T(8,128)S(1)} %collective-permute-done.23), channel_id=1, source_target_pairs={{0,8},{8,0},{1,9},{9,1},{2,10},{10,2},{3,11},{11,3},{4,12},{12,4},... | collective-permute-start | bytes 3956744 | tf_op jit(solution)/shard_map/ppermute | solution.py:289
  67.9 8.0 %collective-permute-start.37 = (f32[2576,128]{1,0:T(8,128)S(1)}, f32[2576,128]{1,0:T(8,128)S(1)}, u32[]{:S(2)}, u32[]{:S(2)}) collective-permute-start(f32[2576,128]{1,0:T(8,128)S(1)} %collective-permute-done.24), channel_id=1, source_target_pairs={{0,8},{8,0},{1,9},{9,1},{2,10},{10,2},{3,11},{11,3},{4,12},{12,4},... | collective-permute-start | bytes 3956744 | tf_op jit(solution)/shard_map/ppermute | solution.py:289
  69.0 3.4 %collective-permute-start.38 = (f32[1280,128]{1,0:T(8,128)S(1)}, f32[1280,128]{1,0:T(8,128)S(1)}, u32[]{:S(2)}, u32[]{:S(2)}) collective-permute-start(f32[1280,128]{1,0:T(8,128)S(1)} %collective-permute-done.29), channel_id=1, source_target_pairs={{0,8},{8,0},{1,9},{9,1},{2,10},{10,2},{3,11},{11,3},{4,12},{12,4},... | collective-permute-start | bytes 1966088 | tf_op jit(solution)/shard_map/ppermute | solution.py:289
  70.2 6.5 %collective-permute-start.39 = (f32[1296,128]{1,0:T(8,128)S(1)}, f32[1296,128]{1,0:T(8,128)S(1)}, u32[]{:S(2)}, u32[]{:S(2)}) collective-permute-start(f32[1296,128]{1,0:T(8,128)S(1)} %collective-permute-done.30), channel_id=1, source_target_pairs={{0,8},{8,0},{1,9},{9,1},{2,10},{10,2},{3,11},{11,3},{4,12},{12,4},... | collective-permute-start | bytes 1990664 | tf_op jit(solution)/shard_map/ppermute | solution.py:289
  70.3 12.3 %collective-permute-start.33 = (f32[1288,128]{1,0:T(8,128)S(1)}, f32[1288,128]{1,0:T(8,128)S(1)}, u32[]{:S(2)}, u32[]{:S(2)}) collective-permute-start(f32[1288,128]{1,0:T(8,128)S(1)} %add.117), channel_id=1, source_target_pairs={{0,2},{1,3},{2,0},{3,1},{4,6},{5,7},{6,4},{7,5},{8,40},{9,41},{10,... | collective-permute-start | bytes 1978376 | tf_op jit(solution)/shard_map/ppermute | solution.py:334
  72.4 17.3 %collective-permute-start.43 = (f32[1280,128]{1,0:T(8,128)S(1)}, f32[1280,128]{1,0:T(8,128)}, u32[]{:S(2)}, u32[]{:S(2)}) collective-permute-start(f32[1280,128]{1,0:T(8,128)S(1)} %slice.64), channel_id=1, source_target_pairs={{0,1},{1,2},{2,3},{3,0},{4,5},{5,6},{6,7},{7,4},{8,24},{9,25},{10,... | collective-permute-start | bytes 1966088 | tf_op jit(solution)/shard_map/ppermute | solution.py:334
  75.6 14.0 %collective-permute-start.44 = (f32[1296,128]{1,0:T(8,128)S(1)}, f32[1296,128]{1,0:T(8,128)}, u32[]{:S(2)}, u32[]{:S(2)}) collective-permute-start(f32[1296,128]{1,0:T(8,128)S(1)} %slice.65), channel_id=1, source_target_pairs={{0,3},{1,0},{2,1},{3,2},{4,7},{5,4},{6,5},{7,6},{8,56},{9,57},{10,... | collective-permute-start | bytes 1990664 | tf_op jit(solution)/shard_map/ppermute | solution.py:334
  76.0 19.3 %collective-permute-start.40 = (f32[2576,128]{1,0:T(8,128)}, f32[2576,128]{1,0:T(8,128)}, u32[]{:S(2)}, u32[]{:S(2)}) collective-permute-start(f32[2576,128]{1,0:T(8,128)} %constant_dynamic-update-slice_fusion), channel_id=1, source_target_pairs={{0,8},{8,0},{1,9},{9,1},{2,10},{10,2},{3,11},{11,3},{4,12},{12,4},... | collective-permute-start | bytes 3956744 | tf_op jit(solution)/shard_map/ppermute | solution.py:289
  76.7 18.6 %collective-permute-start.41 = (f32[2576,128]{1,0:T(8,128)}, f32[2576,128]{1,0:T(8,128)}, u32[]{:S(2)}, u32[]{:S(2)}) collective-permute-start(f32[2576,128]{1,0:T(8,128)} %collective-permute-done.31), channel_id=1, source_target_pairs={{0,8},{8,0},{1,9},{9,1},{2,10},{10,2},{3,11},{11,3},{4,12},{12,4},... | collective-permute-start | bytes 3956744 | tf_op jit(solution)/shard_map/ppermute | solution.py:289
  82.6 12.7 %collective-permute-start.42 = (f32[2576,128]{1,0:T(8,128)}, f32[2576,128]{1,0:T(8,128)}, u32[]{:S(2)}, u32[]{:S(2)}) collective-permute-start(f32[2576,128]{1,0:T(8,128)} %collective-permute-done.32), channel_id=1, source_target_pairs={{0,8},{8,0},{1,9},{9,1},{2,10},{10,2},{3,11},{11,3},{4,12},{12,4},... | collective-permute-start | bytes 3956744 | tf_op jit(solution)/shard_map/ppermute | solution.py:289
  89.6 3.0 %collective-permute-start.34 = (f32[1288,128]{1,0:T(8,128)S(1)}, f32[1288,128]{1,0:T(8,128)S(1)}, u32[]{:S(2)}, u32[]{:S(2)}) collective-permute-start(f32[1288,128]{1,0:T(8,128)S(1)} %add.118), channel_id=1, source_target_pairs={{0,8},{8,0},{1,9},{9,1},{2,10},{10,2},{3,11},{11,3},{4,12},{12,4},... | collective-permute-start | bytes 1978376 | tf_op jit(solution)/shard_map/ppermute | solution.py:289
  89.6 5.7 %collective-permute-start.46 = (f32[1296,128]{1,0:T(8,128)}, f32[1296,128]{1,0:T(8,128)}, u32[]{:S(2)}, u32[]{:S(2)}) collective-permute-start(f32[1296,128]{1,0:T(8,128)} %collective-permute-done.44), channel_id=1, source_target_pairs={{0,8},{8,0},{1,9},{9,1},{2,10},{10,2},{3,11},{11,3},{4,12},{12,4},... | collective-permute-start | bytes 1990664 | tf_op jit(solution)/shard_map/ppermute | solution.py:289
  (13 other events, 200.5 us)
